TPU v7x, 256 devices: a whole 4x4x8 slice. The times are simulated.
256 devices in a mesh: tm: 32 (over z, x_hi, core), dish: 8 (over y, x_lo).
Axes of the slice: x: 4 (x_hi: 2, x_lo: 2; x = x_hi * 2 + x_lo), y: 4, z: 8, core: 2. Of those that a mesh axis runs over, the one named last changes fastest.
Arguments:
- voltages: bfloat16 [2, 64, 131072], P(None, 'dish', 'tm'), may hold values from -6 to 6
- beam_weights: bfloat16 [2, 64], P(None, 'dish'), may hold values from -0.75 to 0.75
- phase_bins: int32 [131072], P('tm'), may hold values from 0 to 1023, as said below
Outputs:
- spectrum: float32 [2048, 2, 1024], P('dish', None, 'tm')
Inputs may be any that keep to these rules, and one draw needn't show every extreme that they name: `phase_bins`: from each time sample to the next the bin stays or advances by one, wrapping from 1023 to 0; every bin occurs.
All inputs are finite; a program needn't handle non-finite values.
Results may differ from a plain program's by a relative error of at most 0.0039.
Values may be sent and summed in bfloat16 or wider, within the bound.
No kernel may reach another device: no remote copies, remote signals or barrier semaphores. Data moves between devices by JAX's collectives and lax.ppermute only.
A program may use at most 64 MiB of HBM per device.

v0:
```python
import math

import jax
import jax.numpy as jnp
from jax import lax
from jax.sharding import PartitionSpec as P

PH = 1024
LAGS = 2048


def from_behind(value, axis, steps):
    count = lax.axis_size(axis)
    first, last = (max(0, -steps), min(count, count - steps))
    return lax.ppermute(value, axis, [(source, source + steps) for source in range(first, last)])


def form_beam(volt_block, weights):
    dish_count = volt_block.shape[1]
    mixer_rows = jnp.stack(
        [jnp.concatenate([weights[0], -weights[1]]), jnp.concatenate([weights[1], weights[0]])]
    )
    flat_volts = volt_block.reshape(2 * dish_count, volt_block.shape[2])
    return jnp.dot(mixer_rows, flat_volts, preferred_element_type=jnp.float32)


def hankel_rows(segment, row_count, lag_count):
    span_width = row_count + lag_count
    tiled_rows = jnp.broadcast_to(segment[:, None, :], (2, row_count + 1, span_width)).reshape(
        2, (row_count + 1) * span_width
    )
    return tiled_rows[:, : row_count * (span_width + 1)].reshape(2, row_count, span_width + 1)[
        :, :, :lag_count
    ]


def fold_block(extended, phase_bins, row_start, lag_start, row_count, lag_count, targets):
    current = lax.dynamic_slice_in_dim(extended, row_start, row_count, 1)
    segment = lax.dynamic_slice_in_dim(extended, row_start + lag_start, row_count + lag_count, 1)
    hankel = hankel_rows(segment, row_count, lag_count)
    upper_half = jnp.concatenate([hankel[0], hankel[1]], 1)
    lower_half = jnp.concatenate([hankel[1], -hankel[0]], 1)
    right_side = jnp.concatenate([upper_half, lower_half], 0)
    bin_block = lax.dynamic_slice_in_dim(phase_bins, row_start, row_count)
    select = (targets[:, None] == bin_block[None, :]).astype(jnp.bfloat16)
    left_side = jnp.concatenate([select * current[0][None, :], select * current[1][None, :]], 1)
    return jnp.dot(left_side, right_side, preferred_element_type=jnp.float32)


def transform_rows(coeffs, row_count, lag_start, lag_count, spectral_scale):
    frequency = jnp.arange(row_count, dtype=jnp.int32)
    lag_index = lag_start + jnp.arange(lag_count, dtype=jnp.int32)
    turn_index = frequency[:, None] * lag_index[None, :] % LAGS
    phase_angle = turn_index.astype(jnp.float32) * (2.0 * math.pi / LAGS)
    cosine = jnp.cos(phase_angle)
    sine_table = jnp.sin(phase_angle)
    left_side = jnp.concatenate(
        [jnp.concatenate([cosine, sine_table], 1), jnp.concatenate([-sine_table, cosine], 1)], 0
    )
    product = lax.dot_general(
        left_side,
        coeffs,
        (((1,), (1,)), ((), ())),
        precision=lax.Precision.HIGHEST,
        preferred_element_type=jnp.float32,
    )
    return jnp.transpose(product.reshape(2, row_count, coeffs.shape[0]), (1, 0, 2)) * spectral_scale


def per_device(voltages, beam_weights, phase_bins):
    samples = phase_bins.shape[0]
    count_tm = lax.axis_size("tm")
    count_dish = lax.axis_size("dish")
    dish_index = lax.axis_index("dish")
    partial_value = form_beam(voltages, beam_weights)
    beam_rows = lax.psum(partial_value, "dish").astype(jnp.bfloat16)
    rim_beam = from_behind(beam_rows[:, :LAGS], "tm", -1)
    extended = jnp.concatenate([beam_rows, rim_beam], 1)
    spectral_scale = 1.0 / math.sqrt(LAGS * samples * count_tm / PH)
    block_rows = min(512, samples)
    lag_share = LAGS // count_dish
    lag_start = dish_index * lag_share
    targets = jnp.arange(PH, dtype=jnp.int32)

    def accumulate(block_step, running):
        return running + fold_block(
            extended, phase_bins, block_step * block_rows, lag_start, block_rows, lag_share, targets
        )

    folded = lax.fori_loop(
        0, samples // block_rows, accumulate, jnp.zeros((PH, 2 * lag_share), jnp.float32)
    )
    owned_fold = lax.psum_scatter(folded, "tm", scatter_dimension=0, tiled=True)
    return lax.psum_scatter(
        transform_rows(
            owned_fold, lag_share * lax.axis_size("dish"), lag_start, lag_share, spectral_scale
        ),
        "dish",
        scatter_dimension=0,
        tiled=True,
    )


def solution(mesh):
    return jax.shard_map(
        per_device,
        mesh=mesh,
        in_specs=(P(None, "dish", "tm"), P(None, "dish"), P("tm")),
        out_specs=P("dish", None, "tm"),
        check_vma=False,
    )
```

profile of v0, /device:TPU:1, one launch (start us, length us, event | category | flops | bytes accessed | tf_op | source)
XLA Modules:
  0.0 342.0 jit_solution(4395846807699343090)
XLA Ops:
  8.2 28.4 %psum.7 = bf16[2,4096]{1,0:T(2,128)(2,1)S(1)} all-reduce(f32[2,4096]{1,0:T(2,128)S(1)} %fusion.39), channel_id=1, replica_groups=mesh['tm'=32,'dish'=8] {'dish'}, use_global_device_ids=true, to_apply=%region_0.0 | all-reduce | flops 8192 | bytes 49152 | tf_op jit(solution)/shard_map/psum | solution.py:76
  36.6 9.6 %collective-permute-start = (bf16[2,2048]{1,0:T(2,128)(2,1)S(1)}, bf16[2,2048]{1,0:T(2,128)(2,1)S(1)}, u32[]{:S(2)}, u32[]{:S(2)}) collective-permute-start(bf16[2,2048]{1,0:T(2,128)(2,1)S(1)} %slice.64), channel_id=1, source_target_pairs={{8,0},{16,8},{24,16},{32,24},{40,32},{48,40},{56,48},{64,56},{72,6... | collective-permute-start | bytes 24584 | tf_op jit(solution)/shard_map/ppermute | solution.py:15
  46.3 3.6 %collective-permute-done = bf16[2,2048]{1,0:T(2,128)(2,1)S(1)} collective-permute-done((bf16[2,2048]{1,0:T(2,128)(2,1)S(1)}, bf16[2,2048]{1,0:T(2,128)(2,1)S(1)}, u32[]{:S(2)}, u32[]{:S(2)}) %collective-permute-start) | collective-permute-done | bytes 8224 | tf_op jit(solution)/shard_map/ppermute | solution.py:15
  49.9 120.4 %while.14 = (s32[]{:T(128)}, f32[1024,512]{1,0:T(8,128)}, s32[4096]{0:T(1024)}, bf16[2,6144]{1,0:T(2,128)(2,1)S(1)}, s32[]{:T(128)}, /*index=5*/s32[]{:T(128)}, ...) while((s32[]{:T(128)}, f32[1024,512]{1,0:T(8,128)}, s32[4096]{0:T(1024)}, ...), condition=%wide.region_2.0_spmd.clone, body=%wide.region_1.0_spmd.clone.sunk | while | flops 1084882944 | bytes 41724228 | solution.py:90
  50.9 1.2 copy.11
  52.2 1.2 slice.78
  54.3 5.2 %reshape.37 = bf16[2,512,769]{2,1,0:T(8,128)(2,1)} reshape(bf16[787456]{0:T(1024)(128)(2,1)S(1)} %reshape.36) | data formatting | bytes 3149824 | tf_op jit(solution)/shard_map/while/body/eval_jaxpr/reshape | solution.py:32
  59.5 1.1 fusion.55
  60.6 1.1 slice_bitcast_fusion.5
  62.2 1.5 select_add_fusion.2
  63.7 1.3 copy-done.2
  66.0 1.2 copy.11
  67.2 1.2 slice.78
  69.4 5.2 %reshape.37 = bf16[2,512,769]{2,1,0:T(8,128)(2,1)} reshape(bf16[787456]{0:T(1024)(128)(2,1)S(1)} %reshape.36) | data formatting | bytes 3149824 | tf_op jit(solution)/shard_map/while/body/eval_jaxpr/reshape | solution.py:32
  74.6 1.1 fusion.55
  75.7 1.1 slice_bitcast_fusion.5
  77.2 1.5 select_add_fusion.2
  78.7 1.3 copy-done.2
  81.0 1.2 copy.11
  82.3 1.2 slice.78
  84.4 5.2 %reshape.37 = bf16[2,512,769]{2,1,0:T(8,128)(2,1)} reshape(bf16[787456]{0:T(1024)(128)(2,1)S(1)} %reshape.36) | data formatting | bytes 3149824 | tf_op jit(solution)/shard_map/while/body/eval_jaxpr/reshape | solution.py:32
  89.6 1.1 fusion.55
  90.7 1.1 slice_bitcast_fusion.5
  92.3 1.5 select_add_fusion.2
  93.8 1.3 copy-done.2
  96.1 1.2 copy.11
  97.3 1.2 slice.78
  99.5 5.2 %reshape.37 = bf16[2,512,769]{2,1,0:T(8,128)(2,1)} reshape(bf16[787456]{0:T(1024)(128)(2,1)S(1)} %reshape.36) | data formatting | bytes 3149824 | tf_op jit(solution)/shard_map/while/body/eval_jaxpr/reshape | solution.py:32
  104.7 1.1 fusion.55
  105.8 1.1 slice_bitcast_fusion.5
  107.3 1.5 select_add_fusion.2
  108.8 1.3 copy-done.2
  111.1 1.2 copy.11
  112.4 1.2 slice.78
  114.5 5.2 %reshape.37 = bf16[2,512,769]{2,1,0:T(8,128)(2,1)} reshape(bf16[787456]{0:T(1024)(128)(2,1)S(1)} %reshape.36) | data formatting | bytes 3149824 | tf_op jit(solution)/shard_map/while/body/eval_jaxpr/reshape | solution.py:32
  119.7 1.1 fusion.55
  120.8 1.1 slice_bitcast_fusion.5
  122.4 1.5 select_add_fusion.2
  123.9 1.3 copy-done.2
  126.2 1.2 copy.11
  127.4 1.2 slice.78
  129.6 5.2 %reshape.37 = bf16[2,512,769]{2,1,0:T(8,128)(2,1)} reshape(bf16[787456]{0:T(1024)(128)(2,1)S(1)} %reshape.36) | data formatting | bytes 3149824 | tf_op jit(solution)/shard_map/while/body/eval_jaxpr/reshape | solution.py:32
  134.8 1.1 fusion.55
  135.9 1.1 slice_bitcast_fusion.5
  137.4 1.5 select_add_fusion.2
  138.9 1.3 copy-done.2
  141.2 1.2 copy.11
  142.5 1.2 slice.78
  144.6 5.2 %reshape.37 = bf16[2,512,769]{2,1,0:T(8,128)(2,1)} reshape(bf16[787456]{0:T(1024)(128)(2,1)S(1)} %reshape.36) | data formatting | bytes 3149824 | tf_op jit(solution)/shard_map/while/body/eval_jaxpr/reshape | solution.py:32
  149.8 1.1 fusion.55
  150.9 1.1 slice_bitcast_fusion.5
  152.5 1.5 select_add_fusion.2
  154.0 1.3 copy-done.2
  156.3 1.2 copy.11
  157.5 1.2 slice.78
  159.7 5.2 %reshape.37 = bf16[2,512,769]{2,1,0:T(8,128)(2,1)} reshape(bf16[787456]{0:T(1024)(128)(2,1)S(1)} %reshape.36) | data formatting | bytes 3149824 | tf_op jit(solution)/shard_map/while/body/eval_jaxpr/reshape | solution.py:32
  164.9 1.1 fusion.55
  166.0 1.1 slice_bitcast_fusion.5
  167.5 1.5 select_add_fusion.2
  169.0 1.3 copy-done.2
  170.6 9.4 %fusion.36 = (f32[2048,256]{1,0:T(8,128)S(1)}, f32[2048,256]{1,0:T(8,128)}, f32[2048,256]{1,0:T(8,128)}) fusion(s32[256]{0:T(256)S(1)} %iota_add_fusion), kind=kLoop, calls=%fused_computation.42 | loop fusion | flops 7864320 | bytes 6292480 | tf_op jit(solution)/shard_map/sin | solution.py:56
  180.0 103.0 %reduce-scatter.3.cloned.1.call-done = f32[32,512]{1,0:T(8,128)} async-done(((f32[1024,512]{1,0:T(8,128)}), f32[32,512]{1,0:T(8,128)}) %reduce-scatter.3.cloned.1.call-update) | async-done | bytes 65552 | tf_op jit(solution)/shard_map/reduce_scatter | solution.py:93
  283.0 11.9 %fusion.27 = f32[4096,32]{0,1:T(8,128)S(1)} fusion(f32[32,512]{1,0:T(8,128)} %reduce-scatter.3.cloned.1.call-done, f32[2048,256]{1,0:T(8,128)} %get-tuple-element.153, f32[2048,256]{1,0:T(8,128)} %get-tuple-element.152, f32[2048,256]{1,0:T(8,128)S(1)} %get-tuple-element.151), kind=kOutput, calls=%fused_computation.32 | convolution fusion | flops 811728896 | bytes 6881280 | tf_op jit(solution)/shard_map/dot_general | solution.py:60
  295.7 39.5 %reduce-scatter.5.cloned.1.call-done = f32[256,2,32]{0,2,1:T(8,128)} async-done(((f32[2048,2,32]{0,2,1:T(8,128)}), f32[256,2,32]{0,2,1:T(8,128)}) %reduce-scatter.5.cloned.1.call-update) | async-done | bytes 65552 | tf_op jit(solution)/shard_map/reduce_scatter | solution.py:94
  (87 shorter events, 22.2 us)
Async XLA Ops:
  6.5 1.5 copy-start
  6.5 276.5 %reduce-scatter.3.cloned.1.call-start = ((), (), s32[]{:S(2)}) async-start(), calls=%async_computation.2 | async-start | bytes 2162688 | tf_op jit(solution)/shard_map/reduce_scatter | solution.py:93
  36.6 13.3 %collective-permute-start = (bf16[2,2048]{1,0:T(2,128)(2,1)S(1)}, bf16[2,2048]{1,0:T(2,128)(2,1)S(1)}, u32[]{:S(2)}, u32[]{:S(2)}) collective-permute-start(bf16[2,2048]{1,0:T(2,128)(2,1)S(1)} %slice.64), channel_id=1, source_target_pairs={{8,0},{16,8},{24,16},{32,24},{40,32},{48,40},{56,48},{64,56},{72,6... | collective-permute-start | bytes 24584 | tf_op jit(solution)/shard_map/ppermute | solution.py:15
  59.5 2.7 copy-start.1
  63.7 1.3 copy-start.2
  74.6 2.7 copy-start.1
  78.7 1.3 copy-start.2
  89.6 2.7 copy-start.1
  93.8 1.3 copy-start.2
  104.7 2.7 copy-start.1
  108.8 1.3 copy-start.2
  119.7 2.7 copy-start.1
  123.9 1.3 copy-start.2
  134.8 2.7 copy-start.1
  138.9 1.3 copy-start.2
  149.8 2.7 copy-start.1
  154.0 1.3 copy-start.2
  164.9 2.7 copy-start.1
  169.0 1.3 copy-start.2
  170.4 164.8 %reduce-scatter.5.cloned.1.call-start = ((), (), s32[]{:S(2)}) async-start(), calls=%async_computation.3 | async-start | bytes 589824 | tf_op jit(solution)/shard_map/reduce_scatter | solution.py:94
Sparse Core Ops, SparseCore 0:
  170.5 112.4 reduce-scatter.2
  295.9 39.2 reduce-scatter.4
where the time goes:
time: 347 us; the launch traced here: 342 us
  waiting for transfers between devices  146 us (42%)
  local copies, waits for them, and re-layouts  96.9 us (28%)
  blocking collectives  28.4 us (8%)
  matrix products  24 us (7%)
  other arithmetic  22.7 us (7%)
  between operations  13.4 us (4%)
  starting transfers between devices  9.86 us (3%)
    reduce_scatter x1, waiting for transfers between devices, per_device(): owned_fold = lax.psum_scatter(folded, 'tm', scatter_dimension=0, tiled=True)  103 us
    reshape x8, local copies, waits for them, and re-layouts, hankel_rows(): tiled_rows[:, :row_count * (span_width + 1)]  41.5 us
    reduce_scatter x1, waiting for transfers between devices, per_device(): lax.psum_scatter(transform_rows(owned_fold, lag_share * lax.axis_size('di...  39.5 us
    while x56, local copies, waits for them, and re-layouts  29.1 us
    psum x1, blocking collectives, per_device(): beam_rows = lax.psum(partial_value, 'dish').astype(jnp.bfloat16)  28.4 us
    dot_general x8, matrix products, fold_block(): return jnp.dot(left_side, right_side, preferred_element_type=jnp.float32)  12 us
    dot_general x1, matrix products, transform_rows(): lax.dot_general(left_side, coeffs, (((1,), (1,)), ((), ())), precision=la...  11.9 us
    ppermute x1, starting transfers between devices, from_behind(): lax.ppermute(value, axis, [(source, source + steps) for source in range(f...  9.64 us
  transfers between devices with their start and end apart: 3, of which 3 were waited for; matrix products, arithmetic and copies ran while one was open for 3% of the time, Pallas kernels for 0%

commit v1 on v0

v1 whole, which is shorter than its diff:
```python
import functools
import math

import jax
import jax.numpy as jnp
import numpy as np
from jax import lax
from jax.experimental import pallas as pl
from jax.experimental.pallas import tpu as pltpu
from jax.sharding import PartitionSpec as P

PH = 1024
LAGS = 2048
SAMPLES = 131072
DISH_WAYS = 8
TM_WAYS = 32
CHIPS = 16
LOCAL = SAMPLES // TM_WAYS
GRAIN = 128
GRAINS = SAMPLES // GRAIN
PER_BLOCK = LOCAL // GRAIN
SPAN = LAGS // GRAIN
BINS = PH // TM_WAYS
FREQS = LAGS // DISH_WAYS
SLOTS = 128
GROUP = 8
SCALE = 1.0 / math.sqrt(LAGS * SAMPLES / PH)

F32 = jnp.float32
BF16 = jnp.bfloat16


def dot(a, b, dims=(((1,), (0,)), ((), ()))):
    return lax.dot_general(a, b, dims, preferred_element_type=F32)


def hi_lo(value):
    hi = value.astype(BF16)
    return hi, (value - hi.astype(F32)).astype(BF16)


def tables():
    grain = np.arange(GRAIN)
    freq = np.arange(FREQS)
    angle = 2 * np.pi * np.outer(grain, freq) / LAGS
    base = np.concatenate([np.cos(angle), np.sin(angle)], 1).astype(np.float32)
    eighth = 2 * np.pi * np.outer(grain, np.arange(DISH_WAYS)) / DISH_WAYS
    turn = np.zeros((GRAIN, 128), np.float32)
    turn[:, :8] = np.cos(eighth)
    turn[:, 8:16] = np.sin(eighth)
    fine = 2 * np.pi * np.outer(grain, np.arange(2 * GRAIN)) / (2 * GRAIN)
    cos2, sin2 = np.cos(fine), np.sin(fine)
    fold2 = np.block([[cos2, sin2], [sin2, -cos2]]).astype(np.float32)
    step2 = np.block([[cos2, -sin2], [sin2, cos2]]).astype(np.float32)
    keep = (grain >= 1)[None, :] / (2.0 * GRAIN)
    back = np.block([[cos2.T * keep, -sin2.T * keep], [sin2.T * keep, cos2.T * keep]])
    sixteenth = 2 * np.pi * np.outer(np.arange(SPAN), freq) / SPAN
    phase = np.concatenate([np.cos(sixteenth), np.sin(sixteenth)], 1).astype(np.float32)
    index = np.zeros((GRAINS, 128), np.float32)
    index[:, 0] = np.arange(GRAINS) // SPAN
    index[:, 1] = np.arange(GRAINS) % SPAN
    return (
        jnp.asarray(base),
        jnp.asarray(turn),
        jnp.asarray(fold2).astype(BF16),
        jnp.asarray(step2).astype(BF16),
        jnp.asarray(back.astype(np.float32)).astype(BF16),
        jnp.asarray(phase),
        jnp.asarray(index).astype(BF16),
    )


def beam_kernel(volts_ref, weights_ref, out_ref):
    weights = weights_ref[...]
    first = dot(weights, volts_ref[0])
    second = dot(weights, volts_ref[1])
    real = first[0:1] - second[1:2]
    imag = first[1:2] + second[0:1]
    for row in range(PER_BLOCK):
        part = slice(row * GRAIN, (row + 1) * GRAIN)
        out_ref[0, row : row + 1, :] = real[:, part]
        out_ref[0, PER_BLOCK + row : PER_BLOCK + row + 1, :] = imag[:, part]
    rows = out_ref[0]
    for way in range(1, DISH_WAYS):
        out_ref[way] = rows


def pack_kernel(parts_ref, bins_ref, out_ref):
    total = parts_ref[0]
    for way in range(1, DISH_WAYS):
        total = total + parts_ref[way]
    bins = bins_ref[...]
    high = bins >> 5
    coded = ((bins & 31) + 32).astype(F32)
    for bit in range(5):
        coded = coded * jnp.where((high >> bit) & 1 == 1, float(2 ** (2**bit)), 1.0)
    coded = coded * (2.0**-16)
    rows = jnp.concatenate([total.astype(BF16), coded.astype(BF16)], 0)
    for chip in range(CHIPS):
        out_ref[chip] = rows


def two_to(exponent):
    value = jnp.float32(2.0**-16)
    for bit in range(5):
        value = value * jnp.where((exponent >> bit) & 1 == 1, jnp.float32(2 ** (2**bit)), jnp.float32(1.0))
    return value


def spectrum_kernel(
    ids,
    own_ref, other_ref, base_ref, turn_ref, fold2_ref, step2_ref, back_ref, phase_ref, index_ref,
    out_ref,
    beam_s, code_s, fold_s, step_s, last_s, phase_s, zhi_s, zlo_s,
    gbeam_s, gcode_s, gdft_s, gstep_s, acc_s,
):
    owner, dish, core = ids()
    for chip in range(CHIPS):
        for ref, which in ((own_ref, core), (other_ref, 1 - core)):
            start = pl.multiple_of((2 * chip + which) * PER_BLOCK, PER_BLOCK)
            rows = pl.ds(start, PER_BLOCK)
            beam_s[rows, 0:GRAIN] = ref[chip, 0:PER_BLOCK, :]
            beam_s[rows, GRAIN:] = ref[chip, PER_BLOCK : 2 * PER_BLOCK, :]
            code_s[rows, :] = ref[chip, 2 * PER_BLOCK :, :]
    beam_s[GRAINS:, :] = jnp.zeros((SPAN, 2 * GRAIN), BF16)
    lane = lax.broadcasted_iota(jnp.int32, (GRAIN, 128), 1)
    turn = turn_ref[...]
    cos8 = jnp.sum(jnp.where(lane == dish, turn, 0.0), axis=1, keepdims=True)
    sin8 = jnp.sum(jnp.where(lane == dish + 8, turn, 0.0), axis=1, keepdims=True)
    cos0, sin0 = base_ref[:, :FREQS], base_ref[:, FREQS:]
    cosine = (cos0 * cos8 - sin0 * sin8).astype(BF16)
    sine = (sin0 * cos8 + cos0 * sin8).astype(BF16)
    fold_s[:GRAIN, :FREQS] = cosine
    fold_s[:GRAIN, FREQS : 2 * FREQS] = sine
    fold_s[GRAIN:, :FREQS] = sine
    fold_s[GRAIN:, FREQS : 2 * FREQS] = -cosine
    fold_s[:, 2 * FREQS :] = fold2_ref[...]
    step_s[:GRAIN, :FREQS] = cosine
    step_s[:GRAIN, FREQS:] = -sine
    step_s[GRAIN:, :FREQS] = sine
    step_s[GRAIN:, FREQS:] = cosine
    last_s[:GRAIN, :FREQS] = cosine
    last_s[:GRAIN, FREQS:] = sine
    last_s[GRAIN:, :FREQS] = -sine
    last_s[GRAIN:, FREQS:] = cosine
    cos16, sin16 = phase_ref[:, :FREQS], phase_ref[:, FREQS:]
    phase_s[...] = jnp.zeros(phase_s.shape, BF16)
    for at, part in ((0, cos16), (FREQS, sin16)):
        hi, lo = hi_lo(part)
        phase_s[0:SPAN, at : at + FREQS] = hi
        phase_s[SPAN : 2 * SPAN, at : at + FREQS] = lo
    turns = 128 // SPAN
    cos_rows = jnp.concatenate([cos16] * turns, 0)
    sin_rows = jnp.concatenate([sin16] * turns, 0)
    for tile in range(GRAINS // 128):
        rows = slice(tile * 128, tile * 128 + 128)
        both = dot(beam_s[rows, :], step_s[...])
        real, imag = both[:, :FREQS], both[:, FREQS:]
        zhi_s[rows, :FREQS], zlo_s[rows, :FREQS] = hi_lo(real * cos_rows + imag * sin_rows)
        zhi_s[rows, FREQS:], zlo_s[rows, FREQS:] = hi_lo(imag * cos_rows - real * sin_rows)
    unit = two_to(owner)
    code = code_s[...].astype(F32)
    inside = jnp.where((code >= unit * 32.0) & (code < unit * 64.0), 1.0, 0.0).astype(BF16)
    hits = dot(jnp.ones((8, GRAIN), BF16), inside, (((1,), (1,)), ((), ())))
    mask = jnp.where(hits > 0.0, 1.0, 0.0)
    upper = (
        lax.broadcasted_iota(jnp.int32, (128, 128), 0) <= lax.broadcasted_iota(jnp.int32, (128, 128), 1)
    )
    upper = jnp.where(upper, 1.0, 0.0).astype(BF16)
    before = jnp.zeros((8, 1), F32)
    ranks = []
    for tile in range(GRAINS // 128):
        part = mask[:, tile * 128 : tile * 128 + 128]
        rank = dot(part.astype(BF16), upper) + before
        before = rank[:, 127:128]
        ranks.append(jnp.where(part > 0.0, rank, 0.0))
    ranked = jnp.concatenate(ranks, 1)[0:1, :]
    count = jnp.max(before).astype(jnp.int32)
    acc_s[...] = jnp.zeros(acc_s.shape, F32)
    bin_key = (
        lax.broadcasted_iota(jnp.int32, (BINS, GRAIN), 0).astype(F32) + 32.0
    ) * unit
    slot_iota = lax.broadcasted_iota(jnp.int32, (SLOTS, GRAINS), 0).astype(F32)
    grain_iota = lax.broadcasted_iota(jnp.int32, (SLOTS, GRAINS), 1).astype(F32)
    lane_iota = lax.broadcasted_iota(jnp.int32, (SLOTS, 128), 1).astype(F32)

    def batch_step(batch, carry):
        first = (batch * SLOTS + 1).astype(F32)
        pick = jnp.where(ranked == slot_iota + first, 1.0, 0.0).astype(BF16)
        here = dot(pick, beam_s[0:GRAINS, :])
        ahead = dot(pick, beam_s[SPAN : GRAINS + SPAN, :])
        gbeam_s[...] = here
        gcode_s[...] = dot(pick, code_s[...])
        place = dot(pick, index_ref[...])
        coarse, offset = place[:, 0:1], place[:, 1:2]
        grain = coarse * float(SPAN) + offset
        window = jnp.where((grain_iota >= grain) & (grain_iota < grain + float(SPAN)), 1.0, 0.0)
        window = window.astype(BF16)
        dft = dot(window, zhi_s[...]) + dot(window, zlo_s[...])
        turner = jnp.where((lane_iota == offset) | (lane_iota == offset + float(SPAN)), 1.0, 0.0)
        turned = dot(turner.astype(BF16), phase_s[...])
        real, imag = dft[:, :FREQS], dft[:, FREQS:]
        cos_g, sin_g = turned[:, :FREQS], turned[:, FREQS:]
        gdft_s[:, :FREQS] = real * cos_g - imag * sin_g
        gdft_s[:, FREQS:] = imag * cos_g + real * sin_g
        gstep_s[...] = dot(ahead.astype(BF16), step2_ref[...]) - dot(here.astype(BF16), step2_ref[...])

        def group_step(group, inner):
            rows = pl.ds(pl.multiple_of(group * GROUP, GROUP), GROUP)
            beam8, code8 = gbeam_s[rows, :], gcode_s[rows, :]
            dft8, step8 = gdft_s[rows, :], gstep_s[rows, :]
            left = []
            for k in range(GROUP):
                chosen = code8[k : k + 1, :] == bin_key
                real = jnp.where(chosen, beam8[k : k + 1, :GRAIN], 0.0)
                imag = jnp.where(chosen, beam8[k : k + 1, GRAIN:], 0.0)
                left.append(jnp.concatenate([real, imag], 1))
            left = jnp.concatenate(left, 0).astype(BF16)
            for at, factor in ((0, dft8), (2 * FREQS, step8)):
                folded = dot(left, fold_s[:, at : at + 2 * FREQS])
                real_sum, imag_sum = acc_s[:, at : at + FREQS], acc_s[:, at + FREQS : at + 2 * FREQS]
                for k in range(GROUP):
                    part = slice(k * BINS, k * BINS + BINS)
                    real, imag = folded[part, :FREQS], folded[part, FREQS:]
                    cos_f, sin_f = factor[k : k + 1, :FREQS], factor[k : k + 1, FREQS:]
                    real_sum = real_sum + (real * cos_f - imag * sin_f)
                    imag_sum = imag_sum + (real * sin_f + imag * cos_f)
                acc_s[:, at : at + FREQS] = real_sum
                acc_s[:, at + FREQS : at + 2 * FREQS] = imag_sum
            return inner

        left_over = jnp.minimum(count - batch * SLOTS, SLOTS)
        return lax.fori_loop(0, (left_over + GROUP - 1) // GROUP, group_step, carry)

    lax.fori_loop(0, (count + SLOTS - 1) // SLOTS, batch_step, 0)
    hi, lo = hi_lo(acc_s[:, 2 * FREQS :])
    short = dot(hi, back_ref[...]) + dot(lo, back_ref[...])
    hi, lo = hi_lo(short)
    short = dot(hi, last_s[...]) + dot(lo, last_s[...])
    out_ref[0] = (acc_s[:, :FREQS] + short[:, :FREQS]) * SCALE
    out_ref[1] = (acc_s[:, FREQS : 2 * FREQS] + short[:, FREQS:]) * SCALE


def vmem(count):
    return [pl.BlockSpec(memory_space=pltpu.VMEM)] * count


def spectrum(own, other, ids):
    return pl.pallas_call(
        functools.partial(spectrum_kernel, ids),
        out_shape=jax.ShapeDtypeStruct((2, BINS, FREQS), F32),
        in_specs=vmem(9),
        out_specs=vmem(1)[0],
        scratch_shapes=[
            pltpu.VMEM((GRAINS + SPAN, 2 * GRAIN), BF16),
            pltpu.VMEM((GRAINS, GRAIN), BF16),
            pltpu.VMEM((2 * GRAIN, 4 * FREQS), BF16),
            pltpu.VMEM((2 * GRAIN, 2 * FREQS), BF16),
            pltpu.VMEM((2 * GRAIN, 2 * FREQS), BF16),
            pltpu.VMEM((128, 2 * FREQS), BF16),
            pltpu.VMEM((GRAINS, 2 * FREQS), BF16),
            pltpu.VMEM((GRAINS, 2 * FREQS), BF16),
            pltpu.VMEM((SLOTS, 2 * GRAIN), F32),
            pltpu.VMEM((SLOTS, GRAIN), F32),
            pltpu.VMEM((SLOTS, 2 * FREQS), F32),
            pltpu.VMEM((SLOTS, 2 * FREQS), F32),
            pltpu.VMEM((BINS, 4 * FREQS), F32),
        ],
        name="spectrum",
    )(own, other, *tables())


def per_device(voltages, beam_weights, phase_bins):
    partial_beam = pl.pallas_call(
        beam_kernel,
        out_shape=jax.ShapeDtypeStruct((DISH_WAYS, 2 * PER_BLOCK, GRAIN), F32),
        in_specs=vmem(2),
        out_specs=vmem(1)[0],
        name="beam",
    )(voltages, beam_weights)
    parts = lax.all_to_all(partial_beam, "dish", 0, 0, tiled=True)
    packed = pl.pallas_call(
        pack_kernel,
        out_shape=jax.ShapeDtypeStruct((CHIPS, 3 * PER_BLOCK, GRAIN), BF16),
        in_specs=vmem(2),
        out_specs=vmem(1)[0],
        name="pack",
    )(parts, phase_bins.reshape(PER_BLOCK, GRAIN))
    own = lax.all_to_all(packed, ("z", "xh"), 0, 0, tiled=True)
    other = lax.ppermute(own, "core", [(0, 1), (1, 0)])

    def ids():
        core = lax.axis_index("core")
        owner = (lax.axis_index("z") * 2 + lax.axis_index("xh")) * 2 + core
        return owner, lax.axis_index("dish"), core

    return jnp.transpose(spectrum(own, other, ids), (2, 0, 1))


def solution(mesh):
    split = jax.sharding.Mesh(mesh.devices.reshape(8, 2, 2, 8), ("z", "xh", "core", "dish"))
    time = ("z", "xh", "core")
    return jax.shard_map(
        per_device,
        mesh=split,
        in_specs=(P(None, "dish", time), P(None, "dish"), P(time)),
        out_specs=P("dish", None, time),
        check_vma=False,
    )
```

time: 347 us -> 55.7 us (0.16); the launches traced: 342 us -> 55.2 us
  waiting for transfers between devices: 146 us -> 1.35 us
  local copies, waits for them, and re-layouts: 96.9 us -> 0.75 us
  matrix products: 24 us -> 0 us
  other arithmetic: 22.7 us -> 0 us
  between operations: 13.4 us -> 0.01 us
  Pallas kernels: 0 us -> 13.3 us
  blocking collectives: 28.4 us -> 36.1 us
  starting transfers between devices: 9.86 us -> 3.7 us
    reduce_scatter x2 -> x0, waiting for transfers between devices: 142 us -> none  [the longest x1 103 us: per_device(): owned_fold = lax.psum_scatter(folded, 'tm', scatter_dimension=0, tiled=True)]
    reshape x8 -> x0, local copies, waits for them, and re-layouts: 41.5 us -> none  [hankel_rows(): tiled_rows[:, :row_count * (span_width + 1)]]
    all_to_all x0 -> x2, blocking collectives: none -> 36.1 us  [the longest x1 23.9 us: per_device(): own = lax.all_to_all(packed, ('z', 'xh'), 0, 0, tiled=True)]
    while x56 -> x0, local copies, waits for them, and re-layouts: 29.1 us -> none
    psum x1 -> x0, blocking collectives: 28.4 us -> none  [per_device(): beam_rows = lax.psum(partial_value, 'dish').astype(jnp.bfloat16)]
    dot_general x10 -> x0, matrix products: 24 us -> none  [the longest x8 12 us: fold_block(): return jnp.dot(left_side, right_side, preferred_element_type=jnp.float32)]
    pallas_call x0 -> x3, Pallas kernels: none -> 13.3 us  [the longest x1 9.72 us: spectrum(): pl.pallas_call(functools.partial(spectrum_kernel, ids), out_shape=jax.Sha...]
    slice x17 -> x0, local copies, waits for them, and re-layouts: 10.1 us -> none  [the longest x8 9.26 us: hankel_rows(): tiled_rows[:, :row_count * (span_width + 1)]]
  transfers between devices with their start and end apart: 3 -> 1, of which waited for: 3 -> 1; matrix products, arithmetic and copies ran while one was open for 3% -> 0% of each run, Pallas kernels for 0% -> 0%
where the time goes in v1:
time: 55.7 us; the launch traced here: 55.2 us
  blocking collectives  36.1 us (65%)
  Pallas kernels  13.3 us (24%)
  starting transfers between devices  3.7 us (7%)
  waiting for transfers between devices  1.35 us (2%)
  local copies, waits for them, and re-layouts  0.75 us (1%)
    all_to_all x1, blocking collectives, per_device(): own = lax.all_to_all(packed, ('z', 'xh'), 0, 0, tiled=True)  23.9 us
    all_to_all x1, blocking collectives, per_device(): parts = lax.all_to_all(partial_beam, 'dish', 0, 0, tiled=True)  12.2 us
    pallas_call x1, Pallas kernels, spectrum(): pl.pallas_call(functools.partial(spectrum_kernel, ids), out_shape=jax.Sha...  9.72 us
    ppermute x1, starting transfers between devices, per_device(): other = lax.ppermute(own, 'core', [(0, 1), (1, 0)])  3.7 us
    pallas_call x1, Pallas kernels, per_device(): pl.pallas_call(beam_kernel, out_shape=jax.ShapeDtypeStruct((DISH_WAYS, 2...  1.82 us
    pallas_call x1, Pallas kernels, per_device(): pl.pallas_call(pack_kernel, out_shape=jax.ShapeDtypeStruct((CHIPS, 3 * PE...  1.74 us
    ppermute x1, waiting for transfers between devices, per_device(): other = lax.ppermute(own, 'core', [(0, 1), (1, 0)])  1.35 us
  transfers between devices with their start and end apart: 1, of which 1 were waited for; matrix products, arithmetic and copies ran while one was open for 0% of the time, Pallas kernels for 0%

profile of v1, /device:TPU:1, one launch (start us, length us, event | category | flops | bytes accessed | tf_op | source)
XLA Modules:
  0.0 55.2 jit_solution(11591588287524644691)
XLA Ops:
  0.0 1.8 %beam.1 = f32[8,64,128]{2,1,0:T(8,128)} custom-call(bf16[2,8,4096]{2,1,0:T(8,128)(2,1)} %volts_ref.1, bf16[2,8]{1,0:T(2,128)(2,1)} %weights_ref.1), custom_call_target="tpu_custom_call" | custom-call | tf_op jit(solution)/shard_map/beam/pallas_call | solution.py:274
  1.8 12.2 %all_to_all.10.parts_ref = f32[8,64,128]{2,1,0:T(8,128)} all-to-all(f32[8,64,128]{2,1,0:T(8,128)} %beam.1), channel_id=1, replica_groups=mesh['z'=8,'xh'=2,'core'=2,'dish'=8] {'dish'}, dimensions={0} | all-to-all | bytes 524288 | tf_op jit(solution)/shard_map/all_to_all | solution.py:281
  14.0 1.7 %pack.1 = bf16[16,96,128]{2,1,0:T(8,128)(2,1)} custom-call(f32[8,64,128]{2,1,0:T(8,128)} %all_to_all.10.parts_ref, s32[32,128]{1,0:T(8,128)} %bitcast.2), custom_call_target="tpu_custom_call" | custom-call | tf_op jit(solution)/shard_map/pack/pallas_call | solution.py:282
  15.8 23.9 %all_to_all.11.own_ref = bf16[16,96,128]{2,1,0:T(8,128)(2,1)S(1)} all-to-all(bf16[16,96,128]{2,1,0:T(8,128)(2,1)} %pack.1), channel_id=1, replica_groups=mesh['z'=8,'xh'=2,'core'=2,'dish'=8] {'z','xh'}, dimensions={0} | all-to-all | bytes 786432 | tf_op jit(solution)/shard_map/all_to_all | solution.py:289
  39.7 0.0 copy-start
  39.7 3.7 %collective-permute-start = (bf16[16,96,128]{2,1,0:T(8,128)(2,1)S(1)}, bf16[16,96,128]{2,1,0:T(8,128)(2,1)S(1)}, u32[]{:S(2)}, u32[]{:S(2)}) collective-permute-start(bf16[16,96,128]{2,1,0:T(8,128)(2,1)S(1)} %all_to_all.11.own_ref), channel_id=1, source_target_pairs={{0,8},{8,0},{1,9},{9,1},{2,10},{10,2},{3,11},{11,3},{4,12},{12,4},... | collective-permute-start | bytes 1179656 | tf_op jit(solution)/shard_map/ppermute | solution.py:290
  43.4 1.3 %collective-permute-done.other_ref = bf16[16,96,128]{2,1,0:T(8,128)(2,1)S(1)} collective-permute-done((bf16[16,96,128]{2,1,0:T(8,128)(2,1)S(1)}, bf16[16,96,128]{2,1,0:T(8,128)(2,1)S(1)}, u32[]{:S(2)}, u32[]{:S(2)}) %collective-permute-start) | collective-permute-done | bytes 393248 | tf_op jit(solution)/shard_map/ppermute | solution.py:290
  44.7 0.0 copy-done
  44.7 0.0 copy-start.1
  44.7 0.7 %copy-done.1 = bf16[16,96,128]{2,1,0:T(8,128)(2,1)} copy-done((bf16[16,96,128]{2,1,0:T(8,128)(2,1)}, bf16[16,96,128]{2,1,0:T(8,128)(2,1)S(1)}, u32[]{:S(2)}) %copy-start.1) | copy-done | bytes 393240
  45.5 9.7 %spectrum.1 = f32[2,32,256]{2,1,0:T(8,128)} custom-call(bf16[16,96,128]{2,1,0:T(8,128)(2,1)} %copy-done, bf16[16,96,128]{2,1,0:T(8,128)(2,1)} %copy-done.1, f32[128,512]{1,0:T(8,128)} %constant.14.clone.base_ref, f32[128,128]{1,0:T(8,128)} %constant.15.clone.turn_ref, bf16[256,512]{1,0:T(8,128)(2,1)} %constant.21.fold2_ref, ...), custom_call_target="tpu_custom_call" | custom-call | tf_op jit(solution)/shard_map/spectrum/pallas_call | solution.py:249
Async XLA Ops:
  39.7 5.1 %copy-start = (bf16[16,96,128]{2,1,0:T(8,128)(2,1)}, bf16[16,96,128]{2,1,0:T(8,128)(2,1)S(1)}, u32[]{:S(2)}) copy-start(bf16[16,96,128]{2,1,0:T(8,128)(2,1)S(1)} %all_to_all.11.own_ref) | copy-start | bytes 1179652
  39.7 5.0 %collective-permute-start = (bf16[16,96,128]{2,1,0:T(8,128)(2,1)S(1)}, bf16[16,96,128]{2,1,0:T(8,128)(2,1)S(1)}, u32[]{:S(2)}, u32[]{:S(2)}) collective-permute-start(bf16[16,96,128]{2,1,0:T(8,128)(2,1)S(1)} %all_to_all.11.own_ref), channel_id=1, source_target_pairs={{0,8},{8,0},{1,9},{9,1},{2,10},{10,2},{3,11},{11,3},{4,12},{12,4},... | collective-permute-start | bytes 1179656 | tf_op jit(solution)/shard_map/ppermute | solution.py:290
  44.7 0.7 %copy-start.1 = (bf16[16,96,128]{2,1,0:T(8,128)(2,1)}, bf16[16,96,128]{2,1,0:T(8,128)(2,1)S(1)}, u32[]{:S(2)}) copy-start(bf16[16,96,128]{2,1,0:T(8,128)(2,1)S(1)} %collective-permute-done.other_ref) | copy-start | bytes 1179652

commit v2 on v1

--- a/solution.py
+++ b/solution.py
@@ -245,6 +245,14 @@
     return [pl.BlockSpec(memory_space=pltpu.VMEM)] * count
 
 
+def near(*values):
+    return [pltpu.with_memory_space_constraint(v, pltpu.VMEM) for v in values]
+
+
+def params(mib):
+    return pltpu.CompilerParams(vmem_limit_bytes=mib << 20)
+
+
 def spectrum(own, other, ids):
     return pl.pallas_call(
         functools.partial(spectrum_kernel, ids),
@@ -266,26 +274,29 @@
             pltpu.VMEM((SLOTS, 2 * FREQS), F32),
             pltpu.VMEM((BINS, 4 * FREQS), F32),
         ],
+        compiler_params=params(24),
         name="spectrum",
-    )(own, other, *tables())
+    )(*near(own, other, *tables()))
 
 
 def per_device(voltages, beam_weights, phase_bins):
     partial_beam = pl.pallas_call(
         beam_kernel,
-        out_shape=jax.ShapeDtypeStruct((DISH_WAYS, 2 * PER_BLOCK, GRAIN), F32),
+        out_shape=pltpu.VMEM((DISH_WAYS, 2 * PER_BLOCK, GRAIN), F32),
         in_specs=vmem(2),
         out_specs=vmem(1)[0],
+        compiler_params=params(8),
         name="beam",
     )(voltages, beam_weights)
     parts = lax.all_to_all(partial_beam, "dish", 0, 0, tiled=True)
     packed = pl.pallas_call(
         pack_kernel,
-        out_shape=jax.ShapeDtypeStruct((CHIPS, 3 * PER_BLOCK, GRAIN), BF16),
+        out_shape=pltpu.VMEM((CHIPS, 3 * PER_BLOCK, GRAIN), BF16),
         in_specs=vmem(2),
         out_specs=vmem(1)[0],
+        compiler_params=params(8),
         name="pack",
-    )(parts, phase_bins.reshape(PER_BLOCK, GRAIN))
+    )(*near(parts, phase_bins.reshape(PER_BLOCK, GRAIN)))
     own = lax.all_to_all(packed, ("z", "xh"), 0, 0, tiled=True)
     other = lax.ppermute(own, "core", [(0, 1), (1, 0)])
 

time: 55.7 us -> 51.3 us (0.921)
  Pallas kernels: 13.3 us -> 8.75 us
  local copies, waits for them, and re-layouts: 0.75 us -> 1.6 us
    pallas_call x2, Pallas kernels: 3.56 us -> 0.26 us  [the longest x1 0.22 us: per_device(): pl.pallas_call(beam_kernel, out_shape=pltpu.VMEM((DISH_WAYS, 2 * PER_BLOC...]
    pallas_call x1, Pallas kernels: 9.72 us -> 8.49 us  [spectrum(): pl.pallas_call(functools.partial(spectrum_kernel, ids), out_shape=jax.Sha...]
    unnamed x4 -> x20, local copies, waits for them, and re-layouts: 0.75 us -> 1.6 us
where the time goes in v2:
time: 51.3 us; the launch traced here: 51.2 us
  blocking collectives  35.8 us (70%)
  Pallas kernels  8.75 us (17%)
  starting transfers between devices  3.69 us (7%)
  local copies, waits for them, and re-layouts  1.6 us (3%)
  waiting for transfers between devices  1.35 us (3%)
    all_to_all x1, blocking collectives, per_device(): own = lax.all_to_all(packed, ('z', 'xh'), 0, 0, tiled=True)  23.9 us
    all_to_all x1, blocking collectives, per_device(): parts = lax.all_to_all(partial_beam, 'dish', 0, 0, tiled=True)  11.9 us
    pallas_call x1, Pallas kernels, spectrum(): pl.pallas_call(functools.partial(spectrum_kernel, ids), out_shape=jax.Sha...  8.49 us
    ppermute x1, starting transfers between devices, per_device(): other = lax.ppermute(own, 'core', [(0, 1), (1, 0)])  3.69 us
    unnamed x20, local copies, waits for them, and re-layouts  1.6 us
    ppermute x1, waiting for transfers between devices, per_device(): other = lax.ppermute(own, 'core', [(0, 1), (1, 0)])  1.35 us
  transfers between devices with their start and end apart: 1, of which 1 were waited for; matrix products, arithmetic and copies ran while one was open for 0% of the time, Pallas kernels for 0%

profile of v2, /device:TPU:1, one launch (start us, length us, event | category | flops | bytes accessed | tf_op | source)
XLA Modules:
  0.0 51.2 jit_solution(1331121565470385005)
XLA Ops:
  0.0 0.0 copy-start.5
  0.0 0.9 %copy-done.5 = bf16[2,8,4096]{2,1,0:T(8,128)(2,1)S(1)} copy-done((bf16[2,8,4096]{2,1,0:T(8,128)(2,1)S(1)}, bf16[2,8,4096]{2,1,0:T(8,128)(2,1)}, u32[]{:S(2)}) %copy-start.5) | copy-done | bytes 131096
  0.9 0.0 copy-start.9
  0.9 0.7 %copy-done.9 = bf16[2,8]{1,0:T(2,128)(2,1)S(1)} copy-done((bf16[2,8]{1,0:T(2,128)(2,1)S(1)}, bf16[2,8]{1,0:T(2,128)(2,1)}, u32[]{:S(2)}) %copy-start.9) | copy-done | bytes 56
  1.6 0.2 beam.1
  1.8 0.0 copy-start.8
  1.8 11.9 %all_to_all.10.parts_ref = f32[8,64,128]{2,1,0:T(8,128)S(1)} all-to-all(f32[8,64,128]{2,1,0:T(8,128)S(1)} %beam.1), channel_id=1, replica_groups=mesh['z'=8,'xh'=2,'core'=2,'dish'=8] {'dish'}, dimensions={0} | all-to-all | bytes 524288 | tf_op jit(solution)/shard_map/all_to_all | solution.py:291
  13.7 0.0 copy-done.8
  13.7 0.0 copy-start.3
  13.7 0.0 copy-start.4
  13.7 0.0 copy-start.6
  13.7 0.0 copy-start.7
  13.8 0.0 copy-start
  13.8 0.0 copy-start.1
  13.8 0.0 copy-start.2
  13.8 23.9 %all_to_all.11.own_ref = bf16[16,96,128]{2,1,0:T(8,128)(2,1)S(1)} all-to-all(bf16[16,96,128]{2,1,0:T(8,128)(2,1)S(1)} %pack.1), channel_id=1, replica_groups=mesh['z'=8,'xh'=2,'core'=2,'dish'=8] {'z','xh'}, dimensions={0} | all-to-all | bytes 786432 | tf_op jit(solution)/shard_map/all_to_all | solution.py:300
  37.7 3.7 %collective-permute-start = (bf16[16,96,128]{2,1,0:T(8,128)(2,1)S(1)}, bf16[16,96,128]{2,1,0:T(8,128)(2,1)S(1)}, u32[]{:S(2)}, u32[]{:S(2)}) collective-permute-start(bf16[16,96,128]{2,1,0:T(8,128)(2,1)S(1)} %all_to_all.11.own_ref), channel_id=1, source_target_pairs={{0,8},{8,0},{1,9},{9,1},{2,10},{10,2},{3,11},{11,3},{4,12},{12,4},... | collective-permute-start | bytes 1179656 | tf_op jit(solution)/shard_map/ppermute | solution.py:301
  41.4 1.3 %collective-permute-done.other_ref = bf16[16,96,128]{2,1,0:T(8,128)(2,1)S(1)} collective-permute-done((bf16[16,96,128]{2,1,0:T(8,128)(2,1)S(1)}, bf16[16,96,128]{2,1,0:T(8,128)(2,1)S(1)}, u32[]{:S(2)}, u32[]{:S(2)}) %collective-permute-start) | collective-permute-done | bytes 393248 | tf_op jit(solution)/shard_map/ppermute | solution.py:301
  42.7 0.0 copy-done.3
  42.7 0.0 copy-done.4
  42.7 0.0 copy-done.6
  42.7 0.0 copy-done.7
  42.7 0.0 copy-done
  42.7 0.0 copy-done.1
  42.7 0.0 copy-done.2
  42.8 8.5 %spectrum.1 = f32[2,32,256]{2,1,0:T(8,128)} custom-call(bf16[16,96,128]{2,1,0:T(8,128)(2,1)S(1)} %all_to_all.11.own_ref, bf16[16,96,128]{2,1,0:T(8,128)(2,1)S(1)} %collective-permute-done.other_ref, f32[128,512]{1,0:T(8,128)S(1)} %copy-done.4, f32[128,128]{1,0:T(8,128)S(1)} %copy-done.6, bf16[256,512]{1,0:T(8,128)(2,1)S(1)} %copy-done.3, ...), custom_call_target="tpu_custom_call" | custom-call | tf_op jit(solution)/shard_map/spectrum/pallas_call | solution.py:257
  (1 shorter events, 0.0 us)
Async XLA Ops:
  0.0 0.9 %copy-start.5 = (bf16[2,8,4096]{2,1,0:T(8,128)(2,1)S(1)}, bf16[2,8,4096]{2,1,0:T(8,128)(2,1)}, u32[]{:S(2)}) copy-start(bf16[2,8,4096]{2,1,0:T(8,128)(2,1)} %volts_ref.1) | copy-start | bytes 393220
  0.9 0.7 %copy-start.9 = (bf16[2,8]{1,0:T(2,128)(2,1)S(1)}, bf16[2,8]{1,0:T(2,128)(2,1)}, u32[]{:S(2)}) copy-start(bf16[2,8]{1,0:T(2,128)(2,1)} %weights_ref.1) | copy-start | bytes 100
  1.8 11.9 %copy-start.8 = (s32[4096]{0:T(1024)S(1)}, s32[4096]{0:T(1024)}, u32[]{:S(2)}) copy-start(s32[4096]{0:T(1024)} %param.12) | copy-start | bytes 49156
  13.7 29.0 %copy-start.3 = (bf16[256,512]{1,0:T(8,128)(2,1)S(1)}, bf16[256,512]{1,0:T(8,128)(2,1)}, u32[]{:S(2)}) copy-start(bf16[256,512]{1,0:T(8,128)(2,1)} %constant.21.fold2_ref) | copy-start | bytes 786436
  13.7 29.0 %copy-start.4 = (f32[128,512]{1,0:T(8,128)S(1)}, f32[128,512]{1,0:T(8,128)}, u32[]{:S(2)}) copy-start(f32[128,512]{1,0:T(8,128)} %constant.14.clone.base_ref) | copy-start | bytes 786436
  13.7 29.0 %copy-start.6 = (f32[128,128]{1,0:T(8,128)S(1)}, f32[128,128]{1,0:T(8,128)}, u32[]{:S(2)}) copy-start(f32[128,128]{1,0:T(8,128)} %constant.15.clone.turn_ref) | copy-start | bytes 196612
  13.7 29.0 %copy-start.7 = (f32[16,512]{1,0:T(8,128)S(1)}, f32[16,512]{1,0:T(8,128)}, u32[]{:S(2)}) copy-start(f32[16,512]{1,0:T(8,128)} %constant.19.clone.phase_ref) | copy-start | bytes 98308
  13.8 28.9 %copy-start = (bf16[1024,128]{1,0:T(8,128)(2,1)S(1)}, bf16[1024,128]{1,0:T(8,128)(2,1)}, u32[]{:S(2)}) copy-start(bf16[1024,128]{1,0:T(8,128)(2,1)} %constant.24.index_ref) | copy-start | bytes 786436
  13.8 28.9 %copy-start.1 = (bf16[512,256]{1,0:T(8,128)(2,1)S(1)}, bf16[512,256]{1,0:T(8,128)(2,1)}, u32[]{:S(2)}) copy-start(bf16[512,256]{1,0:T(8,128)(2,1)} %constant.23.back_ref) | copy-start | bytes 786436
  13.8 28.9 %copy-start.2 = (bf16[256,512]{1,0:T(8,128)(2,1)S(1)}, bf16[256,512]{1,0:T(8,128)(2,1)}, u32[]{:S(2)}) copy-start(bf16[256,512]{1,0:T(8,128)(2,1)} %constant.22.step2_ref) | copy-start | bytes 786436
  37.7 5.0 %collective-permute-start = (bf16[16,96,128]{2,1,0:T(8,128)(2,1)S(1)}, bf16[16,96,128]{2,1,0:T(8,128)(2,1)S(1)}, u32[]{:S(2)}, u32[]{:S(2)}) collective-permute-start(bf16[16,96,128]{2,1,0:T(8,128)(2,1)S(1)} %all_to_all.11.own_ref), channel_id=1, source_target_pairs={{0,8},{8,0},{1,9},{9,1},{2,10},{10,2},{3,11},{11,3},{4,12},{12,4},... | collective-permute-start | bytes 1179656 | tf_op jit(solution)/shard_map/ppermute | solution.py:301

commit v3 on v1

v3 whole, which is shorter than its diff:
```python
import functools
import math

import jax
import jax.numpy as jnp
import numpy as np
from jax import lax
from jax.experimental import pallas as pl
from jax.experimental.pallas import tpu as pltpu
from jax.sharding import PartitionSpec as P


PH = 1024
LAGS = 2048
SAMPLES = 131072
DISH_WAYS = 8
TM_WAYS = 32
CHIPS = 16
HALF = SAMPLES // 2 // 128
LOCAL = SAMPLES // TM_WAYS
GRAIN = 128
PER_BLOCK = LOCAL // GRAIN
SPAN = LAGS // GRAIN
BINS = PH // TM_WAYS
FREQS = LAGS // DISH_WAYS
SLOTS = 128
GROUP = 16
SCALE = 1.0 / math.sqrt(LAGS * SAMPLES / PH)

F32 = jnp.float32
BF16 = jnp.bfloat16


def dot(a, b, dims=(((1,), (0,)), ((), ()))):
    return lax.dot_general(a, b, dims, preferred_element_type=F32)


def hi_lo(value):
    hi = value.astype(BF16)
    return hi, (value - hi.astype(F32)).astype(BF16)


def tables():
    grain = np.arange(GRAIN)
    freq = np.arange(FREQS)
    angle = 2 * np.pi * np.outer(grain, freq) / LAGS
    base = np.concatenate([np.cos(angle), np.sin(angle)], 1).astype(np.float32)
    eighth = 2 * np.pi * np.outer(grain, np.arange(DISH_WAYS)) / DISH_WAYS
    turn = np.zeros((GRAIN, 128), np.float32)
    turn[:, :8] = np.cos(eighth)
    turn[:, 8:16] = np.sin(eighth)
    fine = 2 * np.pi * np.outer(grain, np.arange(2 * GRAIN)) / (2 * GRAIN)
    cos2, sin2 = np.cos(fine), np.sin(fine)
    fold2 = np.block([[cos2, sin2], [sin2, -cos2]]).astype(np.float32)
    step2 = np.block([[cos2, -sin2], [sin2, cos2]]).astype(np.float32)
    keep = (grain >= 1)[None, :] / (2.0 * GRAIN)
    back = np.block([[cos2.T * keep, -sin2.T * keep], [sin2.T * keep, cos2.T * keep]])
    sixteenth = 2 * np.pi * np.outer(np.arange(SPAN), freq) / SPAN
    phase = np.concatenate([np.cos(sixteenth), np.sin(sixteenth)], 1).astype(np.float32)
    place = np.arange(HALF)
    index = np.zeros((HALF, 128), np.float32)
    index[:, 0] = place // PER_BLOCK
    index[:, 1] = place % PER_BLOCK
    index[:, 2] = 1.0
    return {
        "base": jnp.asarray(base),
        "turn": jnp.asarray(turn),
        "fold2": jnp.asarray(fold2).astype(BF16),
        "step2": jnp.asarray(step2).astype(BF16),
        "back": jnp.asarray(back.astype(np.float32)).astype(BF16),
        "phase": jnp.asarray(phase),
        "index": jnp.asarray(index).astype(BF16),
    }


def front_kernel(volts_hbm, weights_hbm, bins_hbm, beam_ref, code_ref, volts_s, weights_s, bins_s, sems):
    copies = [
        pltpu.make_async_copy(source, target, sems.at[k])
        for k, (source, target) in enumerate(
            ((bins_hbm, bins_s), (weights_hbm, weights_s), (volts_hbm, volts_s))
        )
    ]
    for copy in copies:
        copy.start()
    copies[0].wait()
    bins = bins_s[...]
    high = bins >> 5
    coded = ((bins & 31) + 32).astype(F32)
    for bit in range(5):
        coded = coded * jnp.where((high >> bit) & 1 == 1, float(2 ** (2**bit)), 1.0)
    code_ref[...] = (coded * (2.0**-16)).astype(BF16)
    copies[1].wait()
    copies[2].wait()
    weights = weights_s[...]
    first = dot(weights, volts_s[0])
    second = dot(weights, volts_s[1])
    real = first[0:1] - second[1:2]
    imag = first[1:2] + second[0:1]
    for row in range(PER_BLOCK):
        part = slice(row * GRAIN, (row + 1) * GRAIN)
        beam_ref[0, row : row + 1, :] = real[:, part]
        beam_ref[0, PER_BLOCK + row : PER_BLOCK + row + 1, :] = imag[:, part]
    rows = beam_ref[0]
    for way in range(1, DISH_WAYS):
        beam_ref[way] = rows


def pack_kernel(parts_ref, code_ref, out_ref):
    total = parts_ref[0]
    for way in range(1, DISH_WAYS):
        total = total + parts_ref[way]
    rows = jnp.concatenate([total.astype(BF16), code_ref[...]], 0)
    for chip in range(CHIPS):
        out_ref[chip] = rows


def table_kernel(ids, base_ref, turn_ref, fold2_ref, phase_ref, fold_ref, step_ref, last_ref, phases_ref):
    _, dish, _ = ids()
    lane = lax.broadcasted_iota(jnp.int32, (GRAIN, 128), 1)
    turn = turn_ref[...]
    cos8 = jnp.sum(jnp.where(lane == dish, turn, 0.0), axis=1, keepdims=True)
    sin8 = jnp.sum(jnp.where(lane == dish + 8, turn, 0.0), axis=1, keepdims=True)
    cos0, sin0 = base_ref[:, :FREQS], base_ref[:, FREQS:]
    cosine, cosine_lo = hi_lo(cos0 * cos8 - sin0 * sin8)
    sine, sine_lo = hi_lo(sin0 * cos8 + cos0 * sin8)
    fold_ref[:GRAIN, :FREQS] = cosine
    fold_ref[:GRAIN, FREQS : 2 * FREQS] = sine
    fold_ref[GRAIN:, :FREQS] = sine
    fold_ref[GRAIN:, FREQS : 2 * FREQS] = -cosine
    fold_ref[:, 2 * FREQS :] = fold2_ref[...]
    for k, (c, s) in enumerate(((cosine, sine), (cosine_lo, sine_lo))):
        step_ref[k, :GRAIN, :FREQS] = c
        step_ref[k, :GRAIN, FREQS:] = -s
        step_ref[k, GRAIN:, :FREQS] = s
        step_ref[k, GRAIN:, FREQS:] = c
    last_ref[:GRAIN, :FREQS] = cosine
    last_ref[:GRAIN, FREQS:] = sine
    last_ref[GRAIN:, :FREQS] = -sine
    last_ref[GRAIN:, FREQS:] = cosine
    phases_ref[...] = jnp.zeros(phases_ref.shape, BF16)
    hi, lo = hi_lo(phase_ref[...])
    phases_ref[0:SPAN, :] = hi
    phases_ref[SPAN : 2 * SPAN, :] = lo


def two_to(exponent):
    value = jnp.float32(2.0**-16)
    for bit in range(5):
        value = value * jnp.where((exponent >> bit) & 1 == 1, jnp.float32(2 ** (2**bit)), jnp.float32(1.0))
    return value


def beam_rows(ref, first, last):
    rows = [
        jnp.concatenate([ref[chip, :PER_BLOCK, :], ref[chip, PER_BLOCK : 2 * PER_BLOCK, :]], 1)
        for chip in range(first, last)
    ]
    return jnp.concatenate(rows, 0)


def code_rows(ref):
    return jnp.concatenate([ref[chip, 2 * PER_BLOCK :, :] for chip in range(CHIPS)], 0)


def transform(ref, step_ref, phase_ref, z_ref):
    cos16, sin16 = phase_ref[:, :FREQS], phase_ref[:, FREQS:]
    cos_rows = jnp.concatenate([cos16] * (128 // SPAN), 0)
    sin_rows = jnp.concatenate([sin16] * (128 // SPAN), 0)
    for tile in range(HALF // 128):
        rows = slice(tile * 128, tile * 128 + 128)
        beam = beam_rows(ref, 4 * tile, 4 * tile + 4)
        both = dot(beam, step_ref[0]) + dot(beam, step_ref[1])
        real, imag = both[:, :FREQS], both[:, FREQS:]
        z_ref[rows, :FREQS] = (real * cos_rows + imag * sin_rows).astype(BF16)
        z_ref[rows, FREQS:] = (imag * cos_rows - real * sin_rows).astype(BF16)


def rank_half(ref, owner, before):
    unit = two_to(owner)
    code = code_rows(ref).astype(F32)
    inside = jnp.where((code >= unit * 32.0) & (code < unit * 64.0), 1.0, 0.0).astype(BF16)
    hits = dot(jnp.ones((8, GRAIN), BF16), inside, (((1,), (1,)), ((), ())))
    mask = jnp.where(hits > 0.0, 1.0, 0.0)
    upper = (
        lax.broadcasted_iota(jnp.int32, (128, 128), 0) <= lax.broadcasted_iota(jnp.int32, (128, 128), 1)
    )
    upper = jnp.where(upper, 1.0, 0.0).astype(BF16)
    ranks = []
    for tile in range(HALF // 128):
        part = mask[:, tile * 128 : tile * 128 + 128]
        rank = dot(part.astype(BF16), upper) + before
        before = rank[:, 127:128]
        ranks.append(jnp.where(part > 0.0, rank, 0.0))
    return jnp.concatenate(ranks, 1), before


def gather_half(first, ranked, ref, index):
    slot = lax.broadcasted_iota(jnp.int32, (SLOTS, HALF), 0).astype(F32)
    pick = jnp.where(ranked == slot + first, 1.0, 0.0).astype(BF16)
    return dot(pick, beam_rows(ref, 0, CHIPS)), dot(pick, code_rows(ref)), dot(pick, index)


def half_kernel(
    ids, own_ref, step_ref, phase_ref, index_ref, z_ref, rank_ref, last_ref, gbeam_ref, gcode_ref, place_ref
):
    owner, _, _ = ids()
    ranked, last = rank_half(own_ref, owner, jnp.zeros((8, 1), F32))
    rank_ref[...] = ranked
    last_ref[...] = jnp.broadcast_to(last, (8, 128))
    gbeam_ref[...], gcode_ref[...], place_ref[...] = gather_half(
        jnp.float32(1.0), ranked[0:1, :], own_ref, index_ref[...]
    )
    transform(own_ref, step_ref, phase_ref, z_ref)


def grain_row(which):
    place = lax.broadcasted_iota(jnp.int32, (8, HALF), 1)
    grain = (2 * (place >> 5) + which) * PER_BLOCK + (place & (PER_BLOCK - 1))
    return grain.astype(F32)[0:1, :]


def spectrum_kernel(
    ids,
    own_ref, other_ref, z_ref, rank_ref, last_rank_ref, gbeam_ref, gcode_ref, place_ref,
    fold_ref, step_ref, last_ref, phases_ref, step2_ref, back_ref, phase_ref, index_ref,
    out_ref,
    z_s, gdft_s, gstep_s, gbeam_s, gcode_s, acc_s,
):
    owner, _, core = ids()
    ranked, last = rank_half(other_ref, owner, last_rank_ref[:, 0:1])
    count = jnp.max(last).astype(jnp.int32)
    transform(other_ref, step_ref, phase_ref, z_s)
    acc_s[...] = jnp.zeros(acc_s.shape, F32)
    unit = two_to(owner)
    bin_key = (
        lax.broadcasted_iota(jnp.int32, (BINS, GRAIN), 0).astype(F32) + 32.0
    ) * unit
    own_grains = jnp.broadcast_to(grain_row(core), (SLOTS, HALF))
    other_grains = jnp.broadcast_to(grain_row(1 - core), (SLOTS, HALF))
    lane_iota = lax.broadcasted_iota(jnp.int32, (SLOTS, 128), 1).astype(F32)
    core_f = core.astype(F32)

    def fold_batch(batch, gathered):
        first = (batch * SLOTS + 1).astype(F32)
        more = gather_half(first, ranked[0:1, :], other_ref, index_ref[...])
        here = gathered[0] + more[0]
        gbeam_s[...] = here
        gcode_s[...] = gathered[1] + more[1]
        place = gathered[2] + more[2]
        which = gathered[2][:, 2:3] * core_f + more[2][:, 2:3] * (1.0 - core_f)
        in_block = place[:, 1:2]
        grain = (2.0 * place[:, 0:1] + which) * float(PER_BLOCK) + in_block
        dft = jnp.zeros((SLOTS, 2 * FREQS), F32)
        ahead = jnp.zeros((SLOTS, 2 * GRAIN), F32)
        for grains, z, ref in ((own_grains, z_ref, own_ref), (other_grains, z_s, other_ref)):
            window = (grains >= grain) & (grains < grain + float(SPAN))
            dft = dft + dot(jnp.where(window, 1.0, 0.0).astype(BF16), z[...])
            next_pick = jnp.where(grains == grain + float(SPAN), 1.0, 0.0).astype(BF16)
            ahead = ahead + dot(next_pick, beam_rows(ref, 0, CHIPS))
        offset = jnp.where(in_block >= float(SPAN), in_block - float(SPAN), in_block)
        turner = jnp.where((lane_iota == offset) | (lane_iota == offset + float(SPAN)), 1.0, 0.0)
        turned = dot(turner.astype(BF16), phases_ref[...])
        real, imag = dft[:, :FREQS], dft[:, FREQS:]
        cos_g, sin_g = turned[:, :FREQS], turned[:, FREQS:]
        gdft_s[:, :FREQS] = real * cos_g - imag * sin_g
        gdft_s[:, FREQS:] = imag * cos_g + real * sin_g
        gstep_s[...] = dot((ahead - here).astype(BF16), step2_ref[...])

        def group_step(group, inner):
            rows = pl.ds(pl.multiple_of(group * GROUP, GROUP), GROUP)
            beam8, code8 = gbeam_s[rows, :], gcode_s[rows, :]
            dft8, step8 = gdft_s[rows, :], gstep_s[rows, :]
            left = []
            for k in range(GROUP):
                chosen = code8[k : k + 1, :] == bin_key
                real = jnp.where(chosen, beam8[k : k + 1, :GRAIN], 0.0)
                imag = jnp.where(chosen, beam8[k : k + 1, GRAIN:], 0.0)
                left.append(jnp.concatenate([real, imag], 1))
            left = jnp.concatenate(left, 0).astype(BF16)
            for at, factor in ((0, dft8), (2 * FREQS, step8)):
                folded = dot(left, fold_ref[:, at : at + 2 * FREQS])
                real_sum, imag_sum = acc_s[:, at : at + FREQS], acc_s[:, at + FREQS : at + 2 * FREQS]
                for k in range(GROUP):
                    part = slice(k * BINS, k * BINS + BINS)
                    real, imag = folded[part, :FREQS], folded[part, FREQS:]
                    cos_f, sin_f = factor[k : k + 1, :FREQS], factor[k : k + 1, FREQS:]
                    real_sum = real_sum + (real * cos_f - imag * sin_f)
                    imag_sum = imag_sum + (real * sin_f + imag * cos_f)
                acc_s[:, at : at + FREQS] = real_sum
                acc_s[:, at + FREQS : at + 2 * FREQS] = imag_sum
            return inner

        left_over = jnp.minimum(count - batch * SLOTS, SLOTS)
        lax.fori_loop(0, (left_over + GROUP - 1) // GROUP, group_step, 0)

    fold_batch(jnp.int32(0), (gbeam_ref[...], gcode_ref[...], place_ref[...]))

    def batch_step(batch, carry):
        first = (batch * SLOTS + 1).astype(F32)
        fold_batch(batch, gather_half(first, rank_ref[0:1, :], own_ref, index_ref[...]))
        return carry

    lax.fori_loop(1, (count + SLOTS - 1) // SLOTS, batch_step, 0)
    hi, lo = hi_lo(acc_s[:, 2 * FREQS :])
    short = dot(hi, back_ref[...]) + dot(lo, back_ref[...])
    hi, lo = hi_lo(short)
    short = dot(hi, last_ref[...]) + dot(lo, last_ref[...])
    out_ref[0] = (acc_s[:, :FREQS] + short[:, :FREQS]) * SCALE
    out_ref[1] = (acc_s[:, FREQS : 2 * FREQS] + short[:, FREQS:]) * SCALE


def near(*values):
    return [pltpu.with_memory_space_constraint(v, pltpu.VMEM) for v in values]


def call(kernel, outs, values, scratch=(), mib=8, us=1.0):
    one = not isinstance(outs, (tuple, list))
    space = pl.BlockSpec(memory_space=pltpu.VMEM)
    return pl.pallas_call(
        kernel,
        out_shape=outs if one else tuple(outs),
        in_specs=[space] * len(values),
        out_specs=space if one else (space,) * len(outs),
        scratch_shapes=list(scratch),
        compiler_params=pltpu.CompilerParams(vmem_limit_bytes=mib << 20),
        cost_estimate=pl.CostEstimate(flops=int(us * 5e8), bytes_accessed=1 << 20, transcendentals=0),
    )(*near(*values))


GATHERED = (
    pltpu.VMEM((SLOTS, 2 * GRAIN), F32),
    pltpu.VMEM((SLOTS, GRAIN), F32),
    pltpu.VMEM((SLOTS, 128), F32),
)
HALF_Z = pltpu.VMEM((HALF, 2 * FREQS), BF16)


def make_tables(ids):
    given = tables()
    made = call(
        functools.partial(table_kernel, ids),
        (
            pltpu.VMEM((2 * GRAIN, 4 * FREQS), BF16),
            pltpu.VMEM((2, 2 * GRAIN, 2 * FREQS), BF16),
            pltpu.VMEM((2 * GRAIN, 2 * FREQS), BF16),
            pltpu.VMEM((128, 2 * FREQS), BF16),
        ),
        [given[k] for k in ("base", "turn", "fold2", "phase")],
        us=3.0,
    )
    return given, made


def spectrum(own, other, ids, given, made):
    fold, step, last, phases = made
    phase, index = given["phase"], given["index"]
    half = call(
        functools.partial(half_kernel, ids),
        (HALF_Z, pltpu.VMEM((8, HALF), F32), pltpu.VMEM((8, 128), F32), *GATHERED),
        (own, step, phase, index),
        us=1.0,
    )
    scratch = [
        HALF_Z,
        pltpu.VMEM((SLOTS, 2 * FREQS), F32),
        pltpu.VMEM((SLOTS, 2 * FREQS), F32),
        GATHERED[0],
        GATHERED[1],
        pltpu.VMEM((BINS, 4 * FREQS), F32),
    ]
    return call(
        functools.partial(spectrum_kernel, ids),
        jax.ShapeDtypeStruct((2, BINS, FREQS), F32),
        (own, other, *half, fold, step, last, phases, given["step2"], given["back"], phase, index),
        scratch,
        mib=16,
        us=5.0,
    )


def front(voltages, beam_weights, bins):
    far = pl.BlockSpec(memory_space=pltpu.HBM)
    close = pl.BlockSpec(memory_space=pltpu.VMEM)
    return pl.pallas_call(
        front_kernel,
        out_shape=(
            pltpu.VMEM((DISH_WAYS, 2 * PER_BLOCK, GRAIN), F32),
            pltpu.VMEM((PER_BLOCK, GRAIN), BF16),
        ),
        in_specs=[far] * 3,
        out_specs=(close, close),
        scratch_shapes=[
            pltpu.VMEM(voltages.shape, BF16),
            pltpu.VMEM(beam_weights.shape, BF16),
            pltpu.VMEM(bins.shape, jnp.int32),
            pltpu.SemaphoreType.DMA((3,)),
        ],
        compiler_params=pltpu.CompilerParams(vmem_limit_bytes=8 << 20),
        cost_estimate=pl.CostEstimate(flops=1 << 20, bytes_accessed=1 << 20, transcendentals=0),
        name="front",
    )(*(pltpu.with_memory_space_constraint(v, pltpu.HBM) for v in (voltages, beam_weights, bins)))


def steps(voltages, beam_weights, phase_bins):
    def ids():
        core = lax.axis_index("core")
        owner = (lax.axis_index("z") * 2 + lax.axis_index("xh")) * 2 + core
        return owner, lax.axis_index("dish"), core

    given, made = make_tables(ids)
    partial_beam, coded = front(voltages, beam_weights, phase_bins.reshape(PER_BLOCK, GRAIN))
    parts = lax.all_to_all(partial_beam, "dish", 0, 0, tiled=True)
    packed = call(pack_kernel, pltpu.VMEM((CHIPS, 3 * PER_BLOCK, GRAIN), BF16), (parts, coded), us=0.3)
    own = lax.all_to_all(packed, ("z", "xh"), 0, 0, tiled=True)
    other = lax.ppermute(own, "core", [(0, 1), (1, 0)])
    return jnp.transpose(spectrum(own, other, ids, given, made), (2, 0, 1))


def solution(mesh):
    split = jax.sharding.Mesh(mesh.devices.reshape(8, 2, 2, 8), ("z", "xh", "core", "dish"))
    time = ("z", "xh", "core")
    return jax.shard_map(
        steps,
        mesh=split,
        in_specs=(P(None, "dish", time), P(None, "dish"), P(time)),
        out_specs=P("dish", None, time),
        check_vma=False,
    )
```

time: 55.7 us -> 48.1 us (0.86)
  Pallas kernels: 13.3 us -> 8.17 us
  waiting for transfers between devices: 1.35 us -> 0.09 us
  local copies, waits for them, and re-layouts: 0.75 us -> 0.04 us
    pallas_call x3 -> x5, Pallas kernels: 13.3 us -> 8.17 us  [the longest x4 6.98 us: call(): pl.pallas_call(kernel, out_shape=outs if one else tuple(outs), in_specs=[...]
    ppermute x1, waiting for transfers between devices: 1.35 us -> 0.09 us  [steps(): other = lax.ppermute(own, 'core', [(0, 1), (1, 0)])]
    unnamed x4 -> x14, local copies, waits for them, and re-layouts: 0.75 us -> 0.04 us
  transfers between devices with their start and end apart: 1 -> 1, of which waited for: 1 -> 1; matrix products, arithmetic and copies ran while one was open for 0% -> 0% of each run, Pallas kernels for 0% -> 3%
where the time goes in v3:
time: 48.1 us; the launch traced here: 47.8 us
  blocking collectives  35.8 us (74%)
  Pallas kernels  8.17 us (17%)
  starting transfers between devices  3.69 us (8%)
    all_to_all x1, blocking collectives, steps(): own = lax.all_to_all(packed, ('z', 'xh'), 0, 0, tiled=True)  23.9 us
    all_to_all x1, blocking collectives, steps(): parts = lax.all_to_all(partial_beam, 'dish', 0, 0, tiled=True)  11.9 us
    pallas_call x4, Pallas kernels, call(): pl.pallas_call(kernel, out_shape=outs if one else tuple(outs), in_specs=[...  6.98 us
    ppermute x1, starting transfers between devices, steps(): other = lax.ppermute(own, 'core', [(0, 1), (1, 0)])  3.69 us
    pallas_call x1, Pallas kernels, front(): pl.pallas_call(front_kernel, out_shape=(pltpu.VMEM((DISH_WAYS, 2 * PER_BL...  1.19 us
  transfers between devices with their start and end apart: 1, of which 1 were waited for; matrix products, arithmetic and copies ran while one was open for 0% of the time, Pallas kernels for 3%

profile of v3, /device:TPU:1, one launch (start us, length us, event | category | flops | bytes accessed | tf_op | source)
XLA Modules:
  0.0 47.8 jit_solution(13047365893932797844)
XLA Ops:
  0.0 1.2 %front.1 = (f32[8,64,128]{2,1,0:T(8,128)S(1)}, bf16[32,128]{1,0:T(8,128)(2,1)S(1)}) custom-call(bf16[2,8,4096]{2,1,0:T(8,128)(2,1)} %volts_hbm.1, bf16[2,8]{1,0:T(2,128)(2,1)} %weights_hbm.1, s32[32,128]{1,0:T(8,128)} %bitcast.2), custom_call_target="tpu_custom_call" | custom-call | flops 1048576 | bytes 1048576 | tf_op jit(solution)/shard_map/front/pallas_call | solution.py:384
  1.2 11.9 %all_to_all.10.parts_ref = f32[8,64,128]{2,1,0:T(8,128)S(1)} all-to-all(f32[8,64,128]{2,1,0:T(8,128)S(1)} %get-tuple-element.17), channel_id=1, replica_groups=mesh['z'=8,'xh'=2,'core'=2,'dish'=8] {'dish'}, dimensions={0} | all-to-all | bytes 524288 | tf_op jit(solution)/shard_map/all_to_all | solution.py:412
  13.2 0.0 copy-start.2
  13.2 0.0 copy-start.3
  13.2 0.0 copy-start.5
  13.2 0.0 copy-start.6
  13.2 23.9 %all_to_all.11.own_ref = bf16[16,96,128]{2,1,0:T(8,128)(2,1)S(1)} all-to-all(bf16[16,96,128]{2,1,0:T(8,128)(2,1)S(1)} %shard_map.100), channel_id=1, replica_groups=mesh['z'=8,'xh'=2,'core'=2,'dish'=8] {'z','xh'}, dimensions={0} | all-to-all | bytes 786432 | tf_op jit(solution)/shard_map/all_to_all | solution.py:414
  37.1 0.0 copy-start.4
  37.1 3.7 %collective-permute-start = (bf16[16,96,128]{2,1,0:T(8,128)(2,1)S(1)}, bf16[16,96,128]{2,1,0:T(8,128)(2,1)S(1)}, u32[]{:S(2)}, u32[]{:S(2)}) collective-permute-start(bf16[16,96,128]{2,1,0:T(8,128)(2,1)S(1)} %all_to_all.11.own_ref), channel_id=1, source_target_pairs={{0,8},{8,0},{1,9},{9,1},{2,10},{10,2},{3,11},{11,3},{4,12},{12,4},... | collective-permute-start | bytes 1179656 | tf_op jit(solution)/shard_map/ppermute | solution.py:415
  40.8 0.0 copy-done.2
  40.8 0.0 copy-done.3
  40.8 0.0 copy-done.5
  40.8 0.0 copy-done.6
  40.8 0.2 shard_map.101
  41.0 0.0 copy-done.4
  41.0 0.0 copy-start
  41.0 0.0 copy-start.1
  41.0 1.0 %shard_map.102 = (bf16[512,512]{1,0:T(8,128)(2,1)S(1)}, f32[8,512]{1,0:T(8,128)S(1)}, f32[8,128]{1,0:T(8,128)S(1)}, f32[128,256]{1,0:T(8,128)S(1)}, f32[128,128]{1,0:T(8,128)S(1)}, /*index=5*/f32[128,128]{1,0:T(8,128)S(1)}) custom-call(bf16[16,96,128]{2,1,0:T(8,128)(2,1)S(1)} %all_to_all.11.own_ref, bf16[2,256,512]{2,1,0:T(8,128)(2,1)S(1)} %get-tuple-element.19.step_ref, ...), custom_call_target="tpu_custom_call" | custom-call | flops 500000000 | bytes 1048576 | tf_op jit(solution)/shard_map/pallas_call | solution.py:319
  42.0 0.1 collective-permute-done.other_ref
  42.1 0.0 copy-done
  42.1 0.0 copy-done.1
  42.1 5.7 %shard_map.103 = f32[2,32,256]{2,1,0:T(8,128)} custom-call(bf16[16,96,128]{2,1,0:T(8,128)(2,1)S(1)} %all_to_all.11.own_ref, bf16[16,96,128]{2,1,0:T(8,128)(2,1)S(1)} %collective-permute-done.other_ref, bf16[512,512]{1,0:T(8,128)(2,1)S(1)} %get-tuple-element.20.z_ref, f32[8,512]{1,0:T(8,128)S(1)} %get-tuple-element.21.rank_ref, ...), custom_call_target="tpu_custom_call" | custom-call | flops 2500000000 | bytes 1048576 | tf_op jit(solution)/shard_map/pallas_call | solution.py:319
  (1 shorter events, 0.0 us)
Async XLA Ops:
  13.2 27.6 %copy-start.2 = (bf16[256,512]{1,0:T(8,128)(2,1)S(1)}, bf16[256,512]{1,0:T(8,128)(2,1)}, u32[]{:S(2)}) copy-start(bf16[256,512]{1,0:T(8,128)(2,1)} %constant.21.fold2_ref) | copy-start | bytes 786436
  13.2 27.6 %copy-start.3 = (f32[128,512]{1,0:T(8,128)S(1)}, f32[128,512]{1,0:T(8,128)}, u32[]{:S(2)}) copy-start(f32[128,512]{1,0:T(8,128)} %constant.14.clone.base_ref) | copy-start | bytes 786436
  13.2 27.6 %copy-start.5 = (f32[128,128]{1,0:T(8,128)S(1)}, f32[128,128]{1,0:T(8,128)}, u32[]{:S(2)}) copy-start(f32[128,128]{1,0:T(8,128)} %constant.15.clone.turn_ref) | copy-start | bytes 196612
  13.2 27.6 %copy-start.6 = (f32[16,512]{1,0:T(8,128)S(1)}, f32[16,512]{1,0:T(8,128)}, u32[]{:S(2)}) copy-start(f32[16,512]{1,0:T(8,128)} %constant.19.clone.phase_ref) | copy-start | bytes 98308
  37.1 3.9 %copy-start.4 = (bf16[512,128]{1,0:T(8,128)(2,1)S(1)}, bf16[512,128]{1,0:T(8,128)(2,1)}, u32[]{:S(2)}) copy-start(bf16[512,128]{1,0:T(8,128)(2,1)} %constant.22.index_ref) | copy-start | bytes 393220
  37.1 5.0 %collective-permute-start = (bf16[16,96,128]{2,1,0:T(8,128)(2,1)S(1)}, bf16[16,96,128]{2,1,0:T(8,128)(2,1)S(1)}, u32[]{:S(2)}, u32[]{:S(2)}) collective-permute-start(bf16[16,96,128]{2,1,0:T(8,128)(2,1)S(1)} %all_to_all.11.own_ref), channel_id=1, source_target_pairs={{0,8},{8,0},{1,9},{9,1},{2,10},{10,2},{3,11},{11,3},{4,12},{12,4},... | collective-permute-start | bytes 1179656 | tf_op jit(solution)/shard_map/ppermute | solution.py:415
  41.0 1.1 %copy-start = (bf16[512,256]{1,0:T(8,128)(2,1)S(1)}, bf16[512,256]{1,0:T(8,128)(2,1)}, u32[]{:S(2)}) copy-start(bf16[512,256]{1,0:T(8,128)(2,1)} %constant.24.back_ref) | copy-start | bytes 786436
  41.0 1.1 %copy-start.1 = (bf16[256,512]{1,0:T(8,128)(2,1)S(1)}, bf16[256,512]{1,0:T(8,128)(2,1)}, u32[]{:S(2)}) copy-start(bf16[256,512]{1,0:T(8,128)(2,1)} %constant.23.step2_ref) | copy-start | bytes 786436

commit v4 on v3

v4 whole, which is shorter than its diff:
```python
import functools
import math

import jax
import jax.numpy as jnp
import numpy as np
from jax import lax
from jax.experimental import pallas as pl
from jax.experimental.pallas import tpu as pltpu
from jax.sharding import PartitionSpec as P


PH = 1024
LAGS = 2048
SAMPLES = 131072
DISH_WAYS = 8
TM_WAYS = 32
CHIPS = 16
HALF = SAMPLES // 2 // 128
LOCAL = SAMPLES // TM_WAYS
GRAIN = 128
PER_BLOCK = LOCAL // GRAIN
SPAN = LAGS // GRAIN
BINS = PH // TM_WAYS
FREQS = LAGS // DISH_WAYS
SLOTS = 128
GROUP = 16
VISITS = 8
ROWS = 2 * PER_BLOCK + VISITS
SCALE = 1.0 / math.sqrt(LAGS * SAMPLES / PH)

F32 = jnp.float32
BF16 = jnp.bfloat16


def dot(a, b, dims=(((1,), (0,)), ((), ()))):
    return lax.dot_general(a, b, dims, preferred_element_type=F32)


def hi_lo(value):
    hi = value.astype(BF16)
    return hi, (value - hi.astype(F32)).astype(BF16)


def tables():
    grain = np.arange(GRAIN)
    freq = np.arange(FREQS)
    angle = 2 * np.pi * np.outer(grain, freq) / LAGS
    base = np.concatenate([np.cos(angle), np.sin(angle)], 1).astype(np.float32)
    eighth = 2 * np.pi * np.outer(grain, np.arange(DISH_WAYS)) / DISH_WAYS
    turn = np.zeros((GRAIN, 128), np.float32)
    turn[:, :8] = np.cos(eighth)
    turn[:, 8:16] = np.sin(eighth)
    fine = 2 * np.pi * np.outer(grain, np.arange(2 * GRAIN)) / (2 * GRAIN)
    cos2, sin2 = np.cos(fine), np.sin(fine)
    fold2 = np.block([[cos2, sin2], [sin2, -cos2]]).astype(np.float32)
    step2 = np.block([[cos2, -sin2], [sin2, cos2]]).astype(np.float32)
    keep = (grain >= 1)[None, :] / (2.0 * GRAIN)
    back = np.block([[cos2.T * keep, -sin2.T * keep], [sin2.T * keep, cos2.T * keep]])
    sixteenth = 2 * np.pi * np.outer(np.arange(SPAN), freq) / SPAN
    phase = np.concatenate([np.cos(sixteenth), np.sin(sixteenth)], 1).astype(np.float32)
    return {
        "base": jnp.asarray(base),
        "turn": jnp.asarray(turn),
        "fold2": jnp.asarray(fold2).astype(BF16),
        "step2": jnp.asarray(step2).astype(BF16),
        "back": jnp.asarray(back.astype(np.float32)).astype(BF16),
        "phase": jnp.asarray(phase),
    }


def front_kernel(volts_hbm, weights_hbm, beam_ref, volts_s, weights_s, sems):
    copies = [
        pltpu.make_async_copy(source, target, sems.at[k])
        for k, (source, target) in enumerate(((weights_hbm, weights_s), (volts_hbm, volts_s)))
    ]
    for copy in copies:
        copy.start()
    for copy in copies:
        copy.wait()
    weights = weights_s[...]
    first = dot(weights, volts_s[0])
    second = dot(weights, volts_s[1])
    real = first[0:1] - second[1:2]
    imag = first[1:2] + second[0:1]
    for row in range(PER_BLOCK):
        part = slice(row * GRAIN, (row + 1) * GRAIN)
        beam_ref[0, row : row + 1, :] = real[:, part]
        beam_ref[0, PER_BLOCK + row : PER_BLOCK + row + 1, :] = imag[:, part]
    rows = beam_ref[0]
    for way in range(1, DISH_WAYS):
        beam_ref[way] = rows


def pack_kernel(parts_ref, visit_ref, out_ref):
    total = parts_ref[0]
    for way in range(1, DISH_WAYS):
        total = total + parts_ref[way]
    rows = total.astype(BF16)
    for chip in range(CHIPS):
        out_ref[chip, : 2 * PER_BLOCK, :] = rows
        out_ref[chip, 2 * PER_BLOCK :, :] = visit_ref[chip]


def coded_times(shape):
    row = lax.broadcasted_iota(jnp.int32, shape, 0)
    lane = lax.broadcasted_iota(jnp.int32, shape, 1)
    return (lane + 128).astype(F32) * two_to(row)


def triangle(count, strict):
    row = lax.broadcasted_iota(jnp.int32, (count, count), 0)
    column = lax.broadcasted_iota(jnp.int32, (count, count), 1)
    return jnp.where(row < column if strict else row <= column, 1.0, 0.0).astype(BF16)


def visit_kernel(bins_ref, out_ref, time_s, row_s):
    bins = bins_ref[...]
    shape = (PER_BLOCK, GRAIN)
    row = lax.broadcasted_iota(jnp.int32, shape, 0)
    lane = lax.broadcasted_iota(jnp.int32, shape, 1)
    rolled = pltpu.roll(bins, 1, 1)
    before = jnp.where(lane == 0, pltpu.roll(rolled, 1, 0), rolled)
    later = row + lane > 0
    enters = later & (bins != before)
    wraps = jnp.where(later & (bins < before), 1.0, 0.0).astype(BF16)
    in_row = dot(wraps, triangle(GRAIN, False))
    ends = jnp.broadcast_to(in_row[:, GRAIN - 1 :], shape).astype(BF16)
    above = dot(triangle(PER_BLOCK, True), ends, (((0,), (0,)), ((), ())))
    step = bins + PH * (in_row + above).astype(jnp.int32)
    high = jnp.where(enters, step >> 7, -1)
    low = step & 127
    times = coded_times(shape)
    high_iota = lax.broadcasted_iota(jnp.int32, (48, GRAIN), 0)
    low_iota = lax.broadcasted_iota(jnp.int32, (GRAIN, GRAIN), 0)
    found = jnp.zeros((96, GRAIN), F32)
    for pair in range(PER_BLOCK // 2):
        left, right = [], []
        for k in (2 * pair, 2 * pair + 1):
            here = high[k : k + 1, :] == high_iota
            coded = jnp.where(here, times[k : k + 1, :], 0.0)
            left.append(jnp.concatenate([coded, jnp.where(here, float(k), 0.0)], 0))
            right.append(jnp.where(low[k : k + 1, :] == low_iota, 1.0, 0.0))
        left = jnp.concatenate(left, 1).astype(BF16)
        right = jnp.concatenate(right, 1).astype(BF16)
        found = found + dot(left, right, (((1,), (1,)), ((), ())))
    place = high_iota * GRAIN + lax.broadcasted_iota(jnp.int32, (48, GRAIN), 1)
    past, ahead = place <= step[0:1, 0:1], place > step[PER_BLOCK - 1 :, GRAIN - 1 :]
    time_s[:48, :] = jnp.where(past, 2.0**-9, jnp.where(ahead, 2.0**23, found[:48]))
    row_s[:48, :] = jnp.where(past, 0.0, jnp.where(ahead, 32.0, found[48:]))
    time_s[48:, :] = jnp.full((24, GRAIN), 2.0**23, F32)
    row_s[48:, :] = jnp.full((24, GRAIN), 32.0, F32)
    lane = lax.broadcasted_iota(jnp.int32, (VISITS, GRAIN), 1)
    for eighth in range(8):
        now, then = pl.ds(eighth, VISITS, stride=8), pl.ds(eighth + 1, VISITS, stride=8)
        time, rows = time_s[now, :], row_s[now, :]
        next_time, next_rows = time_s[then, :], row_s[then, :]
        even = jnp.where(lane == 65, pltpu.roll(rows, 65, 1), time)
        even = jnp.where(lane == 66, pltpu.roll(rows, 34, 1), even)
        even = jnp.where(lane == 67, pltpu.roll(rows, 3, 1), even)
        odd = jnp.where(lane == 64, pltpu.roll(next_time, 64, 1), pltpu.roll(time, 64, 1))
        odd = jnp.where(lane == 65, pltpu.roll(rows, 1, 1), odd)
        odd = jnp.where(lane == 66, pltpu.roll(rows, 98, 1), odd)
        odd = jnp.where(lane == 67, pltpu.roll(next_rows, 67, 1), odd)
        out_ref[2 * eighth] = even.astype(BF16)
        out_ref[2 * eighth + 1] = odd.astype(BF16)


def two_to(exponent):
    value = jnp.full(jnp.shape(exponent), 2.0**-16, F32)
    for bit in range(5):
        value = value * jnp.where((exponent >> bit) & 1 == 1, float(2 ** (2**bit)), 1.0)
    return value


def table_kernel(ids, base_ref, turn_ref, fold2_ref, phase_ref, fold_ref, step_ref, last_ref, phases_ref):
    _, dish, _ = ids()
    lane = lax.broadcasted_iota(jnp.int32, (GRAIN, 128), 1)
    turn = turn_ref[...]
    cos8 = jnp.sum(jnp.where(lane == dish, turn, 0.0), axis=1, keepdims=True)
    sin8 = jnp.sum(jnp.where(lane == dish + 8, turn, 0.0), axis=1, keepdims=True)
    cos0, sin0 = base_ref[:, :FREQS], base_ref[:, FREQS:]
    cosine, cosine_lo = hi_lo(cos0 * cos8 - sin0 * sin8)
    sine, sine_lo = hi_lo(sin0 * cos8 + cos0 * sin8)
    fold_ref[:GRAIN, :FREQS] = cosine
    fold_ref[:GRAIN, FREQS : 2 * FREQS] = sine
    fold_ref[GRAIN:, :FREQS] = sine
    fold_ref[GRAIN:, FREQS : 2 * FREQS] = -cosine
    fold_ref[:, 2 * FREQS :] = fold2_ref[...]
    for k, (c, s) in enumerate(((cosine, sine), (cosine_lo, sine_lo))):
        step_ref[k, :GRAIN, :FREQS] = c
        step_ref[k, :GRAIN, FREQS:] = -s
        step_ref[k, GRAIN:, :FREQS] = s
        step_ref[k, GRAIN:, FREQS:] = c
    last_ref[:GRAIN, :FREQS] = cosine
    last_ref[:GRAIN, FREQS:] = sine
    last_ref[GRAIN:, :FREQS] = -sine
    last_ref[GRAIN:, FREQS:] = cosine
    phases_ref[...] = jnp.zeros(phases_ref.shape, BF16)
    hi, lo = hi_lo(phase_ref[...])
    phases_ref[0:SPAN, :] = hi
    phases_ref[SPAN : 2 * SPAN, :] = lo


def beam_rows(ref, first, last):
    rows = [
        jnp.concatenate([ref[chip, :PER_BLOCK, :], ref[chip, PER_BLOCK : 2 * PER_BLOCK, :]], 1)
        for chip in range(first, last)
    ]
    return jnp.concatenate(rows, 0)


def transform(ref, step_ref, phase_ref, z_ref):
    cos16, sin16 = phase_ref[:, :FREQS], phase_ref[:, FREQS:]
    cos_rows = jnp.concatenate([cos16] * (128 // SPAN), 0)
    sin_rows = jnp.concatenate([sin16] * (128 // SPAN), 0)
    for tile in range(HALF // 128):
        rows = slice(tile * 128, tile * 128 + 128)
        beam = beam_rows(ref, 4 * tile, 4 * tile + 4)
        both = dot(beam, step_ref[0]) + dot(beam, step_ref[1])
        real, imag = both[:, :FREQS], both[:, FREQS:]
        z_ref[rows, :FREQS] = (real * cos_rows + imag * sin_rows).astype(BF16)
        z_ref[rows, FREQS:] = (imag * cos_rows - real * sin_rows).astype(BF16)


def plan_half(ref, core, before):
    times = jnp.concatenate([ref[chip, 2 * PER_BLOCK :, :].astype(F32) for chip in range(CHIPS)], 0).astype(BF16)
    row = lax.broadcasted_iota(jnp.int32, (8, 128), 0)
    lane = lax.broadcasted_iota(jnp.int32, (8, 128), 1)
    wanted = jnp.where(row == 0, BINS * core, jnp.where(row == 1, BINS * core + BINS, core + 63 + row))
    info = dot(jnp.where(lane == wanted, 1.0, 0.0).astype(BF16), times, (((1,), (1,)), ((), ())))
    start, end, first, last = (info[k : k + 1, :] for k in range(4))
    grains = jnp.where(end > start, jnp.minimum(last, float(PER_BLOCK - 1)) - first + 1.0, 0.0)
    earlier = dot(jnp.broadcast_to(grains, (8, 128)).astype(BF16), triangle(128, True))[0:1, :] + before
    return times, end, first, grains, earlier, earlier[:, 127:] + grains[:, 127:]


def slots_half(slot_0, plan, ref):
    times, end, first, grains, earlier, _ = plan
    slot = lax.broadcasted_iota(jnp.int32, (SLOTS, 128), 0).astype(F32) + slot_0
    visit = lax.broadcasted_iota(jnp.int32, (SLOTS, 128), 1)
    mine = (slot >= earlier) & (slot < earlier + grains)
    place = ((visit >> 3) * PER_BLOCK + 1).astype(F32) + first + (slot - earlier)
    place = jnp.sum(jnp.where(mine, place, 0.0), axis=1, keepdims=True) - 1.0
    ends = jnp.sum(jnp.where(mine, jnp.broadcast_to(end, (SLOTS, 128)), 0.0), axis=1, keepdims=True)
    starts = dot(times, jnp.where(mine, 1.0, 0.0).astype(BF16), (((0,), (1,)), ((), ())))
    places = lax.broadcasted_iota(jnp.int32, (SLOTS, HALF), 1).astype(F32)
    pick = jnp.where(places == place, 1.0, 0.0).astype(BF16)
    return place, ends, starts, dot(pick, beam_rows(ref, 0, CHIPS))


def half_kernel(ids, own_ref, step_ref, phase_ref, z_ref, total_ref, place_ref, ends_ref, starts_ref, gbeam_ref):
    _, _, core = ids()
    plan = plan_half(own_ref, core, jnp.zeros((1, 1), F32))
    place, ends, starts, beam = slots_half(jnp.float32(0.0), plan, own_ref)
    total_ref[...] = jnp.broadcast_to(plan[-1], (8, 128))
    place_ref[...] = jnp.broadcast_to(place, (SLOTS, 128))
    ends_ref[...] = jnp.broadcast_to(ends, (SLOTS, 128))
    starts_ref[...] = starts
    gbeam_ref[...] = beam
    transform(own_ref, step_ref, phase_ref, z_ref)


def grain_row(which):
    place = lax.broadcasted_iota(jnp.int32, (8, HALF), 1)
    grain = (2 * (place >> 5) + which) * PER_BLOCK + (place & (PER_BLOCK - 1))
    return grain.astype(F32)[0:1, :]


def spectrum_kernel(
    ids,
    own_ref, other_ref, z_ref, total_ref, place_ref, ends_ref, starts_ref, gbeam_ref,
    fold_ref, step_ref, last_ref, phases_ref, step2_ref, back_ref, phase_ref,
    out_ref,
    z_s, gdft_s, gstep_s, gbeam_s, gtime_s, gstart_s, acc_s,
):
    _, _, core = ids()
    before = total_ref[0:1, 0:1]
    other_plan = plan_half(other_ref, core, before)
    count = jnp.max(other_plan[-1]).astype(jnp.int32)
    transform(other_ref, step_ref, phase_ref, z_s)
    acc_s[...] = jnp.zeros(acc_s.shape, F32)
    own_grains = jnp.broadcast_to(grain_row(core), (SLOTS, HALF))
    other_grains = jnp.broadcast_to(grain_row(1 - core), (SLOTS, HALF))
    lane_iota = lax.broadcasted_iota(jnp.int32, (SLOTS, 128), 1)

    def fold_batch(batch, mine):
        first = (batch * SLOTS).astype(F32)
        more = slots_half(first, other_plan, other_ref)
        is_mine = mine[0] >= 0.0
        place = jnp.where(is_mine, mine[0], more[0]).astype(jnp.int32)
        which = jnp.where(is_mine, core, 1 - core)
        in_block = place & (PER_BLOCK - 1)
        grain = ((2 * (place >> 5) + which) * PER_BLOCK + in_block).astype(F32)
        here = mine[3] + more[3]
        times = (lane_iota + 128).astype(F32) * two_to(jnp.broadcast_to(in_block, (SLOTS, 128)))
        gtime_s[...] = times
        inside = times < mine[1] + more[1]
        gbeam_s[:, :GRAIN] = jnp.where(inside, here[:, :GRAIN], 0.0)
        gbeam_s[:, GRAIN:] = jnp.where(inside, here[:, GRAIN:], 0.0)
        starts = mine[2] + more[2]
        starts = jnp.where(core == 0, starts[:BINS], starts[BINS : 2 * BINS])
        for group in range(SLOTS // GROUP):
            gstart_s[group] = starts if group == 0 else pltpu.roll(starts, SLOTS - group * GROUP, 1)
        dft = jnp.zeros((SLOTS, 2 * FREQS), F32)
        ahead = jnp.zeros((SLOTS, 2 * GRAIN), F32)
        for grains, z, ref in ((own_grains, z_ref, own_ref), (other_grains, z_s, other_ref)):
            window = (grains >= grain) & (grains < grain + float(SPAN))
            dft = dft + dot(jnp.where(window, 1.0, 0.0).astype(BF16), z[...])
            next_pick = jnp.where(grains == grain + float(SPAN), 1.0, 0.0).astype(BF16)
            ahead = ahead + dot(next_pick, beam_rows(ref, 0, CHIPS))
        offset = in_block & (SPAN - 1)
        turner = jnp.where((lane_iota == offset) | (lane_iota == offset + SPAN), 1.0, 0.0)
        turned = dot(turner.astype(BF16), phases_ref[...])
        real, imag = dft[:, :FREQS], dft[:, FREQS:]
        cos_g, sin_g = turned[:, :FREQS], turned[:, FREQS:]
        gdft_s[:, :FREQS] = real * cos_g - imag * sin_g
        gdft_s[:, FREQS:] = imag * cos_g + real * sin_g
        gstep_s[...] = dot((ahead - here).astype(BF16), step2_ref[...])

        def group_step(group, inner):
            rows = pl.ds(pl.multiple_of(group * GROUP, GROUP), GROUP)
            beam8, time8, start8 = gbeam_s[rows, :], gtime_s[rows, :], gstart_s[group]
            dft8, step8 = gdft_s[rows, :], gstep_s[rows, :]
            left = []
            for k in range(GROUP):
                since = time8[k : k + 1, :] >= start8[:, k : k + 1]
                real = jnp.where(since, beam8[k : k + 1, :GRAIN], 0.0)
                imag = jnp.where(since, beam8[k : k + 1, GRAIN:], 0.0)
                left.append(jnp.concatenate([real, imag], 1))
            left = jnp.concatenate(left, 0).astype(BF16)
            for at, factor in ((0, dft8), (2 * FREQS, step8)):
                folded = dot(left, fold_ref[:, at : at + 2 * FREQS])
                real_sum, imag_sum = acc_s[:, at : at + FREQS], acc_s[:, at + FREQS : at + 2 * FREQS]
                for k in range(GROUP):
                    part = slice(k * BINS, k * BINS + BINS)
                    real, imag = folded[part, :FREQS], folded[part, FREQS:]
                    cos_f, sin_f = factor[k : k + 1, :FREQS], factor[k : k + 1, FREQS:]
                    real_sum = real_sum + (real * cos_f - imag * sin_f)
                    imag_sum = imag_sum + (real * sin_f + imag * cos_f)
                acc_s[:, at : at + FREQS] = real_sum
                acc_s[:, at + FREQS : at + 2 * FREQS] = imag_sum
            return inner

        left_over = jnp.minimum(count - batch * SLOTS, SLOTS)
        lax.fori_loop(0, (left_over + GROUP - 1) // GROUP, group_step, 0)

    fold_batch(jnp.int32(0), (place_ref[:, 0:1], ends_ref[:, 0:1], starts_ref[...], gbeam_ref[...]))

    def batch_step(batch, carry):
        own_plan = plan_half(own_ref, core, jnp.zeros((1, 1), F32))
        fold_batch(batch, slots_half((batch * SLOTS).astype(F32), own_plan, own_ref))
        return carry

    lax.fori_loop(1, (count + SLOTS - 1) // SLOTS, batch_step, 0)
    since = acc_s[...]
    each = since - jnp.concatenate([since[1:], jnp.zeros((1, 4 * FREQS), F32)], 0)
    hi, lo = hi_lo(each[:, 2 * FREQS :])
    short = dot(hi, back_ref[...]) + dot(lo, back_ref[...])
    hi, lo = hi_lo(short)
    short = dot(hi, last_ref[...]) + dot(lo, last_ref[...])
    out_ref[0] = (each[:, :FREQS] + short[:, :FREQS]) * SCALE
    out_ref[1] = (each[:, FREQS : 2 * FREQS] + short[:, FREQS:]) * SCALE


def near(*values):
    return [pltpu.with_memory_space_constraint(v, pltpu.VMEM) for v in values]


def call(kernel, outs, values, scratch=(), mib=8, us=1.0):
    one = not isinstance(outs, (tuple, list))
    space = pl.BlockSpec(memory_space=pltpu.VMEM)
    return pl.pallas_call(
        kernel,
        out_shape=outs if one else tuple(outs),
        in_specs=[space] * len(values),
        out_specs=space if one else (space,) * len(outs),
        scratch_shapes=list(scratch),
        compiler_params=pltpu.CompilerParams(vmem_limit_bytes=mib << 20),
        cost_estimate=pl.CostEstimate(flops=int(us * 5e8), bytes_accessed=1 << 20, transcendentals=0),
    )(*near(*values))


HALF_Z = pltpu.VMEM((HALF, 2 * FREQS), BF16)


def make_tables(ids):
    given = tables()
    made = call(
        functools.partial(table_kernel, ids),
        (
            pltpu.VMEM((2 * GRAIN, 4 * FREQS), BF16),
            pltpu.VMEM((2, 2 * GRAIN, 2 * FREQS), BF16),
            pltpu.VMEM((2 * GRAIN, 2 * FREQS), BF16),
            pltpu.VMEM((128, 2 * FREQS), BF16),
        ),
        [given[k] for k in ("base", "turn", "fold2", "phase")],
        us=3.0,
    )
    return given, made


def spectrum(own, other, ids, given, made):
    fold, step, last, phases = made
    phase = given["phase"]
    half = call(
        functools.partial(half_kernel, ids),
        (
            HALF_Z,
            pltpu.VMEM((8, 128), F32),
            pltpu.VMEM((SLOTS, 128), F32),
            pltpu.VMEM((SLOTS, 128), F32),
            pltpu.VMEM((128, SLOTS), F32),
            pltpu.VMEM((SLOTS, 2 * GRAIN), F32),
        ),
        (own, step, phase),
        us=1.0,
    )
    scratch = [
        HALF_Z,
        pltpu.VMEM((SLOTS, 2 * FREQS), F32),
        pltpu.VMEM((SLOTS, 2 * FREQS), F32),
        pltpu.VMEM((SLOTS, 2 * GRAIN), F32),
        pltpu.VMEM((SLOTS, GRAIN), F32),
        pltpu.VMEM((SLOTS // GROUP, BINS, 128), F32),
        pltpu.VMEM((BINS, 4 * FREQS), F32),
    ]
    return call(
        functools.partial(spectrum_kernel, ids),
        jax.ShapeDtypeStruct((2, BINS, FREQS), F32),
        (own, other, *half, fold, step, last, phases, given["step2"], given["back"], phase),
        scratch,
        mib=16,
        us=5.0,
    )


def front(voltages, beam_weights):
    far = pl.BlockSpec(memory_space=pltpu.HBM)
    return pl.pallas_call(
        front_kernel,
        out_shape=pltpu.VMEM((DISH_WAYS, 2 * PER_BLOCK, GRAIN), F32),
        in_specs=[far] * 2,
        out_specs=pl.BlockSpec(memory_space=pltpu.VMEM),
        scratch_shapes=[
            pltpu.VMEM(voltages.shape, BF16),
            pltpu.VMEM(beam_weights.shape, BF16),
            pltpu.SemaphoreType.DMA((2,)),
        ],
        compiler_params=pltpu.CompilerParams(vmem_limit_bytes=8 << 20),
        cost_estimate=pl.CostEstimate(flops=1 << 20, bytes_accessed=1 << 20, transcendentals=0),
        name="front",
    )(*(pltpu.with_memory_space_constraint(v, pltpu.HBM) for v in (voltages, beam_weights)))


def steps(voltages, beam_weights, phase_bins):
    def ids():
        core = lax.axis_index("core")
        owner = (lax.axis_index("z") * 2 + lax.axis_index("xh")) * 2 + core
        return owner, lax.axis_index("dish"), core

    given, made = make_tables(ids)
    visits = call(
        visit_kernel,
        pltpu.VMEM((CHIPS, VISITS, GRAIN), BF16),
        (phase_bins.reshape(PER_BLOCK, GRAIN),),
        [pltpu.VMEM((72, GRAIN), F32)] * 2,
        us=3.0,
    )
    partial_beam = front(voltages, beam_weights)
    parts = lax.all_to_all(partial_beam, "dish", 0, 0, tiled=True)
    packed = call(pack_kernel, pltpu.VMEM((CHIPS, ROWS, GRAIN), BF16), (parts, visits), us=0.3)
    own = lax.all_to_all(packed, ("z", "xh"), 0, 0, tiled=True)
    other = lax.ppermute(own, "core", [(0, 1), (1, 0)])
    return jnp.transpose(spectrum(own, other, ids, given, made), (2, 0, 1))


def solution(mesh):
    split = jax.sharding.Mesh(mesh.devices.reshape(8, 2, 2, 8), ("z", "xh", "core", "dish"))
    time = ("z", "xh", "core")
    return jax.shard_map(
        steps,
        mesh=split,
        in_specs=(P(None, "dish", time), P(None, "dish"), P(time)),
        out_specs=P("dish", None, time),
        check_vma=False,
    )
```

time: 48.1 us -> 47.1 us (0.979)
  blocking collectives: 35.8 us -> 21.8 us
  starting transfers between devices: 3.69 us -> 9.83 us
  waiting for transfers between devices: 0.09 us -> 5.35 us
  Pallas kernels: 8.17 us -> 9.7 us
    all_to_all x1 -> x0, blocking collectives: 11.9 us -> none  [steps(): parts = lax.all_to_all(partial_beam, 'dish', 0, 0, tiled=True)]
    all_to_all x0 -> x1, starting transfers between devices: none -> 5.95 us  [steps(): parts = lax.all_to_all(partial_beam, 'dish', 0, 0, tiled=True)]
    all_to_all x0 -> x1, waiting for transfers between devices: none -> 5.2 us  [steps(): parts = lax.all_to_all(partial_beam, 'dish', 0, 0, tiled=True)]
    all_to_all x1, blocking collectives: 23.9 us -> 21.8 us  [steps(): own = lax.all_to_all(packed, ('z', 'xh'), 0, 0, tiled=True)]
    pallas_call x4 -> x5, Pallas kernels: 6.98 us -> 7.83 us  [call(): pl.pallas_call(kernel, out_shape=outs if one else tuple(outs), in_specs=[...]
    pallas_call x1, Pallas kernels: 1.19 us -> 1.87 us  [front(): pl.pallas_call(front_kernel, out_shape=pltpu.VMEM((DISH_WAYS, 2 * PER_BLO...]
  transfers between devices with their start and end apart: 1 -> 2, of which waited for: 1 -> 2; matrix products, arithmetic and copies ran while one was open for 0% -> 0% of each run, Pallas kernels for 3% -> 4%
where the time goes in v4:
time: 47.1 us; the launch traced here: 46.9 us
  blocking collectives  21.8 us (46%)
  starting transfers between devices  9.83 us (21%)
  Pallas kernels  9.7 us (21%)
  waiting for transfers between devices  5.35 us (11%)
    all_to_all x1, blocking collectives, steps(): own = lax.all_to_all(packed, ('z', 'xh'), 0, 0, tiled=True)  21.8 us
    pallas_call x5, Pallas kernels, call(): pl.pallas_call(kernel, out_shape=outs if one else tuple(outs), in_specs=[...  7.83 us
    all_to_all x1, starting transfers between devices, steps(): parts = lax.all_to_all(partial_beam, 'dish', 0, 0, tiled=True)  5.95 us
    all_to_all x1, waiting for transfers between devices, steps(): parts = lax.all_to_all(partial_beam, 'dish', 0, 0, tiled=True)  5.2 us
    ppermute x1, starting transfers between devices, steps(): other = lax.ppermute(own, 'core', [(0, 1), (1, 0)])  3.88 us
    pallas_call x1, Pallas kernels, front(): pl.pallas_call(front_kernel, out_shape=pltpu.VMEM((DISH_WAYS, 2 * PER_BLO...  1.87 us
  transfers between devices with their start and end apart: 2, of which 2 were waited for; matrix products, arithmetic and copies ran while one was open for 0% of the time, Pallas kernels for 4%

profile of v4, /device:TPU:1, one launch (start us, length us, event | category | flops | bytes accessed | tf_op | source)
XLA Modules:
  0.0 46.9 jit_solution(14864062820962189207)
XLA Ops:
  0.0 1.9 %front.1 = f32[8,64,128]{2,1,0:T(8,128)} custom-call(bf16[2,8,4096]{2,1,0:T(8,128)(2,1)} %volts_hbm.1, bf16[2,8]{1,0:T(2,128)(2,1)} %weights_hbm.1), custom_call_target="tpu_custom_call" | custom-call | flops 1048576 | bytes 1048576 | tf_op jit(solution)/shard_map/front/pallas_call | solution.py:440
  1.9 0.0 copy-start
  1.9 5.9 %all-to-all-start = ((f32[8,64,128]{2,1,0:T(8,128)}), f32[8,64,128]{2,1,0:T(8,128)S(1)}, u32[]{:S(2)}, u32[]{:S(2)}) async-start(f32[8,64,128]{2,1,0:T(8,128)} %front.1), calls=%async_computation | async-start | bytes 524288 | tf_op jit(solution)/shard_map/all_to_all | solution.py:471
  7.8 0.0 copy-done
  7.8 1.0 %shard_map.91.visit_ref = bf16[16,8,128]{2,1,0:T(8,128)(2,1)S(1)} custom-call(s32[32,128]{1,0:T(8,128)S(1)} %bitcast.2), custom_call_target="tpu_custom_call" | custom-call | flops 1500000000 | bytes 1048576 | tf_op jit(solution)/shard_map/pallas_call | solution.py:373
  8.8 5.2 %all-to-all-done.parts_ref = f32[8,64,128]{2,1,0:T(8,128)S(1)} async-done(((f32[8,64,128]{2,1,0:T(8,128)}), f32[8,64,128]{2,1,0:T(8,128)S(1)}, u32[]{:S(2)}, u32[]{:S(2)}) %all-to-all-start) | async-done | bytes 262176 | tf_op jit(solution)/shard_map/all_to_all | solution.py:471
  14.0 0.0 copy-start.6
  14.1 0.0 copy-start.3
  14.1 0.0 copy-start.4
  14.1 0.0 copy-start.5
  14.1 21.8 %all_to_all.10.own_ref = bf16[16,72,128]{2,1,0:T(8,128)(2,1)S(1)} all-to-all(bf16[16,72,128]{2,1,0:T(8,128)(2,1)S(1)} %shard_map.92), channel_id=1, replica_groups=mesh['z'=8,'xh'=2,'core'=2,'dish'=8] {'z','xh'}, dimensions={0} | all-to-all | bytes 589824 | tf_op jit(solution)/shard_map/all_to_all | solution.py:473
  35.9 3.9 %collective-permute-start = (bf16[16,72,128]{2,1,0:T(8,128)(2,1)S(1)}, bf16[16,72,128]{2,1,0:T(8,128)(2,1)S(1)}, u32[]{:S(2)}, u32[]{:S(2)}) collective-permute-start(bf16[16,72,128]{2,1,0:T(8,128)(2,1)S(1)} %all_to_all.10.own_ref), channel_id=1, source_target_pairs={{0,8},{8,0},{1,9},{9,1},{2,10},{10,2},{3,11},{11,3},{4,12},{12,4},... | collective-permute-start | bytes 884744 | tf_op jit(solution)/shard_map/ppermute | solution.py:474
  39.8 0.0 copy-done.6
  39.8 0.0 copy-done.3
  39.8 0.0 copy-done.4
  39.8 0.0 copy-done.5
  39.8 0.2 shard_map.93
  40.0 0.0 copy-start.1
  40.0 0.0 copy-start.2
  40.0 0.8 %shard_map.94 = (bf16[512,512]{1,0:T(8,128)(2,1)S(1)}, f32[8,128]{1,0:T(8,128)S(1)}, f32[128,128]{1,0:T(8,128)S(1)}, f32[128,128]{1,0:T(8,128)S(1)}, f32[128,128]{1,0:T(8,128)S(1)}, /*index=5*/f32[128,256]{1,0:T(8,128)S(1)}) custom-call(bf16[16,72,128]{2,1,0:T(8,128)(2,1)S(1)} %all_to_all.10.own_ref, bf16[2,256,512]{2,1,0:T(8,128)(2,1)S(1)} %get-tuple-element.15.step_ref, ...), custom_call_target="tpu_custom_call" | custom-call | flops 500000000 | bytes 1048576 | tf_op jit(solution)/shard_map/pallas_call | solution.py:373
  40.8 0.2 collective-permute-done.other_ref
  41.0 0.0 copy-done.1
  41.0 0.0 copy-done.2
  41.0 5.8 %shard_map.95 = f32[2,32,256]{2,1,0:T(8,128)} custom-call(bf16[16,72,128]{2,1,0:T(8,128)(2,1)S(1)} %all_to_all.10.own_ref, bf16[16,72,128]{2,1,0:T(8,128)(2,1)S(1)} %collective-permute-done.other_ref, bf16[512,512]{1,0:T(8,128)(2,1)S(1)} %get-tuple-element.16.z_ref, f32[8,128]{1,0:T(8,128)S(1)} %get-tuple-element.17.total_ref, ...), custom_call_target="tpu_custom_call" | custom-call | flops 2500000000 | bytes 1048576 | tf_op jit(solution)/shard_map/pallas_call | solution.py:373
  (1 shorter events, 0.0 us)
Async XLA Ops:
  1.9 6.0 %copy-start = (s32[4096]{0:T(1024)S(1)}, s32[4096]{0:T(1024)}, u32[]{:S(2)}) copy-start(s32[4096]{0:T(1024)} %param.11) | copy-start | bytes 49156
  1.9 12.1 %all-to-all-start = ((f32[8,64,128]{2,1,0:T(8,128)}), f32[8,64,128]{2,1,0:T(8,128)S(1)}, u32[]{:S(2)}, u32[]{:S(2)}) async-start(f32[8,64,128]{2,1,0:T(8,128)} %front.1), calls=%async_computation | async-start | bytes 524288 | tf_op jit(solution)/shard_map/all_to_all | solution.py:471
  14.0 25.8 %copy-start.6 = (f32[16,512]{1,0:T(8,128)S(1)}, f32[16,512]{1,0:T(8,128)}, u32[]{:S(2)}) copy-start(f32[16,512]{1,0:T(8,128)} %constant.17.clone.phase_ref) | copy-start | bytes 98308
  14.1 25.7 %copy-start.3 = (bf16[256,512]{1,0:T(8,128)(2,1)S(1)}, bf16[256,512]{1,0:T(8,128)(2,1)}, u32[]{:S(2)}) copy-start(bf16[256,512]{1,0:T(8,128)(2,1)} %constant.18.fold2_ref) | copy-start | bytes 786436
  14.1 25.7 %copy-start.4 = (f32[128,512]{1,0:T(8,128)S(1)}, f32[128,512]{1,0:T(8,128)}, u32[]{:S(2)}) copy-start(f32[128,512]{1,0:T(8,128)} %constant.12.clone.base_ref) | copy-start | bytes 786436
  14.1 25.7 %copy-start.5 = (f32[128,128]{1,0:T(8,128)S(1)}, f32[128,128]{1,0:T(8,128)}, u32[]{:S(2)}) copy-start(f32[128,128]{1,0:T(8,128)} %constant.13.clone.turn_ref) | copy-start | bytes 196612
  35.9 5.1 %collective-permute-start = (bf16[16,72,128]{2,1,0:T(8,128)(2,1)S(1)}, bf16[16,72,128]{2,1,0:T(8,128)(2,1)S(1)}, u32[]{:S(2)}, u32[]{:S(2)}) collective-permute-start(bf16[16,72,128]{2,1,0:T(8,128)(2,1)S(1)} %all_to_all.10.own_ref), channel_id=1, source_target_pairs={{0,8},{8,0},{1,9},{9,1},{2,10},{10,2},{3,11},{11,3},{4,12},{12,4},... | collective-permute-start | bytes 884744 | tf_op jit(solution)/shard_map/ppermute | solution.py:474
  40.0 1.0 %copy-start.1 = (bf16[512,256]{1,0:T(8,128)(2,1)S(1)}, bf16[512,256]{1,0:T(8,128)(2,1)}, u32[]{:S(2)}) copy-start(bf16[512,256]{1,0:T(8,128)(2,1)} %constant.20.back_ref) | copy-start | bytes 786436
  40.0 1.0 %copy-start.2 = (bf16[256,512]{1,0:T(8,128)(2,1)S(1)}, bf16[256,512]{1,0:T(8,128)(2,1)}, u32[]{:S(2)}) copy-start(bf16[256,512]{1,0:T(8,128)(2,1)} %constant.19.step2_ref) | copy-start | bytes 786436

commit v5 on v4

--- a/solution.py
+++ b/solution.py
@@ -69,7 +69,7 @@
     }
 
 
-def front_kernel(volts_hbm, weights_hbm, beam_ref, volts_s, weights_s, sems):
+def front_kernel(volts_hbm, weights_hbm, beam_hbm, volts_s, weights_s, beam_s, sems):
     copies = [
         pltpu.make_async_copy(source, target, sems.at[k])
         for k, (source, target) in enumerate(((weights_hbm, weights_s), (volts_hbm, volts_s)))
@@ -85,11 +85,15 @@
     imag = first[1:2] + second[0:1]
     for row in range(PER_BLOCK):
         part = slice(row * GRAIN, (row + 1) * GRAIN)
-        beam_ref[0, row : row + 1, :] = real[:, part]
-        beam_ref[0, PER_BLOCK + row : PER_BLOCK + row + 1, :] = imag[:, part]
-    rows = beam_ref[0]
-    for way in range(1, DISH_WAYS):
-        beam_ref[way] = rows
+        beam_s[row : row + 1, :] = real[:, part]
+        beam_s[PER_BLOCK + row : PER_BLOCK + row + 1, :] = imag[:, part]
+    copies = [
+        pltpu.make_async_copy(beam_s, beam_hbm.at[way], sems.at[2 + way]) for way in range(DISH_WAYS)
+    ]
+    for copy in copies:
+        copy.start()
+    for copy in copies:
+        copy.wait()
 
 
 def pack_kernel(parts_ref, visit_ref, out_ref):
@@ -272,7 +276,7 @@
     own_ref, other_ref, z_ref, total_ref, place_ref, ends_ref, starts_ref, gbeam_ref,
     fold_ref, step_ref, last_ref, phases_ref, step2_ref, back_ref, phase_ref,
     out_ref,
-    z_s, gdft_s, gstep_s, gbeam_s, gtime_s, gstart_s, acc_s,
+    z_s, gdft_s, gstep_s, gbeam_s, gtime_s, gstart_s, acc_s, fold_s,
 ):
     _, _, core = ids()
     before = total_ref[0:1, 0:1]
@@ -280,6 +284,7 @@
     count = jnp.max(other_plan[-1]).astype(jnp.int32)
     transform(other_ref, step_ref, phase_ref, z_s)
     acc_s[...] = jnp.zeros(acc_s.shape, F32)
+    fold_s[...] = fold_ref[...]
     own_grains = jnp.broadcast_to(grain_row(core), (SLOTS, HALF))
     other_grains = jnp.broadcast_to(grain_row(1 - core), (SLOTS, HALF))
     lane_iota = lax.broadcasted_iota(jnp.int32, (SLOTS, 128), 1)
@@ -314,9 +319,14 @@
         turned = dot(turner.astype(BF16), phases_ref[...])
         real, imag = dft[:, :FREQS], dft[:, FREQS:]
         cos_g, sin_g = turned[:, :FREQS], turned[:, FREQS:]
-        gdft_s[:, :FREQS] = real * cos_g - imag * sin_g
-        gdft_s[:, FREQS:] = imag * cos_g + real * sin_g
-        gstep_s[...] = dot((ahead - here).astype(BF16), step2_ref[...])
+        step = dot((ahead - here).astype(BF16), step2_ref[...])
+        for ref, real, imag in (
+            (gdft_s, real * cos_g - imag * sin_g, imag * cos_g + real * sin_g),
+            (gstep_s, step[:, :FREQS], step[:, FREQS:]),
+        ):
+            ref[:, :FREQS] = real
+            ref[:, FREQS : 2 * FREQS] = imag - real
+            ref[:, 2 * FREQS :] = real + imag
 
         def group_step(group, inner):
             rows = pl.ds(pl.multiple_of(group * GROUP, GROUP), GROUP)
@@ -329,21 +339,25 @@
                 imag = jnp.where(since, beam8[k : k + 1, GRAIN:], 0.0)
                 left.append(jnp.concatenate([real, imag], 1))
             left = jnp.concatenate(left, 0).astype(BF16)
-            for at, factor in ((0, dft8), (2 * FREQS, step8)):
-                folded = dot(left, fold_ref[:, at : at + 2 * FREQS])
-                real_sum, imag_sum = acc_s[:, at : at + FREQS], acc_s[:, at + FREQS : at + 2 * FREQS]
+            for part, factor in ((0, dft8), (1, step8)):
+                folded = dot(left, fold_s[:, part * 2 * FREQS : part * 2 * FREQS + 2 * FREQS])
+                sums = [acc_s[:, k * FREQS : k * FREQS + FREQS] for k in range(3 * part, 3 * part + 3)]
                 for k in range(GROUP):
-                    part = slice(k * BINS, k * BINS + BINS)
-                    real, imag = folded[part, :FREQS], folded[part, FREQS:]
-                    cos_f, sin_f = factor[k : k + 1, :FREQS], factor[k : k + 1, FREQS:]
-                    real_sum = real_sum + (real * cos_f - imag * sin_f)
-                    imag_sum = imag_sum + (real * sin_f + imag * cos_f)
-                acc_s[:, at : at + FREQS] = real_sum
-                acc_s[:, at + FREQS : at + 2 * FREQS] = imag_sum
+                    rows = slice(k * BINS, k * BINS + BINS)
+                    real, imag = folded[rows, :FREQS], folded[rows, FREQS:]
+                    for n, value in enumerate((real + imag, real, imag)):
+                        sums[n] = sums[n] + value * factor[k : k + 1, n * FREQS : n * FREQS + FREQS]
+                for n in range(3):
+                    acc_s[:, (3 * part + n) * FREQS : (3 * part + n + 1) * FREQS] = sums[n]
             return inner
 
-        left_over = jnp.minimum(count - batch * SLOTS, SLOTS)
-        lax.fori_loop(0, (left_over + GROUP - 1) // GROUP, group_step, 0)
+        def pair_step(pair, inner):
+            group_step(2 * pair, inner)
+            return group_step(2 * pair + 1, inner)
+
+        groups = (jnp.minimum(count - batch * SLOTS, SLOTS) + GROUP - 1) // GROUP
+        lax.fori_loop(0, groups // 2, pair_step, 0)
+        lax.fori_loop(groups // 2 * 2, groups, group_step, 0)
 
     fold_batch(jnp.int32(0), (place_ref[:, 0:1], ends_ref[:, 0:1], starts_ref[...], gbeam_ref[...]))
 
@@ -354,13 +368,14 @@
 
     lax.fori_loop(1, (count + SLOTS - 1) // SLOTS, batch_step, 0)
     since = acc_s[...]
-    each = since - jnp.concatenate([since[1:], jnp.zeros((1, 4 * FREQS), F32)], 0)
-    hi, lo = hi_lo(each[:, 2 * FREQS :])
+    each = since - jnp.concatenate([since[1:], jnp.zeros((1, 6 * FREQS), F32)], 0)
+    both, real, imag, both2, real2, imag2 = (each[:, k * FREQS : k * FREQS + FREQS] for k in range(6))
+    hi, lo = hi_lo(jnp.concatenate([both2 - imag2, both2 + real2], 1))
     short = dot(hi, back_ref[...]) + dot(lo, back_ref[...])
     hi, lo = hi_lo(short)
     short = dot(hi, last_ref[...]) + dot(lo, last_ref[...])
-    out_ref[0] = (each[:, :FREQS] + short[:, :FREQS]) * SCALE
-    out_ref[1] = (each[:, FREQS : 2 * FREQS] + short[:, FREQS:]) * SCALE
+    out_ref[0] = (both - imag + short[:, :FREQS]) * SCALE
+    out_ref[1] = (both + real + short[:, FREQS:]) * SCALE
 
 
 def near(*values):
@@ -418,12 +433,13 @@
     )
     scratch = [
         HALF_Z,
-        pltpu.VMEM((SLOTS, 2 * FREQS), F32),
-        pltpu.VMEM((SLOTS, 2 * FREQS), F32),
+        pltpu.VMEM((SLOTS, 3 * FREQS), F32),
+        pltpu.VMEM((SLOTS, 3 * FREQS), F32),
         pltpu.VMEM((SLOTS, 2 * GRAIN), F32),
         pltpu.VMEM((SLOTS, GRAIN), F32),
         pltpu.VMEM((SLOTS // GROUP, BINS, 128), F32),
-        pltpu.VMEM((BINS, 4 * FREQS), F32),
+        pltpu.VMEM((BINS, 6 * FREQS), F32),
+        pltpu.VMEM((2 * GRAIN, 4 * FREQS), BF16),
     ]
     return call(
         functools.partial(spectrum_kernel, ids),
@@ -439,13 +455,14 @@
     far = pl.BlockSpec(memory_space=pltpu.HBM)
     return pl.pallas_call(
         front_kernel,
-        out_shape=pltpu.VMEM((DISH_WAYS, 2 * PER_BLOCK, GRAIN), F32),
+        out_shape=jax.ShapeDtypeStruct((DISH_WAYS, 2 * PER_BLOCK, GRAIN), F32),
         in_specs=[far] * 2,
-        out_specs=pl.BlockSpec(memory_space=pltpu.VMEM),
+        out_specs=far,
         scratch_shapes=[
             pltpu.VMEM(voltages.shape, BF16),
             pltpu.VMEM(beam_weights.shape, BF16),
-            pltpu.SemaphoreType.DMA((2,)),
+            pltpu.VMEM((2 * PER_BLOCK, GRAIN), F32),
+            pltpu.SemaphoreType.DMA((2 + DISH_WAYS,)),
         ],
         compiler_params=pltpu.CompilerParams(vmem_limit_bytes=8 << 20),
         cost_estimate=pl.CostEstimate(flops=1 << 20, bytes_accessed=1 << 20, transcendentals=0),

time: 47.1 us -> 46.5 us (0.987)
  Pallas kernels: 9.7 us -> 9.1 us
    pallas_call x5, Pallas kernels: 7.83 us -> 7.18 us  [call(): pl.pallas_call(kernel, out_shape=outs if one else tuple(outs), in_specs=[...]
where the time goes in v5:
time: 46.5 us; the launch traced here: 46.3 us
  blocking collectives  21.8 us (47%)
  starting transfers between devices  9.83 us (21%)
  Pallas kernels  9.1 us (20%)
  waiting for transfers between devices  5.36 us (12%)
    all_to_all x1, blocking collectives, steps(): own = lax.all_to_all(packed, ('z', 'xh'), 0, 0, tiled=True)  21.8 us
    pallas_call x5, Pallas kernels, call(): pl.pallas_call(kernel, out_shape=outs if one else tuple(outs), in_specs=[...  7.18 us
    all_to_all x1, starting transfers between devices, steps(): parts = lax.all_to_all(partial_beam, 'dish', 0, 0, tiled=True)  5.95 us
    all_to_all x1, waiting for transfers between devices, steps(): parts = lax.all_to_all(partial_beam, 'dish', 0, 0, tiled=True)  5.2 us
    ppermute x1, starting transfers between devices, steps(): other = lax.ppermute(own, 'core', [(0, 1), (1, 0)])  3.88 us
    pallas_call x1, Pallas kernels, front(): pl.pallas_call(front_kernel, out_shape=jax.ShapeDtypeStruct((DISH_WAYS, 2...  1.91 us
  transfers between devices with their start and end apart: 2, of which 2 were waited for; matrix products, arithmetic and copies ran while one was open for 0% of the time, Pallas kernels for 4%

profile of v5, /device:TPU:1, one launch (start us, length us, event | category | flops | bytes accessed | tf_op | source)
XLA Modules:
  0.0 46.3 jit_solution(17320639847985008011)
XLA Ops:
  0.0 1.9 %front.1 = f32[8,64,128]{2,1,0:T(8,128)} custom-call(bf16[2,8,4096]{2,1,0:T(8,128)(2,1)} %volts_hbm.1, bf16[2,8]{1,0:T(2,128)(2,1)} %weights_hbm.1), custom_call_target="tpu_custom_call" | custom-call | flops 1048576 | bytes 1048576 | tf_op jit(solution)/shard_map/front/pallas_call | solution.py:456
  1.9 0.0 copy-start
  1.9 5.9 %all-to-all-start = ((f32[8,64,128]{2,1,0:T(8,128)}), f32[8,64,128]{2,1,0:T(8,128)S(1)}, u32[]{:S(2)}, u32[]{:S(2)}) async-start(f32[8,64,128]{2,1,0:T(8,128)} %front.1), calls=%async_computation | async-start | bytes 524288 | tf_op jit(solution)/shard_map/all_to_all | solution.py:488
  7.9 0.0 copy-done
  7.9 1.0 %shard_map.91.visit_ref = bf16[16,8,128]{2,1,0:T(8,128)(2,1)S(1)} custom-call(s32[32,128]{1,0:T(8,128)S(1)} %bitcast.2), custom_call_target="tpu_custom_call" | custom-call | flops 1500000000 | bytes 1048576 | tf_op jit(solution)/shard_map/pallas_call | solution.py:388
  8.9 5.2 %all-to-all-done.parts_ref = f32[8,64,128]{2,1,0:T(8,128)S(1)} async-done(((f32[8,64,128]{2,1,0:T(8,128)}), f32[8,64,128]{2,1,0:T(8,128)S(1)}, u32[]{:S(2)}, u32[]{:S(2)}) %all-to-all-start) | async-done | bytes 262176 | tf_op jit(solution)/shard_map/all_to_all | solution.py:488
  14.1 0.0 copy-start.6
  14.1 0.0 copy-start.3
  14.1 0.0 copy-start.4
  14.1 0.0 copy-start.5
  14.1 21.8 %all_to_all.10.own_ref = bf16[16,72,128]{2,1,0:T(8,128)(2,1)S(1)} all-to-all(bf16[16,72,128]{2,1,0:T(8,128)(2,1)S(1)} %shard_map.92), channel_id=1, replica_groups=mesh['z'=8,'xh'=2,'core'=2,'dish'=8] {'z','xh'}, dimensions={0} | all-to-all | bytes 589824 | tf_op jit(solution)/shard_map/all_to_all | solution.py:490
  35.9 3.9 %collective-permute-start = (bf16[16,72,128]{2,1,0:T(8,128)(2,1)S(1)}, bf16[16,72,128]{2,1,0:T(8,128)(2,1)S(1)}, u32[]{:S(2)}, u32[]{:S(2)}) collective-permute-start(bf16[16,72,128]{2,1,0:T(8,128)(2,1)S(1)} %all_to_all.10.own_ref), channel_id=1, source_target_pairs={{0,8},{8,0},{1,9},{9,1},{2,10},{10,2},{3,11},{11,3},{4,12},{12,4},... | collective-permute-start | bytes 884744 | tf_op jit(solution)/shard_map/ppermute | solution.py:491
  39.8 0.0 copy-done.6
  39.8 0.0 copy-done.3
  39.8 0.0 copy-done.4
  39.8 0.0 copy-done.5
  39.8 0.2 shard_map.93
  40.0 0.0 copy-start.1
  40.0 0.0 copy-start.2
  40.1 0.8 %shard_map.94 = (bf16[512,512]{1,0:T(8,128)(2,1)S(1)}, f32[8,128]{1,0:T(8,128)S(1)}, f32[128,128]{1,0:T(8,128)S(1)}, f32[128,128]{1,0:T(8,128)S(1)}, f32[128,128]{1,0:T(8,128)S(1)}, /*index=5*/f32[128,256]{1,0:T(8,128)S(1)}) custom-call(bf16[16,72,128]{2,1,0:T(8,128)(2,1)S(1)} %all_to_all.10.own_ref, bf16[2,256,512]{2,1,0:T(8,128)(2,1)S(1)} %get-tuple-element.15.step_ref, ...), custom_call_target="tpu_custom_call" | custom-call | flops 500000000 | bytes 1048576 | tf_op jit(solution)/shard_map/pallas_call | solution.py:388
  40.9 0.2 collective-permute-done.other_ref
  41.0 0.0 copy-done.1
  41.0 0.0 copy-done.2
  41.1 5.2 %shard_map.95 = f32[2,32,256]{2,1,0:T(8,128)} custom-call(bf16[16,72,128]{2,1,0:T(8,128)(2,1)S(1)} %all_to_all.10.own_ref, bf16[16,72,128]{2,1,0:T(8,128)(2,1)S(1)} %collective-permute-done.other_ref, bf16[512,512]{1,0:T(8,128)(2,1)S(1)} %get-tuple-element.16.z_ref, f32[8,128]{1,0:T(8,128)S(1)} %get-tuple-element.17.total_ref, ...), custom_call_target="tpu_custom_call" | custom-call | flops 2500000000 | bytes 1048576 | tf_op jit(solution)/shard_map/pallas_call | solution.py:388
  (1 shorter events, 0.0 us)
Async XLA Ops:
  1.9 6.0 %copy-start = (s32[4096]{0:T(1024)S(1)}, s32[4096]{0:T(1024)}, u32[]{:S(2)}) copy-start(s32[4096]{0:T(1024)} %param.11) | copy-start | bytes 49156
  1.9 12.1 %all-to-all-start = ((f32[8,64,128]{2,1,0:T(8,128)}), f32[8,64,128]{2,1,0:T(8,128)S(1)}, u32[]{:S(2)}, u32[]{:S(2)}) async-start(f32[8,64,128]{2,1,0:T(8,128)} %front.1), calls=%async_computation | async-start | bytes 524288 | tf_op jit(solution)/shard_map/all_to_all | solution.py:488
  14.1 25.8 %copy-start.6 = (f32[16,512]{1,0:T(8,128)S(1)}, f32[16,512]{1,0:T(8,128)}, u32[]{:S(2)}) copy-start(f32[16,512]{1,0:T(8,128)} %constant.17.clone.phase_ref) | copy-start | bytes 98308
  14.1 25.7 %copy-start.3 = (bf16[256,512]{1,0:T(8,128)(2,1)S(1)}, bf16[256,512]{1,0:T(8,128)(2,1)}, u32[]{:S(2)}) copy-start(bf16[256,512]{1,0:T(8,128)(2,1)} %constant.18.fold2_ref) | copy-start | bytes 786436
  14.1 25.7 %copy-start.4 = (f32[128,512]{1,0:T(8,128)S(1)}, f32[128,512]{1,0:T(8,128)}, u32[]{:S(2)}) copy-start(f32[128,512]{1,0:T(8,128)} %constant.12.clone.base_ref) | copy-start | bytes 786436
  14.1 25.7 %copy-start.5 = (f32[128,128]{1,0:T(8,128)S(1)}, f32[128,128]{1,0:T(8,128)}, u32[]{:S(2)}) copy-start(f32[128,128]{1,0:T(8,128)} %constant.13.clone.turn_ref) | copy-start | bytes 196612
  35.9 5.1 %collective-permute-start = (bf16[16,72,128]{2,1,0:T(8,128)(2,1)S(1)}, bf16[16,72,128]{2,1,0:T(8,128)(2,1)S(1)}, u32[]{:S(2)}, u32[]{:S(2)}) collective-permute-start(bf16[16,72,128]{2,1,0:T(8,128)(2,1)S(1)} %all_to_all.10.own_ref), channel_id=1, source_target_pairs={{0,8},{8,0},{1,9},{9,1},{2,10},{10,2},{3,11},{11,3},{4,12},{12,4},... | collective-permute-start | bytes 884744 | tf_op jit(solution)/shard_map/ppermute | solution.py:491
  40.0 1.0 %copy-start.1 = (bf16[512,256]{1,0:T(8,128)(2,1)S(1)}, bf16[512,256]{1,0:T(8,128)(2,1)}, u32[]{:S(2)}) copy-start(bf16[512,256]{1,0:T(8,128)(2,1)} %constant.20.back_ref) | copy-start | bytes 786436
  40.0 1.0 %copy-start.2 = (bf16[256,512]{1,0:T(8,128)(2,1)S(1)}, bf16[256,512]{1,0:T(8,128)(2,1)}, u32[]{:S(2)}) copy-start(bf16[256,512]{1,0:T(8,128)(2,1)} %constant.19.step2_ref) | copy-start | bytes 786436

commit v6 on v5

--- a/solution.py
+++ b/solution.py
@@ -177,7 +177,9 @@
     return value
 
 
-def table_kernel(ids, base_ref, turn_ref, fold2_ref, phase_ref, fold_ref, step_ref, last_ref, phases_ref):
+def table_kernel(
+    ids, base_ref, turn_ref, fold2_ref, phase_ref, back_ref, fold_ref, step_ref, short_ref, phases_ref, last_s
+):
     _, dish, _ = ids()
     lane = lax.broadcasted_iota(jnp.int32, (GRAIN, 128), 1)
     turn = turn_ref[...]
@@ -196,10 +198,11 @@
         step_ref[k, :GRAIN, FREQS:] = -s
         step_ref[k, GRAIN:, :FREQS] = s
         step_ref[k, GRAIN:, FREQS:] = c
-    last_ref[:GRAIN, :FREQS] = cosine
-    last_ref[:GRAIN, FREQS:] = sine
-    last_ref[GRAIN:, :FREQS] = -sine
-    last_ref[GRAIN:, FREQS:] = cosine
+    last_s[:GRAIN, :FREQS] = cosine
+    last_s[:GRAIN, FREQS:] = sine
+    last_s[GRAIN:, :FREQS] = -sine
+    last_s[GRAIN:, FREQS:] = cosine
+    short_ref[...] = dot(back_ref[...], last_s[...]).astype(BF16)
     phases_ref[...] = jnp.zeros(phases_ref.shape, BF16)
     hi, lo = hi_lo(phase_ref[...])
     phases_ref[0:SPAN, :] = hi
@@ -274,7 +277,7 @@
 def spectrum_kernel(
     ids,
     own_ref, other_ref, z_ref, total_ref, place_ref, ends_ref, starts_ref, gbeam_ref,
-    fold_ref, step_ref, last_ref, phases_ref, step2_ref, back_ref, phase_ref,
+    fold_ref, step_ref, short_ref, phases_ref, step2_ref, phase_ref,
     out_ref,
     z_s, gdft_s, gstep_s, gbeam_s, gtime_s, gstart_s, acc_s, fold_s,
 ):
@@ -370,10 +373,7 @@
     since = acc_s[...]
     each = since - jnp.concatenate([since[1:], jnp.zeros((1, 6 * FREQS), F32)], 0)
     both, real, imag, both2, real2, imag2 = (each[:, k * FREQS : k * FREQS + FREQS] for k in range(6))
-    hi, lo = hi_lo(jnp.concatenate([both2 - imag2, both2 + real2], 1))
-    short = dot(hi, back_ref[...]) + dot(lo, back_ref[...])
-    hi, lo = hi_lo(short)
-    short = dot(hi, last_ref[...]) + dot(lo, last_ref[...])
+    short = dot(jnp.concatenate([both2 - imag2, both2 + real2], 1).astype(BF16), short_ref[...])
     out_ref[0] = (both - imag + short[:, :FREQS]) * SCALE
     out_ref[1] = (both + real + short[:, FREQS:]) * SCALE
 
@@ -406,17 +406,18 @@
         (
             pltpu.VMEM((2 * GRAIN, 4 * FREQS), BF16),
             pltpu.VMEM((2, 2 * GRAIN, 2 * FREQS), BF16),
-            pltpu.VMEM((2 * GRAIN, 2 * FREQS), BF16),
+            pltpu.VMEM((2 * FREQS, 2 * FREQS), BF16),
             pltpu.VMEM((128, 2 * FREQS), BF16),
         ),
-        [given[k] for k in ("base", "turn", "fold2", "phase")],
+        [given[k] for k in ("base", "turn", "fold2", "phase", "back")],
+        [pltpu.VMEM((2 * GRAIN, 2 * FREQS), BF16)],
         us=3.0,
     )
     return given, made
 
 
 def spectrum(own, other, ids, given, made):
-    fold, step, last, phases = made
+    fold, step, short, phases = made
     phase = given["phase"]
     half = call(
         functools.partial(half_kernel, ids),
@@ -444,7 +445,7 @@
     return call(
         functools.partial(spectrum_kernel, ids),
         jax.ShapeDtypeStruct((2, BINS, FREQS), F32),
-        (own, other, *half, fold, step, last, phases, given["step2"], given["back"], phase),
+        (own, other, *half, fold, step, short, phases, given["step2"], phase),
         scratch,
         mib=16,
         us=5.0,

time: 46.5 us -> 46.4 us (level)
  transfers between devices with their start and end apart: 2 -> 2, of which waited for: 2 -> 1; matrix products, arithmetic and copies ran while one was open for 0% -> 0% of each run, Pallas kernels for 4% -> 5%
where the time goes in v6:
time: 46.4 us; the launch traced here: 46.1 us
  blocking collectives  21.8 us (47%)
  starting transfers between devices  9.83 us (21%)
  Pallas kernels  9.06 us (20%)
  waiting for transfers between devices  5.2 us (11%)
    all_to_all x1, blocking collectives, steps(): own = lax.all_to_all(packed, ('z', 'xh'), 0, 0, tiled=True)  21.8 us
    pallas_call x5, Pallas kernels, call(): pl.pallas_call(kernel, out_shape=outs if one else tuple(outs), in_specs=[...  7.15 us
    all_to_all x1, starting transfers between devices, steps(): parts = lax.all_to_all(partial_beam, 'dish', 0, 0, tiled=True)  5.95 us
    all_to_all x1, waiting for transfers between devices, steps(): parts = lax.all_to_all(partial_beam, 'dish', 0, 0, tiled=True)  5.2 us
    ppermute x1, starting transfers between devices, steps(): other = lax.ppermute(own, 'core', [(0, 1), (1, 0)])  3.88 us
    pallas_call x1, Pallas kernels, front(): pl.pallas_call(front_kernel, out_shape=jax.ShapeDtypeStruct((DISH_WAYS, 2...  1.91 us
  transfers between devices with their start and end apart: 2, of which 1 were waited for; matrix products, arithmetic and copies ran while one was open for 0% of the time, Pallas kernels for 5%

profile of v6, /device:TPU:1, one launch (start us, length us, event | category | flops | bytes accessed | tf_op | source)
XLA Modules:
  0.0 46.1 jit_solution(6598841569568708729)
XLA Ops:
  0.0 1.9 %front.1 = f32[8,64,128]{2,1,0:T(8,128)} custom-call(bf16[2,8,4096]{2,1,0:T(8,128)(2,1)} %volts_hbm.1, bf16[2,8]{1,0:T(2,128)(2,1)} %weights_hbm.1), custom_call_target="tpu_custom_call" | custom-call | flops 1048576 | bytes 1048576 | tf_op jit(solution)/shard_map/front/pallas_call | solution.py:457
  1.9 0.0 copy-start
  1.9 5.9 %all-to-all-start = ((f32[8,64,128]{2,1,0:T(8,128)}), f32[8,64,128]{2,1,0:T(8,128)S(1)}, u32[]{:S(2)}, u32[]{:S(2)}) async-start(f32[8,64,128]{2,1,0:T(8,128)} %front.1), calls=%async_computation | async-start | bytes 524288 | tf_op jit(solution)/shard_map/all_to_all | solution.py:489
  7.9 0.0 copy-done
  7.9 1.0 %shard_map.91.visit_ref = bf16[16,8,128]{2,1,0:T(8,128)(2,1)S(1)} custom-call(s32[32,128]{1,0:T(8,128)S(1)} %bitcast.2), custom_call_target="tpu_custom_call" | custom-call | flops 1500000000 | bytes 1048576 | tf_op jit(solution)/shard_map/pallas_call | solution.py:388
  8.9 5.2 %all-to-all-done.parts_ref = f32[8,64,128]{2,1,0:T(8,128)S(1)} async-done(((f32[8,64,128]{2,1,0:T(8,128)}), f32[8,64,128]{2,1,0:T(8,128)S(1)}, u32[]{:S(2)}, u32[]{:S(2)}) %all-to-all-start) | async-done | bytes 262176 | tf_op jit(solution)/shard_map/all_to_all | solution.py:489
  14.1 0.0 copy-start.4
  14.1 0.0 copy-start.6
  14.1 0.0 copy-start.2
  14.1 0.0 copy-start.3
  14.1 0.0 copy-start.5
  14.1 21.8 %all_to_all.10.own_ref = bf16[16,72,128]{2,1,0:T(8,128)(2,1)S(1)} all-to-all(bf16[16,72,128]{2,1,0:T(8,128)(2,1)S(1)} %shard_map.92), channel_id=1, replica_groups=mesh['z'=8,'xh'=2,'core'=2,'dish'=8] {'z','xh'}, dimensions={0} | all-to-all | bytes 589824 | tf_op jit(solution)/shard_map/all_to_all | solution.py:491
  35.9 3.9 %collective-permute-start = (bf16[16,72,128]{2,1,0:T(8,128)(2,1)S(1)}, bf16[16,72,128]{2,1,0:T(8,128)(2,1)S(1)}, u32[]{:S(2)}, u32[]{:S(2)}) collective-permute-start(bf16[16,72,128]{2,1,0:T(8,128)(2,1)S(1)} %all_to_all.10.own_ref), channel_id=1, source_target_pairs={{0,8},{8,0},{1,9},{9,1},{2,10},{10,2},{3,11},{11,3},{4,12},{12,4},... | collective-permute-start | bytes 884744 | tf_op jit(solution)/shard_map/ppermute | solution.py:492
  39.8 0.0 copy-done.4
  39.8 0.0 copy-done.6
  39.8 0.0 copy-done.2
  39.8 0.0 copy-done.3
  39.8 0.0 copy-done.5
  39.8 0.4 shard_map.93
  40.3 0.0 copy-start.1
  40.3 0.8 %shard_map.94 = (bf16[512,512]{1,0:T(8,128)(2,1)S(1)}, f32[8,128]{1,0:T(8,128)S(1)}, f32[128,128]{1,0:T(8,128)S(1)}, f32[128,128]{1,0:T(8,128)S(1)}, f32[128,128]{1,0:T(8,128)S(1)}, /*index=5*/f32[128,256]{1,0:T(8,128)S(1)}) custom-call(bf16[16,72,128]{2,1,0:T(8,128)(2,1)S(1)} %all_to_all.10.own_ref, bf16[2,256,512]{2,1,0:T(8,128)(2,1)S(1)} %get-tuple-element.15.step_ref, ...), custom_call_target="tpu_custom_call" | custom-call | flops 500000000 | bytes 1048576 | tf_op jit(solution)/shard_map/pallas_call | solution.py:388
  41.1 0.0 collective-permute-done.other_ref
  41.1 0.1 copy-done.1
  41.2 4.9 %shard_map.95 = f32[2,32,256]{2,1,0:T(8,128)} custom-call(bf16[16,72,128]{2,1,0:T(8,128)(2,1)S(1)} %all_to_all.10.own_ref, bf16[16,72,128]{2,1,0:T(8,128)(2,1)S(1)} %collective-permute-done.other_ref, bf16[512,512]{1,0:T(8,128)(2,1)S(1)} %get-tuple-element.16.z_ref, f32[8,128]{1,0:T(8,128)S(1)} %get-tuple-element.17.total_ref, ...), custom_call_target="tpu_custom_call" | custom-call | flops 2500000000 | bytes 1048576 | tf_op jit(solution)/shard_map/pallas_call | solution.py:388
  (1 shorter events, 0.0 us)
Async XLA Ops:
  1.9 6.0 %copy-start = (s32[4096]{0:T(1024)S(1)}, s32[4096]{0:T(1024)}, u32[]{:S(2)}) copy-start(s32[4096]{0:T(1024)} %param.11) | copy-start | bytes 49156
  1.9 12.1 %all-to-all-start = ((f32[8,64,128]{2,1,0:T(8,128)}), f32[8,64,128]{2,1,0:T(8,128)S(1)}, u32[]{:S(2)}, u32[]{:S(2)}) async-start(f32[8,64,128]{2,1,0:T(8,128)} %front.1), calls=%async_computation | async-start | bytes 524288 | tf_op jit(solution)/shard_map/all_to_all | solution.py:489
  14.1 25.8 %copy-start.4 = (f32[128,512]{1,0:T(8,128)S(1)}, f32[128,512]{1,0:T(8,128)}, u32[]{:S(2)}) copy-start(f32[128,512]{1,0:T(8,128)} %constant.12.clone.base_ref) | copy-start | bytes 786436
  14.1 25.8 %copy-start.6 = (f32[16,512]{1,0:T(8,128)S(1)}, f32[16,512]{1,0:T(8,128)}, u32[]{:S(2)}) copy-start(f32[16,512]{1,0:T(8,128)} %constant.17.clone.phase_ref) | copy-start | bytes 98308
  14.1 25.7 %copy-start.2 = (bf16[512,256]{1,0:T(8,128)(2,1)S(1)}, bf16[512,256]{1,0:T(8,128)(2,1)}, u32[]{:S(2)}) copy-start(bf16[512,256]{1,0:T(8,128)(2,1)} %constant.19.back_ref) | copy-start | bytes 786436
  14.1 25.7 %copy-start.3 = (bf16[256,512]{1,0:T(8,128)(2,1)S(1)}, bf16[256,512]{1,0:T(8,128)(2,1)}, u32[]{:S(2)}) copy-start(bf16[256,512]{1,0:T(8,128)(2,1)} %constant.18.fold2_ref) | copy-start | bytes 786436
  14.1 25.7 %copy-start.5 = (f32[128,128]{1,0:T(8,128)S(1)}, f32[128,128]{1,0:T(8,128)}, u32[]{:S(2)}) copy-start(f32[128,128]{1,0:T(8,128)} %constant.13.clone.turn_ref) | copy-start | bytes 196612
  35.9 5.2 %collective-permute-start = (bf16[16,72,128]{2,1,0:T(8,128)(2,1)S(1)}, bf16[16,72,128]{2,1,0:T(8,128)(2,1)S(1)}, u32[]{:S(2)}, u32[]{:S(2)}) collective-permute-start(bf16[16,72,128]{2,1,0:T(8,128)(2,1)S(1)} %all_to_all.10.own_ref), channel_id=1, source_target_pairs={{0,8},{8,0},{1,9},{9,1},{2,10},{10,2},{3,11},{11,3},{4,12},{12,4},... | collective-permute-start | bytes 884744 | tf_op jit(solution)/shard_map/ppermute | solution.py:492
  40.3 1.0 %copy-start.1 = (bf16[256,512]{1,0:T(8,128)(2,1)S(1)}, bf16[256,512]{1,0:T(8,128)(2,1)}, u32[]{:S(2)}) copy-start(bf16[256,512]{1,0:T(8,128)(2,1)} %constant.20.step2_ref) | copy-start | bytes 786436

commit v7 on v6

--- a/solution.py
+++ b/solution.py
@@ -69,15 +69,21 @@
     }
 
 
-def front_kernel(volts_hbm, weights_hbm, beam_hbm, volts_s, weights_s, beam_s, sems):
+def front_kernel(
+    volts_hbm, weights_hbm, bins_hbm, beam_ref, visit_ref, volts_s, weights_s, bins_s, time_s, row_s, sems
+):
     copies = [
         pltpu.make_async_copy(source, target, sems.at[k])
-        for k, (source, target) in enumerate(((weights_hbm, weights_s), (volts_hbm, volts_s)))
+        for k, (source, target) in enumerate(
+            ((bins_hbm, bins_s), (weights_hbm, weights_s), (volts_hbm, volts_s))
+        )
     ]
     for copy in copies:
         copy.start()
-    for copy in copies:
-        copy.wait()
+    copies[0].wait()
+    make_visits(bins_s, visit_ref, time_s, row_s)
+    copies[1].wait()
+    copies[2].wait()
     weights = weights_s[...]
     first = dot(weights, volts_s[0])
     second = dot(weights, volts_s[1])
@@ -85,15 +91,11 @@
     imag = first[1:2] + second[0:1]
     for row in range(PER_BLOCK):
         part = slice(row * GRAIN, (row + 1) * GRAIN)
-        beam_s[row : row + 1, :] = real[:, part]
-        beam_s[PER_BLOCK + row : PER_BLOCK + row + 1, :] = imag[:, part]
-    copies = [
-        pltpu.make_async_copy(beam_s, beam_hbm.at[way], sems.at[2 + way]) for way in range(DISH_WAYS)
-    ]
-    for copy in copies:
-        copy.start()
-    for copy in copies:
-        copy.wait()
+        beam_ref[0, row : row + 1, :] = real[:, part]
+        beam_ref[0, PER_BLOCK + row : PER_BLOCK + row + 1, :] = imag[:, part]
+    rows = beam_ref[0]
+    for way in range(1, DISH_WAYS):
+        beam_ref[way] = rows
 
 
 def pack_kernel(parts_ref, visit_ref, out_ref):
@@ -118,7 +120,7 @@
     return jnp.where(row < column if strict else row <= column, 1.0, 0.0).astype(BF16)
 
 
-def visit_kernel(bins_ref, out_ref, time_s, row_s):
+def make_visits(bins_ref, out_ref, time_s, row_s):
     bins = bins_ref[...]
     shape = (PER_BLOCK, GRAIN)
     row = lax.broadcasted_iota(jnp.int32, shape, 0)
@@ -452,23 +454,29 @@
     )
 
 
-def front(voltages, beam_weights):
+def front(voltages, beam_weights, bins):
     far = pl.BlockSpec(memory_space=pltpu.HBM)
+    close = pl.BlockSpec(memory_space=pltpu.VMEM)
     return pl.pallas_call(
         front_kernel,
-        out_shape=jax.ShapeDtypeStruct((DISH_WAYS, 2 * PER_BLOCK, GRAIN), F32),
-        in_specs=[far] * 2,
-        out_specs=far,
+        out_shape=(
+            pltpu.VMEM((DISH_WAYS, 2 * PER_BLOCK, GRAIN), F32),
+            pltpu.VMEM((CHIPS, VISITS, GRAIN), BF16),
+        ),
+        in_specs=[far] * 3,
+        out_specs=(close, close),
         scratch_shapes=[
             pltpu.VMEM(voltages.shape, BF16),
             pltpu.VMEM(beam_weights.shape, BF16),
-            pltpu.VMEM((2 * PER_BLOCK, GRAIN), F32),
-            pltpu.SemaphoreType.DMA((2 + DISH_WAYS,)),
+            pltpu.VMEM(bins.shape, jnp.int32),
+            pltpu.VMEM((72, GRAIN), F32),
+            pltpu.VMEM((72, GRAIN), F32),
+            pltpu.SemaphoreType.DMA((3,)),
         ],
         compiler_params=pltpu.CompilerParams(vmem_limit_bytes=8 << 20),
         cost_estimate=pl.CostEstimate(flops=1 << 20, bytes_accessed=1 << 20, transcendentals=0),
         name="front",
-    )(*(pltpu.with_memory_space_constraint(v, pltpu.HBM) for v in (voltages, beam_weights)))
+    )(*(pltpu.with_memory_space_constraint(v, pltpu.HBM) for v in (voltages, beam_weights, bins)))
 
 
 def steps(voltages, beam_weights, phase_bins):
@@ -478,14 +486,7 @@
         return owner, lax.axis_index("dish"), core
 
     given, made = make_tables(ids)
-    visits = call(
-        visit_kernel,
-        pltpu.VMEM((CHIPS, VISITS, GRAIN), BF16),
-        (phase_bins.reshape(PER_BLOCK, GRAIN),),
-        [pltpu.VMEM((72, GRAIN), F32)] * 2,
-        us=3.0,
-    )
-    partial_beam = front(voltages, beam_weights)
+    partial_beam, visits = front(voltages, beam_weights, phase_bins.reshape(PER_BLOCK, GRAIN))
     parts = lax.all_to_all(partial_beam, "dish", 0, 0, tiled=True)
     packed = call(pack_kernel, pltpu.VMEM((CHIPS, ROWS, GRAIN), BF16), (parts, visits), us=0.3)
     own = lax.all_to_all(packed, ("z", "xh"), 0, 0, tiled=True)

time: 46.4 us -> 46.3 us (level)
  blocking collectives: 21.8 us -> 33.7 us
  starting transfers between devices: 9.83 us -> 3.88 us
  waiting for transfers between devices: 5.2 us -> 0.01 us
  Pallas kernels: 9.06 us -> 8.23 us
    all_to_all x0 -> x1, blocking collectives: none -> 11.9 us  [steps(): parts = lax.all_to_all(partial_beam, 'dish', 0, 0, tiled=True)]
    all_to_all x1 -> x0, starting transfers between devices: 5.95 us -> none  [steps(): parts = lax.all_to_all(partial_beam, 'dish', 0, 0, tiled=True)]
    all_to_all x1 -> x0, waiting for transfers between devices: 5.2 us -> none  [steps(): parts = lax.all_to_all(partial_beam, 'dish', 0, 0, tiled=True)]
    pallas_call x5 -> x4, Pallas kernels: 7.15 us -> 6.18 us  [call(): pl.pallas_call(kernel, out_shape=outs if one else tuple(outs), in_specs=[...]
  transfers between devices with their start and end apart: 2 -> 1, of which waited for: 1 -> 0; matrix products, arithmetic and copies ran while one was open for 0% -> 0% of each run, Pallas kernels for 5% -> 3%
where the time goes in v7:
time: 46.3 us; the launch traced here: 46.1 us
  blocking collectives  33.7 us (73%)
  Pallas kernels  8.23 us (18%)
  starting transfers between devices  3.88 us (8%)
    all_to_all x1, blocking collectives, steps(): own = lax.all_to_all(packed, ('z', 'xh'), 0, 0, tiled=True)  21.8 us
    all_to_all x1, blocking collectives, steps(): parts = lax.all_to_all(partial_beam, 'dish', 0, 0, tiled=True)  11.9 us
    pallas_call x4, Pallas kernels, call(): pl.pallas_call(kernel, out_shape=outs if one else tuple(outs), in_specs=[...  6.18 us
    ppermute x1, starting transfers between devices, steps(): other = lax.ppermute(own, 'core', [(0, 1), (1, 0)])  3.88 us
    pallas_call x1, Pallas kernels, front(): pl.pallas_call(front_kernel, out_shape=(pltpu.VMEM((DISH_WAYS, 2 * PER_BL...  2.05 us
  transfers between devices with their start and end apart: 1, of which 0 were waited for; matrix products, arithmetic and copies ran while one was open for 0% of the time, Pallas kernels for 3%

profile of v7, /device:TPU:1, one launch (start us, length us, event | category | flops | bytes accessed | tf_op | source)
XLA Modules:
  0.0 46.1 jit_solution(2618671152548919343)
XLA Ops:
  0.0 2.0 %front.1 = (f32[8,64,128]{2,1,0:T(8,128)S(1)}, bf16[16,8,128]{2,1,0:T(8,128)(2,1)S(1)}) custom-call(bf16[2,8,4096]{2,1,0:T(8,128)(2,1)} %volts_hbm.1, bf16[2,8]{1,0:T(2,128)(2,1)} %weights_hbm.1, s32[32,128]{1,0:T(8,128)} %bitcast.2), custom_call_target="tpu_custom_call" | custom-call | flops 1048576 | bytes 1048576 | tf_op jit(solution)/shard_map/front/pallas_call | solution.py:460
  2.1 11.9 %all_to_all.10.parts_ref = f32[8,64,128]{2,1,0:T(8,128)S(1)} all-to-all(f32[8,64,128]{2,1,0:T(8,128)S(1)} %get-tuple-element.17), channel_id=1, replica_groups=mesh['z'=8,'xh'=2,'core'=2,'dish'=8] {'dish'}, dimensions={0} | all-to-all | bytes 524288 | tf_op jit(solution)/shard_map/all_to_all | solution.py:490
  14.0 0.0 copy-start.3
  14.0 0.0 copy-start.5
  14.0 0.0 copy-start.1
  14.0 0.0 copy-start.2
  14.0 0.0 copy-start.4
  14.0 21.8 %all_to_all.11.own_ref = bf16[16,72,128]{2,1,0:T(8,128)(2,1)S(1)} all-to-all(bf16[16,72,128]{2,1,0:T(8,128)(2,1)S(1)} %shard_map.91), channel_id=1, replica_groups=mesh['z'=8,'xh'=2,'core'=2,'dish'=8] {'z','xh'}, dimensions={0} | all-to-all | bytes 589824 | tf_op jit(solution)/shard_map/all_to_all | solution.py:492
  35.8 3.9 %collective-permute-start = (bf16[16,72,128]{2,1,0:T(8,128)(2,1)S(1)}, bf16[16,72,128]{2,1,0:T(8,128)(2,1)S(1)}, u32[]{:S(2)}, u32[]{:S(2)}) collective-permute-start(bf16[16,72,128]{2,1,0:T(8,128)(2,1)S(1)} %all_to_all.11.own_ref), channel_id=1, source_target_pairs={{0,8},{8,0},{1,9},{9,1},{2,10},{10,2},{3,11},{11,3},{4,12},{12,4},... | collective-permute-start | bytes 884744 | tf_op jit(solution)/shard_map/ppermute | solution.py:493
  39.7 0.0 copy-done.3
  39.7 0.0 copy-done.5
  39.7 0.0 copy-done.1
  39.7 0.0 copy-done.2
  39.7 0.0 copy-done.4
  39.8 0.4 shard_map.92
  40.2 0.0 copy-start
  40.2 0.8 %shard_map.93 = (bf16[512,512]{1,0:T(8,128)(2,1)S(1)}, f32[8,128]{1,0:T(8,128)S(1)}, f32[128,128]{1,0:T(8,128)S(1)}, f32[128,128]{1,0:T(8,128)S(1)}, f32[128,128]{1,0:T(8,128)S(1)}, /*index=5*/f32[128,256]{1,0:T(8,128)S(1)}) custom-call(bf16[16,72,128]{2,1,0:T(8,128)(2,1)S(1)} %all_to_all.11.own_ref, bf16[2,256,512]{2,1,0:T(8,128)(2,1)S(1)} %get-tuple-element.19.step_ref, ...), custom_call_target="tpu_custom_call" | custom-call | flops 500000000 | bytes 1048576 | tf_op jit(solution)/shard_map/pallas_call | solution.py:390
  41.0 0.0 collective-permute-done.other_ref
  41.0 0.1 copy-done
  41.1 4.9 %shard_map.94 = f32[2,32,256]{2,1,0:T(8,128)} custom-call(bf16[16,72,128]{2,1,0:T(8,128)(2,1)S(1)} %all_to_all.11.own_ref, bf16[16,72,128]{2,1,0:T(8,128)(2,1)S(1)} %collective-permute-done.other_ref, bf16[512,512]{1,0:T(8,128)(2,1)S(1)} %get-tuple-element.20.z_ref, f32[8,128]{1,0:T(8,128)S(1)} %get-tuple-element.21.total_ref, ...), custom_call_target="tpu_custom_call" | custom-call | flops 2500000000 | bytes 1048576 | tf_op jit(solution)/shard_map/pallas_call | solution.py:390
  (1 shorter events, 0.0 us)
Async XLA Ops:
  14.0 25.8 %copy-start.3 = (f32[128,512]{1,0:T(8,128)S(1)}, f32[128,512]{1,0:T(8,128)}, u32[]{:S(2)}) copy-start(f32[128,512]{1,0:T(8,128)} %constant.12.clone.base_ref) | copy-start | bytes 786436
  14.0 25.8 %copy-start.5 = (f32[16,512]{1,0:T(8,128)S(1)}, f32[16,512]{1,0:T(8,128)}, u32[]{:S(2)}) copy-start(f32[16,512]{1,0:T(8,128)} %constant.17.clone.phase_ref) | copy-start | bytes 98308
  14.0 25.7 %copy-start.1 = (bf16[512,256]{1,0:T(8,128)(2,1)S(1)}, bf16[512,256]{1,0:T(8,128)(2,1)}, u32[]{:S(2)}) copy-start(bf16[512,256]{1,0:T(8,128)(2,1)} %constant.19.back_ref) | copy-start | bytes 786436
  14.0 25.7 %copy-start.2 = (bf16[256,512]{1,0:T(8,128)(2,1)S(1)}, bf16[256,512]{1,0:T(8,128)(2,1)}, u32[]{:S(2)}) copy-start(bf16[256,512]{1,0:T(8,128)(2,1)} %constant.18.fold2_ref) | copy-start | bytes 786436
  14.0 25.7 %copy-start.4 = (f32[128,128]{1,0:T(8,128)S(1)}, f32[128,128]{1,0:T(8,128)}, u32[]{:S(2)}) copy-start(f32[128,128]{1,0:T(8,128)} %constant.13.clone.turn_ref) | copy-start | bytes 196612
  35.8 5.2 %collective-permute-start = (bf16[16,72,128]{2,1,0:T(8,128)(2,1)S(1)}, bf16[16,72,128]{2,1,0:T(8,128)(2,1)S(1)}, u32[]{:S(2)}, u32[]{:S(2)}) collective-permute-start(bf16[16,72,128]{2,1,0:T(8,128)(2,1)S(1)} %all_to_all.11.own_ref), channel_id=1, source_target_pairs={{0,8},{8,0},{1,9},{9,1},{2,10},{10,2},{3,11},{11,3},{4,12},{12,4},... | collective-permute-start | bytes 884744 | tf_op jit(solution)/shard_map/ppermute | solution.py:493
  40.2 1.0 %copy-start = (bf16[256,512]{1,0:T(8,128)(2,1)S(1)}, bf16[256,512]{1,0:T(8,128)(2,1)}, u32[]{:S(2)}) copy-start(bf16[256,512]{1,0:T(8,128)(2,1)} %constant.20.step2_ref) | copy-start | bytes 786436

commit v8 on v7

--- a/solution.py
+++ b/solution.py
@@ -80,10 +80,8 @@
     ]
     for copy in copies:
         copy.start()
-    copies[0].wait()
-    make_visits(bins_s, visit_ref, time_s, row_s)
-    copies[1].wait()
-    copies[2].wait()
+    for copy in copies:
+        copy.wait()
     weights = weights_s[...]
     first = dot(weights, volts_s[0])
     second = dot(weights, volts_s[1])
@@ -93,6 +91,7 @@
         part = slice(row * GRAIN, (row + 1) * GRAIN)
         beam_ref[0, row : row + 1, :] = real[:, part]
         beam_ref[0, PER_BLOCK + row : PER_BLOCK + row + 1, :] = imag[:, part]
+    make_visits(bins_s, visit_ref, time_s, row_s)
     rows = beam_ref[0]
     for way in range(1, DISH_WAYS):
         beam_ref[way] = rows
@@ -134,21 +133,28 @@
     ends = jnp.broadcast_to(in_row[:, GRAIN - 1 :], shape).astype(BF16)
     above = dot(triangle(PER_BLOCK, True), ends, (((0,), (0,)), ((), ())))
     step = bins + PH * (in_row + above).astype(jnp.int32)
-    high = jnp.where(enters, step >> 7, -1)
-    low = step & 127
+    high = jnp.where(enters, step >> 7, -1).astype(F32)
+    low = (step & 127).astype(F32)
     times = coded_times(shape)
     high_iota = lax.broadcasted_iota(jnp.int32, (48, GRAIN), 0)
-    low_iota = lax.broadcasted_iota(jnp.int32, (GRAIN, GRAIN), 0)
+    high_rows = high_iota.astype(F32).astype(BF16)
+    low_rows = lax.broadcasted_iota(jnp.int32, (GRAIN, GRAIN), 0).astype(F32).astype(BF16)
+    zero, one = jnp.zeros((), BF16), jnp.ones((), BF16)
+
+    def spread(value, k, count):
+        tile = jnp.broadcast_to(value[k : k + 1, :], (16, GRAIN)).astype(BF16)
+        return jnp.concatenate([tile] * (count // 16), 0)
+
     found = jnp.zeros((96, GRAIN), F32)
     for pair in range(PER_BLOCK // 2):
         left, right = [], []
         for k in (2 * pair, 2 * pair + 1):
-            here = high[k : k + 1, :] == high_iota
-            coded = jnp.where(here, times[k : k + 1, :], 0.0)
-            left.append(jnp.concatenate([coded, jnp.where(here, float(k), 0.0)], 0))
-            right.append(jnp.where(low[k : k + 1, :] == low_iota, 1.0, 0.0))
-        left = jnp.concatenate(left, 1).astype(BF16)
-        right = jnp.concatenate(right, 1).astype(BF16)
+            here = spread(high, k, 48) == high_rows
+            coded = jnp.where(here, spread(times, k, 48), zero)
+            left.append(jnp.concatenate([coded, jnp.where(here, jnp.full((), k, BF16), zero)], 0))
+            right.append(jnp.where(spread(low, k, GRAIN) == low_rows, one, zero))
+        left = jnp.concatenate(left, 1)
+        right = jnp.concatenate(right, 1)
         found = found + dot(left, right, (((1,), (1,)), ((), ())))
     place = high_iota * GRAIN + lax.broadcasted_iota(jnp.int32, (48, GRAIN), 1)
     past, ahead = place <= step[0:1, 0:1], place > step[PER_BLOCK - 1 :, GRAIN - 1 :]
@@ -281,7 +287,7 @@
     own_ref, other_ref, z_ref, total_ref, place_ref, ends_ref, starts_ref, gbeam_ref,
     fold_ref, step_ref, short_ref, phases_ref, step2_ref, phase_ref,
     out_ref,
-    z_s, gdft_s, gstep_s, gbeam_s, gtime_s, gstart_s, acc_s, fold_s,
+    z_s, gdft_s, gstep_s, gbeam_s, gtime_s, gstart_s, acc_s,
 ):
     _, _, core = ids()
     before = total_ref[0:1, 0:1]
@@ -289,7 +295,6 @@
     count = jnp.max(other_plan[-1]).astype(jnp.int32)
     transform(other_ref, step_ref, phase_ref, z_s)
     acc_s[...] = jnp.zeros(acc_s.shape, F32)
-    fold_s[...] = fold_ref[...]
     own_grains = jnp.broadcast_to(grain_row(core), (SLOTS, HALF))
     other_grains = jnp.broadcast_to(grain_row(1 - core), (SLOTS, HALF))
     lane_iota = lax.broadcasted_iota(jnp.int32, (SLOTS, 128), 1)
@@ -345,7 +350,7 @@
                 left.append(jnp.concatenate([real, imag], 1))
             left = jnp.concatenate(left, 0).astype(BF16)
             for part, factor in ((0, dft8), (1, step8)):
-                folded = dot(left, fold_s[:, part * 2 * FREQS : part * 2 * FREQS + 2 * FREQS])
+                folded = dot(left, fold_ref[:, part * 2 * FREQS : part * 2 * FREQS + 2 * FREQS])
                 sums = [acc_s[:, k * FREQS : k * FREQS + FREQS] for k in range(3 * part, 3 * part + 3)]
                 for k in range(GROUP):
                     rows = slice(k * BINS, k * BINS + BINS)
@@ -442,7 +447,6 @@
         pltpu.VMEM((SLOTS, GRAIN), F32),
         pltpu.VMEM((SLOTS // GROUP, BINS, 128), F32),
         pltpu.VMEM((BINS, 6 * FREQS), F32),
-        pltpu.VMEM((2 * GRAIN, 4 * FREQS), BF16),
     ]
     return call(
         functools.partial(spectrum_kernel, ids),

time: 46.3 us -> 46.2 us (level)
  no operation moved by 1% of the time
where the time goes in v8:
time: 46.2 us; the launch traced here: 46 us
  blocking collectives  33.7 us (73%)
  Pallas kernels  8.15 us (18%)
  starting transfers between devices  3.88 us (8%)
    all_to_all x1, blocking collectives, steps(): own = lax.all_to_all(packed, ('z', 'xh'), 0, 0, tiled=True)  21.8 us
    all_to_all x1, blocking collectives, steps(): parts = lax.all_to_all(partial_beam, 'dish', 0, 0, tiled=True)  11.9 us
    pallas_call x4, Pallas kernels, call(): pl.pallas_call(kernel, out_shape=outs if one else tuple(outs), in_specs=[...  6.17 us
    ppermute x1, starting transfers between devices, steps(): other = lax.ppermute(own, 'core', [(0, 1), (1, 0)])  3.88 us
    pallas_call x1, Pallas kernels, front(): pl.pallas_call(front_kernel, out_shape=(pltpu.VMEM((DISH_WAYS, 2 * PER_BL...  1.97 us
  transfers between devices with their start and end apart: 1, of which 0 were waited for; matrix products, arithmetic and copies ran while one was open for 0% of the time, Pallas kernels for 3%

profile of v8, /device:TPU:1, one launch (start us, length us, event | category | flops | bytes accessed | tf_op | source)
XLA Modules:
  0.0 46.0 jit_solution(7063746720095125673)
XLA Ops:
  0.0 2.0 %front.1 = (f32[8,64,128]{2,1,0:T(8,128)S(1)}, bf16[16,8,128]{2,1,0:T(8,128)(2,1)S(1)}) custom-call(bf16[2,8,4096]{2,1,0:T(8,128)(2,1)} %volts_hbm.1, bf16[2,8]{1,0:T(2,128)(2,1)} %weights_hbm.1, s32[32,128]{1,0:T(8,128)} %bitcast.2), custom_call_target="tpu_custom_call" | custom-call | flops 1048576 | bytes 1048576 | tf_op jit(solution)/shard_map/front/pallas_call | solution.py:464
  2.0 11.9 %all_to_all.10.parts_ref = f32[8,64,128]{2,1,0:T(8,128)S(1)} all-to-all(f32[8,64,128]{2,1,0:T(8,128)S(1)} %get-tuple-element.17), channel_id=1, replica_groups=mesh['z'=8,'xh'=2,'core'=2,'dish'=8] {'dish'}, dimensions={0} | all-to-all | bytes 524288 | tf_op jit(solution)/shard_map/all_to_all | solution.py:494
  13.9 0.0 copy-start.3
  13.9 0.0 copy-start.5
  13.9 0.0 copy-start.1
  14.0 0.0 copy-start.2
  14.0 0.0 copy-start.4
  14.0 21.8 %all_to_all.11.own_ref = bf16[16,72,128]{2,1,0:T(8,128)(2,1)S(1)} all-to-all(bf16[16,72,128]{2,1,0:T(8,128)(2,1)S(1)} %shard_map.91), channel_id=1, replica_groups=mesh['z'=8,'xh'=2,'core'=2,'dish'=8] {'z','xh'}, dimensions={0} | all-to-all | bytes 589824 | tf_op jit(solution)/shard_map/all_to_all | solution.py:496
  35.8 3.9 %collective-permute-start = (bf16[16,72,128]{2,1,0:T(8,128)(2,1)S(1)}, bf16[16,72,128]{2,1,0:T(8,128)(2,1)S(1)}, u32[]{:S(2)}, u32[]{:S(2)}) collective-permute-start(bf16[16,72,128]{2,1,0:T(8,128)(2,1)S(1)} %all_to_all.11.own_ref), channel_id=1, source_target_pairs={{0,8},{8,0},{1,9},{9,1},{2,10},{10,2},{3,11},{11,3},{4,12},{12,4},... | collective-permute-start | bytes 884744 | tf_op jit(solution)/shard_map/ppermute | solution.py:497
  39.7 0.0 copy-done.3
  39.7 0.0 copy-done.5
  39.7 0.0 copy-done.1
  39.7 0.0 copy-done.2
  39.7 0.0 copy-done.4
  39.7 0.4 shard_map.92
  40.1 0.0 copy-start
  40.1 0.8 %shard_map.93 = (bf16[512,512]{1,0:T(8,128)(2,1)S(1)}, f32[8,128]{1,0:T(8,128)S(1)}, f32[128,128]{1,0:T(8,128)S(1)}, f32[128,128]{1,0:T(8,128)S(1)}, f32[128,128]{1,0:T(8,128)S(1)}, /*index=5*/f32[128,256]{1,0:T(8,128)S(1)}) custom-call(bf16[16,72,128]{2,1,0:T(8,128)(2,1)S(1)} %all_to_all.11.own_ref, bf16[2,256,512]{2,1,0:T(8,128)(2,1)S(1)} %get-tuple-element.19.step_ref, ...), custom_call_target="tpu_custom_call" | custom-call | flops 500000000 | bytes 1048576 | tf_op jit(solution)/shard_map/pallas_call | solution.py:395
  40.9 0.0 collective-permute-done.other_ref
  41.0 0.1 copy-done
  41.1 4.9 %shard_map.94 = f32[2,32,256]{2,1,0:T(8,128)} custom-call(bf16[16,72,128]{2,1,0:T(8,128)(2,1)S(1)} %all_to_all.11.own_ref, bf16[16,72,128]{2,1,0:T(8,128)(2,1)S(1)} %collective-permute-done.other_ref, bf16[512,512]{1,0:T(8,128)(2,1)S(1)} %get-tuple-element.20.z_ref, f32[8,128]{1,0:T(8,128)S(1)} %get-tuple-element.21.total_ref, ...), custom_call_target="tpu_custom_call" | custom-call | flops 2500000000 | bytes 1048576 | tf_op jit(solution)/shard_map/pallas_call | solution.py:395
  (1 shorter events, 0.0 us)
Async XLA Ops:
  13.9 25.8 %copy-start.3 = (f32[128,512]{1,0:T(8,128)S(1)}, f32[128,512]{1,0:T(8,128)}, u32[]{:S(2)}) copy-start(f32[128,512]{1,0:T(8,128)} %constant.12.clone.base_ref) | copy-start | bytes 786436
  13.9 25.8 %copy-start.5 = (f32[16,512]{1,0:T(8,128)S(1)}, f32[16,512]{1,0:T(8,128)}, u32[]{:S(2)}) copy-start(f32[16,512]{1,0:T(8,128)} %constant.17.clone.phase_ref) | copy-start | bytes 98308
  13.9 25.7 %copy-start.1 = (bf16[512,256]{1,0:T(8,128)(2,1)S(1)}, bf16[512,256]{1,0:T(8,128)(2,1)}, u32[]{:S(2)}) copy-start(bf16[512,256]{1,0:T(8,128)(2,1)} %constant.19.back_ref) | copy-start | bytes 786436
  14.0 25.7 %copy-start.2 = (bf16[256,512]{1,0:T(8,128)(2,1)S(1)}, bf16[256,512]{1,0:T(8,128)(2,1)}, u32[]{:S(2)}) copy-start(bf16[256,512]{1,0:T(8,128)(2,1)} %constant.18.fold2_ref) | copy-start | bytes 786436
  14.0 25.7 %copy-start.4 = (f32[128,128]{1,0:T(8,128)S(1)}, f32[128,128]{1,0:T(8,128)}, u32[]{:S(2)}) copy-start(f32[128,128]{1,0:T(8,128)} %constant.13.clone.turn_ref) | copy-start | bytes 196612
  35.8 5.2 %collective-permute-start = (bf16[16,72,128]{2,1,0:T(8,128)(2,1)S(1)}, bf16[16,72,128]{2,1,0:T(8,128)(2,1)S(1)}, u32[]{:S(2)}, u32[]{:S(2)}) collective-permute-start(bf16[16,72,128]{2,1,0:T(8,128)(2,1)S(1)} %all_to_all.11.own_ref), channel_id=1, source_target_pairs={{0,8},{8,0},{1,9},{9,1},{2,10},{10,2},{3,11},{11,3},{4,12},{12,4},... | collective-permute-start | bytes 884744 | tf_op jit(solution)/shard_map/ppermute | solution.py:497
  40.1 1.0 %copy-start = (bf16[256,512]{1,0:T(8,128)(2,1)S(1)}, bf16[256,512]{1,0:T(8,128)(2,1)}, u32[]{:S(2)}) copy-start(bf16[256,512]{1,0:T(8,128)(2,1)} %constant.20.step2_ref) | copy-start | bytes 786436

commit v9 on v8

--- a/solution.py
+++ b/solution.py
@@ -20,10 +20,11 @@
 LOCAL = SAMPLES // TM_WAYS
 GRAIN = 128
 PER_BLOCK = LOCAL // GRAIN
+SIDE = GRAIN // 2
 SPAN = LAGS // GRAIN
 BINS = PH // TM_WAYS
 FREQS = LAGS // DISH_WAYS
-SLOTS = 128
+SLOTS = 96
 GROUP = 16
 VISITS = 8
 ROWS = 2 * PER_BLOCK + VISITS
@@ -55,10 +56,14 @@
     cos2, sin2 = np.cos(fine), np.sin(fine)
     fold2 = np.block([[cos2, sin2], [sin2, -cos2]]).astype(np.float32)
     step2 = np.block([[cos2, -sin2], [sin2, cos2]]).astype(np.float32)
+    sides = np.concatenate([np.arange(k, k + SIDE) for k in (0, GRAIN, SIDE, GRAIN + SIDE)])
+    fold2, step2 = fold2[sides], step2[sides]
     keep = (grain >= 1)[None, :] / (2.0 * GRAIN)
     back = np.block([[cos2.T * keep, -sin2.T * keep], [sin2.T * keep, cos2.T * keep]])
     sixteenth = 2 * np.pi * np.outer(np.arange(SPAN), freq) / SPAN
     phase = np.concatenate([np.cos(sixteenth), np.sin(sixteenth)], 1).astype(np.float32)
+    fine = np.pi * np.outer(np.arange(2 * SPAN), freq) / SPAN
+    start = np.concatenate([np.cos(fine), np.sin(fine)], 1).astype(np.float32)
     return {
         "base": jnp.asarray(base),
         "turn": jnp.asarray(turn),
@@ -66,6 +71,7 @@
         "step2": jnp.asarray(step2).astype(BF16),
         "back": jnp.asarray(back.astype(np.float32)).astype(BF16),
         "phase": jnp.asarray(phase),
+        "start": jnp.asarray(start),
     }
 
 
@@ -101,7 +107,11 @@
     total = parts_ref[0]
     for way in range(1, DISH_WAYS):
         total = total + parts_ref[way]
-    rows = total.astype(BF16)
+    real, imag = total[:PER_BLOCK], total[PER_BLOCK:]
+    early = lax.broadcasted_iota(jnp.int32, (PER_BLOCK, GRAIN), 1) < SIDE
+    early_side = jnp.where(early, real, pltpu.roll(imag, SIDE, 1))
+    late_side = jnp.where(early, pltpu.roll(real, SIDE, 1), imag)
+    rows = jnp.concatenate([early_side, late_side], 0).astype(BF16)
     for chip in range(CHIPS):
         out_ref[chip, : 2 * PER_BLOCK, :] = rows
         out_ref[chip, 2 * PER_BLOCK :, :] = visit_ref[chip]
@@ -140,6 +150,7 @@
     high_rows = high_iota.astype(F32).astype(BF16)
     low_rows = lax.broadcasted_iota(jnp.int32, (GRAIN, GRAIN), 0).astype(F32).astype(BF16)
     zero, one = jnp.zeros((), BF16), jnp.ones((), BF16)
+    late = jnp.where(lax.broadcasted_iota(jnp.int32, (48, GRAIN), 1) >= SIDE, 1.0, 0.0).astype(BF16)
 
     def spread(value, k, count):
         tile = jnp.broadcast_to(value[k : k + 1, :], (16, GRAIN)).astype(BF16)
@@ -151,7 +162,7 @@
         for k in (2 * pair, 2 * pair + 1):
             here = spread(high, k, 48) == high_rows
             coded = jnp.where(here, spread(times, k, 48), zero)
-            left.append(jnp.concatenate([coded, jnp.where(here, jnp.full((), k, BF16), zero)], 0))
+            left.append(jnp.concatenate([coded, jnp.where(here, late + jnp.full((), 2 * k, BF16), zero)], 0))
             right.append(jnp.where(spread(low, k, GRAIN) == low_rows, one, zero))
         left = jnp.concatenate(left, 1)
         right = jnp.concatenate(right, 1)
@@ -159,9 +170,9 @@
     place = high_iota * GRAIN + lax.broadcasted_iota(jnp.int32, (48, GRAIN), 1)
     past, ahead = place <= step[0:1, 0:1], place > step[PER_BLOCK - 1 :, GRAIN - 1 :]
     time_s[:48, :] = jnp.where(past, 2.0**-9, jnp.where(ahead, 2.0**23, found[:48]))
-    row_s[:48, :] = jnp.where(past, 0.0, jnp.where(ahead, 32.0, found[48:]))
+    row_s[:48, :] = jnp.where(past, 0.0, jnp.where(ahead, 64.0, found[48:]))
     time_s[48:, :] = jnp.full((24, GRAIN), 2.0**23, F32)
-    row_s[48:, :] = jnp.full((24, GRAIN), 32.0, F32)
+    row_s[48:, :] = jnp.full((24, GRAIN), 64.0, F32)
     lane = lax.broadcasted_iota(jnp.int32, (VISITS, GRAIN), 1)
     for eighth in range(8):
         now, then = pl.ds(eighth, VISITS, stride=8), pl.ds(eighth + 1, VISITS, stride=8)
@@ -180,13 +191,13 @@
 
 def two_to(exponent):
     value = jnp.full(jnp.shape(exponent), 2.0**-16, F32)
-    for bit in range(5):
+    for bit in range(6):
         value = value * jnp.where((exponent >> bit) & 1 == 1, float(2 ** (2**bit)), 1.0)
     return value
 
 
 def table_kernel(
-    ids, base_ref, turn_ref, fold2_ref, phase_ref, back_ref, fold_ref, step_ref, short_ref, phases_ref, last_s
+    ids, base_ref, turn_ref, fold2_ref, start_ref, back_ref, fold_ref, step_ref, short_ref, phases_ref, side_ref, last_s
 ):
     _, dish, _ = ids()
     lane = lax.broadcasted_iota(jnp.int32, (GRAIN, 128), 1)
@@ -194,27 +205,39 @@
     cos8 = jnp.sum(jnp.where(lane == dish, turn, 0.0), axis=1, keepdims=True)
     sin8 = jnp.sum(jnp.where(lane == dish + 8, turn, 0.0), axis=1, keepdims=True)
     cos0, sin0 = base_ref[:, :FREQS], base_ref[:, FREQS:]
-    cosine, cosine_lo = hi_lo(cos0 * cos8 - sin0 * sin8)
-    sine, sine_lo = hi_lo(sin0 * cos8 + cos0 * sin8)
-    fold_ref[:GRAIN, :FREQS] = cosine
-    fold_ref[:GRAIN, FREQS : 2 * FREQS] = sine
-    fold_ref[GRAIN:, :FREQS] = sine
-    fold_ref[GRAIN:, FREQS : 2 * FREQS] = -cosine
+    cos_f, sin_f = cos0 * cos8 - sin0 * sin8, sin0 * cos8 + cos0 * sin8
+    cosine, cosine_lo = hi_lo(cos_f)
+    sine, sine_lo = hi_lo(sin_f)
+    for side in range(2):
+        part = slice(side * SIDE, side * SIDE + SIDE)
+        reals = slice(side * GRAIN, side * GRAIN + SIDE)
+        imags = slice(side * GRAIN + SIDE, side * GRAIN + GRAIN)
+        fold_ref[reals, :FREQS] = cosine[part]
+        fold_ref[reals, FREQS : 2 * FREQS] = sine[part]
+        fold_ref[imags, :FREQS] = sine[part]
+        fold_ref[imags, FREQS : 2 * FREQS] = -cosine[part]
+        for k, (c, s) in enumerate(((cosine, sine), (cosine_lo, sine_lo))):
+            step_ref[k, reals, :FREQS] = c[part]
+            step_ref[k, reals, FREQS:] = -s[part]
+            step_ref[k, imags, :FREQS] = s[part]
+            step_ref[k, imags, FREQS:] = c[part]
     fold_ref[:, 2 * FREQS :] = fold2_ref[...]
-    for k, (c, s) in enumerate(((cosine, sine), (cosine_lo, sine_lo))):
-        step_ref[k, :GRAIN, :FREQS] = c
-        step_ref[k, :GRAIN, FREQS:] = -s
-        step_ref[k, GRAIN:, :FREQS] = s
-        step_ref[k, GRAIN:, FREQS:] = c
+    cos_side, sin_side = cos_f[SIDE : SIDE + 1], sin_f[SIDE : SIDE + 1]
+    side_real = cos_f[:SIDE] * cos_side + sin_f[:SIDE] * sin_side
+    side_imag = cos_f[:SIDE] * sin_side - sin_f[:SIDE] * cos_side
+    side_ref[:SIDE, :FREQS] = side_real.astype(BF16)
+    side_ref[:SIDE, FREQS:] = side_imag.astype(BF16)
+    side_ref[SIDE:, :FREQS] = -side_imag.astype(BF16)
+    side_ref[SIDE:, FREQS:] = side_real.astype(BF16)
     last_s[:GRAIN, :FREQS] = cosine
     last_s[:GRAIN, FREQS:] = sine
     last_s[GRAIN:, :FREQS] = -sine
     last_s[GRAIN:, FREQS:] = cosine
     short_ref[...] = dot(back_ref[...], last_s[...]).astype(BF16)
     phases_ref[...] = jnp.zeros(phases_ref.shape, BF16)
-    hi, lo = hi_lo(phase_ref[...])
-    phases_ref[0:SPAN, :] = hi
-    phases_ref[SPAN : 2 * SPAN, :] = lo
+    hi, lo = hi_lo(start_ref[...])
+    phases_ref[: 2 * SPAN, :] = hi
+    phases_ref[2 * SPAN : 4 * SPAN, :] = lo
 
 
 def beam_rows(ref, first, last):
@@ -223,6 +246,15 @@
         for chip in range(first, last)
     ]
     return jnp.concatenate(rows, 0)
+
+
+def side_rows(ref, side):
+    part = slice(side * PER_BLOCK, side * PER_BLOCK + PER_BLOCK)
+    return jnp.concatenate([ref[chip, part, :] for chip in range(CHIPS)], 0)
+
+
+def swap_sides(odd, early, late):
+    return jnp.concatenate([jnp.where(odd > 0.0, late, early), jnp.where(odd > 0.0, early, late)], 1)
 
 
 def transform(ref, step_ref, phase_ref, z_ref):
@@ -245,23 +277,28 @@
     wanted = jnp.where(row == 0, BINS * core, jnp.where(row == 1, BINS * core + BINS, core + 63 + row))
     info = dot(jnp.where(lane == wanted, 1.0, 0.0).astype(BF16), times, (((1,), (1,)), ((), ())))
     start, end, first, last = (info[k : k + 1, :] for k in range(4))
-    grains = jnp.where(end > start, jnp.minimum(last, float(PER_BLOCK - 1)) - first + 1.0, 0.0)
+    sides = jnp.minimum(last, float(2 * PER_BLOCK - 1)) - first
+    grains = jnp.where(end > start, jnp.floor(sides * 0.5) + 1.0, 0.0)
     earlier = dot(jnp.broadcast_to(grains, (8, 128)).astype(BF16), triangle(128, True))[0:1, :] + before
     return times, end, first, grains, earlier, earlier[:, 127:] + grains[:, 127:]
 
 
 def slots_half(slot_0, plan, ref):
     times, end, first, grains, earlier, _ = plan
-    slot = lax.broadcasted_iota(jnp.int32, (SLOTS, 128), 0).astype(F32) + slot_0
+    slot = lax.broadcasted_iota(jnp.int32, (128, 128), 0).astype(F32) + slot_0
     visit = lax.broadcasted_iota(jnp.int32, (SLOTS, 128), 1)
     mine = (slot >= earlier) & (slot < earlier + grains)
-    place = ((visit >> 3) * PER_BLOCK + 1).astype(F32) + first + (slot - earlier)
+    starts = dot(times, jnp.where(mine, 1.0, 0.0).astype(BF16), (((0,), (1,)), ((), ())))
+    slot, mine = slot[:SLOTS], mine[:SLOTS]
+    place = ((visit >> 3) * (2 * PER_BLOCK) + 1).astype(F32) + first + 2.0 * (slot - earlier)
     place = jnp.sum(jnp.where(mine, place, 0.0), axis=1, keepdims=True) - 1.0
     ends = jnp.sum(jnp.where(mine, jnp.broadcast_to(end, (SLOTS, 128)), 0.0), axis=1, keepdims=True)
-    starts = dot(times, jnp.where(mine, 1.0, 0.0).astype(BF16), (((0,), (1,)), ((), ())))
     places = lax.broadcasted_iota(jnp.int32, (SLOTS, HALF), 1).astype(F32)
-    pick = jnp.where(places == place, 1.0, 0.0).astype(BF16)
-    return place, ends, starts, dot(pick, beam_rows(ref, 0, CHIPS))
+    whole = jnp.where(place < 0.0, -4.0, jnp.floor(place * 0.5))
+    odd = jnp.where(place < 0.0, 0.0, place - 2.0 * whole)
+    early = dot(jnp.where(places == whole + odd, 1.0, 0.0).astype(BF16), side_rows(ref, 0))
+    late = dot(jnp.where(places == whole, 1.0, 0.0).astype(BF16), side_rows(ref, 1))
+    return place, ends, starts, swap_sides(odd, early, late)
 
 
 def half_kernel(ids, own_ref, step_ref, phase_ref, z_ref, total_ref, place_ref, ends_ref, starts_ref, gbeam_ref):
@@ -285,7 +322,7 @@
 def spectrum_kernel(
     ids,
     own_ref, other_ref, z_ref, total_ref, place_ref, ends_ref, starts_ref, gbeam_ref,
-    fold_ref, step_ref, short_ref, phases_ref, step2_ref, phase_ref,
+    fold_ref, step_ref, short_ref, phases_ref, side_ref, step2_ref, phase_ref,
     out_ref,
     z_s, gdft_s, gstep_s, gbeam_s, gtime_s, gstart_s, acc_s,
 ):
@@ -305,69 +342,92 @@
         is_mine = mine[0] >= 0.0
         place = jnp.where(is_mine, mine[0], more[0]).astype(jnp.int32)
         which = jnp.where(is_mine, core, 1 - core)
-        in_block = place & (PER_BLOCK - 1)
-        grain = ((2 * (place >> 5) + which) * PER_BLOCK + in_block).astype(F32)
+        side = place & (2 * PER_BLOCK - 1)
+        in_block, odd = side >> 1, (side & 1).astype(F32)
+        grain = ((2 * (place >> 6) + which) * PER_BLOCK + in_block).astype(F32)
         here = mine[3] + more[3]
-        times = (lane_iota + 128).astype(F32) * two_to(jnp.broadcast_to(in_block, (SLOTS, 128)))
-        gtime_s[...] = times
-        inside = times < mine[1] + more[1]
-        gbeam_s[:, :GRAIN] = jnp.where(inside, here[:, :GRAIN], 0.0)
-        gbeam_s[:, GRAIN:] = jnp.where(inside, here[:, GRAIN:], 0.0)
+        ends = mine[1] + more[1]
+        for k in range(2):
+            at = jnp.broadcast_to(side + k, (SLOTS, GRAIN))
+            times = (128 + (at & 1) * SIDE + (lane_iota & (SIDE - 1))).astype(F32) * two_to(at >> 1)
+            part = slice(k * GRAIN, k * GRAIN + GRAIN)
+            gtime_s[:, part] = times
+            gbeam_s[:, part] = jnp.where(times < ends, here[:, part], 0.0)
         starts = mine[2] + more[2]
         starts = jnp.where(core == 0, starts[:BINS], starts[BINS : 2 * BINS])
         for group in range(SLOTS // GROUP):
-            gstart_s[group] = starts if group == 0 else pltpu.roll(starts, SLOTS - group * GROUP, 1)
+            gstart_s[group] = starts if group == 0 else pltpu.roll(starts, 128 - group * GROUP, 1)
         dft = jnp.zeros((SLOTS, 2 * FREQS), F32)
-        ahead = jnp.zeros((SLOTS, 2 * GRAIN), F32)
+        early, late, gone = (jnp.zeros((SLOTS, GRAIN), F32) for _ in range(3))
         for grains, z, ref in ((own_grains, z_ref, own_ref), (other_grains, z_s, other_ref)):
             window = (grains >= grain) & (grains < grain + float(SPAN))
             dft = dft + dot(jnp.where(window, 1.0, 0.0).astype(BF16), z[...])
-            next_pick = jnp.where(grains == grain + float(SPAN), 1.0, 0.0).astype(BF16)
-            ahead = ahead + dot(next_pick, beam_rows(ref, 0, CHIPS))
-        offset = in_block & (SPAN - 1)
-        turner = jnp.where((lane_iota == offset) | (lane_iota == offset + SPAN), 1.0, 0.0)
+            then = grains == grain + float(SPAN)
+            early_pick = jnp.where(grains == grain + float(SPAN) + odd, 1.0, 0.0).astype(BF16)
+            late_pick = jnp.where(then, 1.0, 0.0).astype(BF16)
+            gone_pick = jnp.where(then, odd, jnp.where(grains == grain, -odd, 0.0)).astype(BF16)
+            early = early + dot(early_pick, side_rows(ref, 0))
+            late = late + dot(late_pick, side_rows(ref, 1))
+            gone = gone + dot(gone_pick, side_rows(ref, 0))
+        ahead = swap_sides(odd, early, late)
+        moved = dot(gone.astype(BF16), side_ref[...])
+        offset = side & (2 * SPAN - 1)
+        turner = jnp.where((lane_iota == offset) | (lane_iota == offset + 2 * SPAN), 1.0, 0.0)
         turned = dot(turner.astype(BF16), phases_ref[...])
         real, imag = dft[:, :FREQS], dft[:, FREQS:]
         cos_g, sin_g = turned[:, :FREQS], turned[:, FREQS:]
         step = dot((ahead - here).astype(BF16), step2_ref[...])
         for ref, real, imag in (
-            (gdft_s, real * cos_g - imag * sin_g, imag * cos_g + real * sin_g),
+            (gdft_s, real * cos_g - imag * sin_g + moved[:, :FREQS], imag * cos_g + real * sin_g + moved[:, FREQS:]),
             (gstep_s, step[:, :FREQS], step[:, FREQS:]),
         ):
             ref[:, :FREQS] = real
             ref[:, FREQS : 2 * FREQS] = imag - real
             ref[:, 2 * FREQS :] = real + imag
 
-        def group_step(group, inner):
-            rows = pl.ds(pl.multiple_of(group * GROUP, GROUP), GROUP)
-            beam8, time8, start8 = gbeam_s[rows, :], gtime_s[rows, :], gstart_s[group]
+        def fold(slot, size):
+            rows = pl.ds(pl.multiple_of(slot, 8), size)
+            beam8, time8, start8 = gbeam_s[rows, :], gtime_s[rows, :], gstart_s[slot // GROUP]
             dft8, step8 = gdft_s[rows, :], gstep_s[rows, :]
             left = []
-            for k in range(GROUP):
-                since = time8[k : k + 1, :] >= start8[:, k : k + 1]
-                real = jnp.where(since, beam8[k : k + 1, :GRAIN], 0.0)
-                imag = jnp.where(since, beam8[k : k + 1, GRAIN:], 0.0)
-                left.append(jnp.concatenate([real, imag], 1))
+            for k in range(size):
+                start = start8[:, k : k + 1]
+                sides = [
+                    jnp.where(time8[k : k + 1, at : at + GRAIN] >= start, beam8[k : k + 1, at : at + GRAIN], 0.0)
+                    for at in (0, GRAIN)
+                ]
+                left.append(jnp.concatenate(sides, 1))
             left = jnp.concatenate(left, 0).astype(BF16)
             for part, factor in ((0, dft8), (1, step8)):
                 folded = dot(left, fold_ref[:, part * 2 * FREQS : part * 2 * FREQS + 2 * FREQS])
                 sums = [acc_s[:, k * FREQS : k * FREQS + FREQS] for k in range(3 * part, 3 * part + 3)]
-                for k in range(GROUP):
+                for k in range(size):
                     rows = slice(k * BINS, k * BINS + BINS)
                     real, imag = folded[rows, :FREQS], folded[rows, FREQS:]
                     for n, value in enumerate((real + imag, real, imag)):
                         sums[n] = sums[n] + value * factor[k : k + 1, n * FREQS : n * FREQS + FREQS]
                 for n in range(3):
                     acc_s[:, (3 * part + n) * FREQS : (3 * part + n + 1) * FREQS] = sums[n]
+
+        def pair_step(pair, inner):
+            fold(2 * GROUP * pair, GROUP)
+            fold(2 * GROUP * pair + GROUP, GROUP)
             return inner
 
-        def pair_step(pair, inner):
-            group_step(2 * pair, inner)
-            return group_step(2 * pair + 1, inner)
-
-        groups = (jnp.minimum(count - batch * SLOTS, SLOTS) + GROUP - 1) // GROUP
-        lax.fori_loop(0, groups // 2, pair_step, 0)
-        lax.fori_loop(groups // 2 * 2, groups, group_step, 0)
+        def one_step(_, inner):
+            fold(pairs * 2 * GROUP, GROUP)
+            return inner
+
+        def half_step(_, inner):
+            fold(pairs * 2 * GROUP + rest // 2 * GROUP, GROUP // 2)
+            return inner
+
+        eights = (jnp.minimum(count - batch * SLOTS, SLOTS) + 7) // 8
+        pairs = eights // 4
+        rest = eights - 4 * pairs
+        lax.fori_loop(0, pairs, pair_step, 0)
+        lax.fori_loop(0, rest // 2, one_step, 0)
+        lax.fori_loop(0, rest % 2, half_step, 0)
 
     fold_batch(jnp.int32(0), (place_ref[:, 0:1], ends_ref[:, 0:1], starts_ref[...], gbeam_ref[...]))
 
@@ -415,8 +475,9 @@
             pltpu.VMEM((2, 2 * GRAIN, 2 * FREQS), BF16),
             pltpu.VMEM((2 * FREQS, 2 * FREQS), BF16),
             pltpu.VMEM((128, 2 * FREQS), BF16),
+            pltpu.VMEM((GRAIN, 2 * FREQS), BF16),
         ),
-        [given[k] for k in ("base", "turn", "fold2", "phase", "back")],
+        [given[k] for k in ("base", "turn", "fold2", "start", "back")],
         [pltpu.VMEM((2 * GRAIN, 2 * FREQS), BF16)],
         us=3.0,
     )
@@ -424,7 +485,7 @@
 
 
 def spectrum(own, other, ids, given, made):
-    fold, step, short, phases = made
+    fold, step, short, phases, side = made
     phase = given["phase"]
     half = call(
         functools.partial(half_kernel, ids),
@@ -433,7 +494,7 @@
             pltpu.VMEM((8, 128), F32),
             pltpu.VMEM((SLOTS, 128), F32),
             pltpu.VMEM((SLOTS, 128), F32),
-            pltpu.VMEM((128, SLOTS), F32),
+            pltpu.VMEM((128, 128), F32),
             pltpu.VMEM((SLOTS, 2 * GRAIN), F32),
         ),
         (own, step, phase),
@@ -444,14 +505,14 @@
         pltpu.VMEM((SLOTS, 3 * FREQS), F32),
         pltpu.VMEM((SLOTS, 3 * FREQS), F32),
         pltpu.VMEM((SLOTS, 2 * GRAIN), F32),
-        pltpu.VMEM((SLOTS, GRAIN), F32),
+        pltpu.VMEM((SLOTS, 2 * GRAIN), F32),
         pltpu.VMEM((SLOTS // GROUP, BINS, 128), F32),
         pltpu.VMEM((BINS, 6 * FREQS), F32),
     ]
     return call(
         functools.partial(spectrum_kernel, ids),
         jax.ShapeDtypeStruct((2, BINS, FREQS), F32),
-        (own, other, *half, fold, step, short, phases, given["step2"], phase),
+        (own, other, *half, fold, step, short, phases, side, given["step2"], phase),
         scratch,
         mib=16,
         us=5.0,

time: 46.2 us -> 45.8 us (level)
  no operation moved by 1% of the time
where the time goes in v9:
time: 45.8 us; the launch traced here: 45.5 us
  blocking collectives  33.7 us (74%)
  Pallas kernels  7.72 us (17%)
  starting transfers between devices  3.88 us (8%)
    all_to_all x1, blocking collectives, steps(): own = lax.all_to_all(packed, ('z', 'xh'), 0, 0, tiled=True)  21.8 us
    all_to_all x1, blocking collectives, steps(): parts = lax.all_to_all(partial_beam, 'dish', 0, 0, tiled=True)  11.9 us
    pallas_call x4, Pallas kernels, call(): pl.pallas_call(kernel, out_shape=outs if one else tuple(outs), in_specs=[...  5.75 us
    ppermute x1, starting transfers between devices, steps(): other = lax.ppermute(own, 'core', [(0, 1), (1, 0)])  3.88 us
    pallas_call x1, Pallas kernels, front(): pl.pallas_call(front_kernel, out_shape=(pltpu.VMEM((DISH_WAYS, 2 * PER_BL...  1.97 us
  transfers between devices with their start and end apart: 1, of which 0 were waited for; matrix products, arithmetic and copies ran while one was open for 0% of the time, Pallas kernels for 3%

profile of v9, /device:TPU:1, one launch (start us, length us, event | category | flops | bytes accessed | tf_op | source)
XLA Modules:
  0.0 45.5 jit_solution(14434771648041021104)
XLA Ops:
  0.0 2.0 %front.1 = (f32[8,64,128]{2,1,0:T(8,128)S(1)}, bf16[16,8,128]{2,1,0:T(8,128)(2,1)S(1)}) custom-call(bf16[2,8,4096]{2,1,0:T(8,128)(2,1)} %volts_hbm.1, bf16[2,8]{1,0:T(2,128)(2,1)} %weights_hbm.1, s32[32,128]{1,0:T(8,128)} %bitcast.2), custom_call_target="tpu_custom_call" | custom-call | flops 1048576 | bytes 1048576 | tf_op jit(solution)/shard_map/front/pallas_call | solution.py:525
  2.0 11.9 %all_to_all.10.parts_ref = f32[8,64,128]{2,1,0:T(8,128)S(1)} all-to-all(f32[8,64,128]{2,1,0:T(8,128)S(1)} %get-tuple-element.18), channel_id=1, replica_groups=mesh['z'=8,'xh'=2,'core'=2,'dish'=8] {'dish'}, dimensions={0} | all-to-all | bytes 524288 | tf_op jit(solution)/shard_map/all_to_all | solution.py:555
  13.9 0.0 copy-start.3
  13.9 0.0 copy-start.5
  13.9 0.1 shard_map.100
  14.0 0.0 copy-start.1
  14.0 0.0 copy-start.2
  14.0 0.0 copy-start.4
  14.0 21.8 %all_to_all.11.own_ref = bf16[16,72,128]{2,1,0:T(8,128)(2,1)S(1)} all-to-all(bf16[16,72,128]{2,1,0:T(8,128)(2,1)S(1)} %shard_map.100), channel_id=1, replica_groups=mesh['z'=8,'xh'=2,'core'=2,'dish'=8] {'z','xh'}, dimensions={0} | all-to-all | bytes 589824 | tf_op jit(solution)/shard_map/all_to_all | solution.py:557
  35.8 0.0 copy-start.6
  35.8 3.9 %collective-permute-start = (bf16[16,72,128]{2,1,0:T(8,128)(2,1)S(1)}, bf16[16,72,128]{2,1,0:T(8,128)(2,1)S(1)}, u32[]{:S(2)}, u32[]{:S(2)}) collective-permute-start(bf16[16,72,128]{2,1,0:T(8,128)(2,1)S(1)} %all_to_all.11.own_ref), channel_id=1, source_target_pairs={{0,8},{8,0},{1,9},{9,1},{2,10},{10,2},{3,11},{11,3},{4,12},{12,4},... | collective-permute-start | bytes 884744 | tf_op jit(solution)/shard_map/ppermute | solution.py:558
  39.7 0.0 copy-done.3
  39.7 0.0 copy-done.5
  39.7 0.0 copy-done.1
  39.7 0.0 copy-done.2
  39.7 0.0 copy-done.4
  39.7 0.5 %shard_map.101 = (bf16[256,1024]{1,0:T(8,128)(2,1)S(1)}, bf16[2,256,512]{2,1,0:T(8,128)(2,1)S(1)}, bf16[512,512]{1,0:T(8,128)(2,1)S(1)}, bf16[128,512]{1,0:T(8,128)(2,1)S(1)}, bf16[128,512]{1,0:T(8,128)(2,1)S(1)}) custom-call(f32[128,512]{1,0:T(8,128)S(1)} %copy-done.3, f32[128,128]{1,0:T(8,128)S(1)} %copy-done.5, bf16[256,512]{1,0:T(8,128)(2,1)S(1)} %copy-done.2, ...), custom_call_target="tpu_custom_call" | custom-call | flops 1500000000 | bytes 1048576 | tf_op jit(solution)/shard_map/pallas_call | solution.py:455
  40.2 0.0 copy-done.6
  40.2 0.0 copy-start
  40.2 0.8 %shard_map.102 = (bf16[512,512]{1,0:T(8,128)(2,1)S(1)}, f32[8,128]{1,0:T(8,128)S(1)}, f32[96,128]{1,0:T(8,128)S(1)}, f32[96,128]{1,0:T(8,128)S(1)}, f32[128,128]{1,0:T(8,128)S(1)}, /*index=5*/f32[96,256]{1,0:T(8,128)S(1)}) custom-call(bf16[16,72,128]{2,1,0:T(8,128)(2,1)S(1)} %all_to_all.11.own_ref, bf16[2,256,512]{2,1,0:T(8,128)(2,1)S(1)} %get-tuple-element.20.step_ref, ...), custom_call_target="tpu_custom_call" | custom-call | flops 500000000 | bytes 1048576 | tf_op jit(solution)/shard_map/pallas_call | solution.py:455
  41.1 0.0 collective-permute-done.other_ref
  41.1 0.1 copy-done
  41.2 4.3 %shard_map.103 = f32[2,32,256]{2,1,0:T(8,128)} custom-call(bf16[16,72,128]{2,1,0:T(8,128)(2,1)S(1)} %all_to_all.11.own_ref, bf16[16,72,128]{2,1,0:T(8,128)(2,1)S(1)} %collective-permute-done.other_ref, bf16[512,512]{1,0:T(8,128)(2,1)S(1)} %get-tuple-element.21.z_ref, f32[8,128]{1,0:T(8,128)S(1)} %get-tuple-element.22.total_ref, ...), custom_call_target="tpu_custom_call" | custom-call | flops 2500000000 | bytes 1048576 | tf_op jit(solution)/shard_map/pallas_call | solution.py:455
Async XLA Ops:
  13.9 25.8 %copy-start.3 = (f32[128,512]{1,0:T(8,128)S(1)}, f32[128,512]{1,0:T(8,128)}, u32[]{:S(2)}) copy-start(f32[128,512]{1,0:T(8,128)} %constant.14.clone.base_ref) | copy-start | bytes 786436
  13.9 25.8 %copy-start.5 = (f32[128,128]{1,0:T(8,128)S(1)}, f32[128,128]{1,0:T(8,128)}, u32[]{:S(2)}) copy-start(f32[128,128]{1,0:T(8,128)} %constant.15.clone.turn_ref) | copy-start | bytes 196612
  14.0 25.7 %copy-start.1 = (bf16[512,256]{1,0:T(8,128)(2,1)S(1)}, bf16[512,256]{1,0:T(8,128)(2,1)}, u32[]{:S(2)}) copy-start(bf16[512,256]{1,0:T(8,128)(2,1)} %constant.22.back_ref) | copy-start | bytes 786436
  14.0 25.7 %copy-start.2 = (bf16[256,512]{1,0:T(8,128)(2,1)S(1)}, bf16[256,512]{1,0:T(8,128)(2,1)}, u32[]{:S(2)}) copy-start(bf16[256,512]{1,0:T(8,128)(2,1)} %constant.21.fold2_ref) | copy-start | bytes 786436
  14.0 25.7 %copy-start.4 = (f32[32,512]{1,0:T(8,128)S(1)}, f32[32,512]{1,0:T(8,128)}, u32[]{:S(2)}) copy-start(f32[32,512]{1,0:T(8,128)} %constant.20.clone.start_ref) | copy-start | bytes 196612
  35.8 4.4 %copy-start.6 = (f32[16,512]{1,0:T(8,128)S(1)}, f32[16,512]{1,0:T(8,128)}, u32[]{:S(2)}) copy-start(f32[16,512]{1,0:T(8,128)} %constant.19.clone.phase_ref) | copy-start | bytes 98308
  35.8 5.2 %collective-permute-start = (bf16[16,72,128]{2,1,0:T(8,128)(2,1)S(1)}, bf16[16,72,128]{2,1,0:T(8,128)(2,1)S(1)}, u32[]{:S(2)}, u32[]{:S(2)}) collective-permute-start(bf16[16,72,128]{2,1,0:T(8,128)(2,1)S(1)} %all_to_all.11.own_ref), channel_id=1, source_target_pairs={{0,8},{8,0},{1,9},{9,1},{2,10},{10,2},{3,11},{11,3},{4,12},{12,4},... | collective-permute-start | bytes 884744 | tf_op jit(solution)/shard_map/ppermute | solution.py:558
  40.2 1.0 %copy-start = (bf16[256,512]{1,0:T(8,128)(2,1)S(1)}, bf16[256,512]{1,0:T(8,128)(2,1)}, u32[]{:S(2)}) copy-start(bf16[256,512]{1,0:T(8,128)(2,1)} %constant.23.step2_ref) | copy-start | bytes 786436

commit v10 on v9

--- a/solution.py
+++ b/solution.py
@@ -75,14 +75,16 @@
     }
 
 
+PIECES = [slice(k % 4 * (LOCAL // 4), k % 4 * (LOCAL // 4) + LOCAL // 4) for k in range(8)]
+
+
 def front_kernel(
     volts_hbm, weights_hbm, bins_hbm, beam_ref, visit_ref, volts_s, weights_s, bins_s, time_s, row_s, sems
 ):
+    parts = [(volts_hbm.at[k // 4, :, at], volts_s.at[k // 4, :, at]) for k, at in enumerate(PIECES)]
+    parts += [(bins_hbm, bins_s), (weights_hbm, weights_s)]
     copies = [
-        pltpu.make_async_copy(source, target, sems.at[k])
-        for k, (source, target) in enumerate(
-            ((bins_hbm, bins_s), (weights_hbm, weights_s), (volts_hbm, volts_s))
-        )
+        pltpu.make_async_copy(source, target, sems.at[k]) for k, (source, target) in enumerate(parts)
     ]
     for copy in copies:
         copy.start()
@@ -257,14 +259,16 @@
     return jnp.concatenate([jnp.where(odd > 0.0, late, early), jnp.where(odd > 0.0, early, late)], 1)
 
 
-def transform(ref, step_ref, phase_ref, z_ref):
+def transform(ref, step_ref, phase_ref, z_ref, fine):
     cos16, sin16 = phase_ref[:, :FREQS], phase_ref[:, FREQS:]
     cos_rows = jnp.concatenate([cos16] * (128 // SPAN), 0)
     sin_rows = jnp.concatenate([sin16] * (128 // SPAN), 0)
     for tile in range(HALF // 128):
         rows = slice(tile * 128, tile * 128 + 128)
         beam = beam_rows(ref, 4 * tile, 4 * tile + 4)
-        both = dot(beam, step_ref[0]) + dot(beam, step_ref[1])
+        both = dot(beam, step_ref[0])
+        if fine:
+            both = both + dot(beam, step_ref[1])
         real, imag = both[:, :FREQS], both[:, FREQS:]
         z_ref[rows, :FREQS] = (real * cos_rows + imag * sin_rows).astype(BF16)
         z_ref[rows, FREQS:] = (imag * cos_rows - real * sin_rows).astype(BF16)
@@ -310,7 +314,7 @@
     ends_ref[...] = jnp.broadcast_to(ends, (SLOTS, 128))
     starts_ref[...] = starts
     gbeam_ref[...] = beam
-    transform(own_ref, step_ref, phase_ref, z_ref)
+    transform(own_ref, step_ref, phase_ref, z_ref, True)
 
 
 def grain_row(which):
@@ -330,7 +334,7 @@
     before = total_ref[0:1, 0:1]
     other_plan = plan_half(other_ref, core, before)
     count = jnp.max(other_plan[-1]).astype(jnp.int32)
-    transform(other_ref, step_ref, phase_ref, z_s)
+    transform(other_ref, step_ref, phase_ref, z_s, False)
     acc_s[...] = jnp.zeros(acc_s.shape, F32)
     own_grains = jnp.broadcast_to(grain_row(core), (SLOTS, HALF))
     other_grains = jnp.broadcast_to(grain_row(1 - core), (SLOTS, HALF))
@@ -536,7 +540,7 @@
             pltpu.VMEM(bins.shape, jnp.int32),
             pltpu.VMEM((72, GRAIN), F32),
             pltpu.VMEM((72, GRAIN), F32),
-            pltpu.SemaphoreType.DMA((3,)),
+            pltpu.SemaphoreType.DMA((len(PIECES) + 2,)),
         ],
         compiler_params=pltpu.CompilerParams(vmem_limit_bytes=8 << 20),
         cost_estimate=pl.CostEstimate(flops=1 << 20, bytes_accessed=1 << 20, transcendentals=0),

time: 45.8 us -> 45.7 us (level)
  no operation moved by 1% of the time
where the time goes in v10:
time: 45.7 us; the launch traced here: 45.4 us
  blocking collectives  33.7 us (74%)
  Pallas kernels  7.6 us (17%)
  starting transfers between devices  3.88 us (8%)
    all_to_all x1, blocking collectives, steps(): own = lax.all_to_all(packed, ('z', 'xh'), 0, 0, tiled=True)  21.8 us
    all_to_all x1, blocking collectives, steps(): parts = lax.all_to_all(partial_beam, 'dish', 0, 0, tiled=True)  11.9 us
    pallas_call x4, Pallas kernels, call(): pl.pallas_call(kernel, out_shape=outs if one else tuple(outs), in_specs=[...  5.65 us
    ppermute x1, starting transfers between devices, steps(): other = lax.ppermute(own, 'core', [(0, 1), (1, 0)])  3.88 us
    pallas_call x1, Pallas kernels, front(): pl.pallas_call(front_kernel, out_shape=(pltpu.VMEM((DISH_WAYS, 2 * PER_BL...  1.96 us
  transfers between devices with their start and end apart: 1, of which 0 were waited for; matrix products, arithmetic and copies ran while one was open for 0% of the time, Pallas kernels for 3%

profile of v10, /device:TPU:1, one launch (start us, length us, event | category | flops | bytes accessed | tf_op | source)
XLA Modules:
  0.0 45.4 jit_solution(11690689654500721727)
XLA Ops:
  0.0 2.0 %front.1 = (f32[8,64,128]{2,1,0:T(8,128)S(1)}, bf16[16,8,128]{2,1,0:T(8,128)(2,1)S(1)}) custom-call(bf16[2,8,4096]{2,1,0:T(8,128)(2,1)} %volts_hbm.1, bf16[2,8]{1,0:T(2,128)(2,1)} %weights_hbm.1, s32[32,128]{1,0:T(8,128)} %bitcast.2), custom_call_target="tpu_custom_call" | custom-call | flops 1048576 | bytes 1048576 | tf_op jit(solution)/shard_map/front/pallas_call | solution.py:529
  2.0 11.9 %all_to_all.10.parts_ref = f32[8,64,128]{2,1,0:T(8,128)S(1)} all-to-all(f32[8,64,128]{2,1,0:T(8,128)S(1)} %get-tuple-element.18), channel_id=1, replica_groups=mesh['z'=8,'xh'=2,'core'=2,'dish'=8] {'dish'}, dimensions={0} | all-to-all | bytes 524288 | tf_op jit(solution)/shard_map/all_to_all | solution.py:559
  13.9 0.0 copy-start.3
  13.9 0.0 copy-start.5
  13.9 0.1 shard_map.100
  14.0 0.0 copy-start.1
  14.0 0.0 copy-start.2
  14.0 0.0 copy-start.4
  14.0 21.8 %all_to_all.11.own_ref = bf16[16,72,128]{2,1,0:T(8,128)(2,1)S(1)} all-to-all(bf16[16,72,128]{2,1,0:T(8,128)(2,1)S(1)} %shard_map.100), channel_id=1, replica_groups=mesh['z'=8,'xh'=2,'core'=2,'dish'=8] {'z','xh'}, dimensions={0} | all-to-all | bytes 589824 | tf_op jit(solution)/shard_map/all_to_all | solution.py:561
  35.8 0.0 copy-start.6
  35.8 3.9 %collective-permute-start = (bf16[16,72,128]{2,1,0:T(8,128)(2,1)S(1)}, bf16[16,72,128]{2,1,0:T(8,128)(2,1)S(1)}, u32[]{:S(2)}, u32[]{:S(2)}) collective-permute-start(bf16[16,72,128]{2,1,0:T(8,128)(2,1)S(1)} %all_to_all.11.own_ref), channel_id=1, source_target_pairs={{0,8},{8,0},{1,9},{9,1},{2,10},{10,2},{3,11},{11,3},{4,12},{12,4},... | collective-permute-start | bytes 884744 | tf_op jit(solution)/shard_map/ppermute | solution.py:562
  39.7 0.0 copy-done.3
  39.7 0.0 copy-done.5
  39.7 0.0 copy-done.1
  39.7 0.0 copy-done.2
  39.7 0.0 copy-done.4
  39.7 0.5 %shard_map.101 = (bf16[256,1024]{1,0:T(8,128)(2,1)S(1)}, bf16[2,256,512]{2,1,0:T(8,128)(2,1)S(1)}, bf16[512,512]{1,0:T(8,128)(2,1)S(1)}, bf16[128,512]{1,0:T(8,128)(2,1)S(1)}, bf16[128,512]{1,0:T(8,128)(2,1)S(1)}) custom-call(f32[128,512]{1,0:T(8,128)S(1)} %copy-done.3, f32[128,128]{1,0:T(8,128)S(1)} %copy-done.5, bf16[256,512]{1,0:T(8,128)(2,1)S(1)} %copy-done.2, ...), custom_call_target="tpu_custom_call" | custom-call | flops 1500000000 | bytes 1048576 | tf_op jit(solution)/shard_map/pallas_call | solution.py:459
  40.2 0.0 copy-done.6
  40.2 0.0 copy-start
  40.2 0.8 %shard_map.102 = (bf16[512,512]{1,0:T(8,128)(2,1)S(1)}, f32[8,128]{1,0:T(8,128)S(1)}, f32[96,128]{1,0:T(8,128)S(1)}, f32[96,128]{1,0:T(8,128)S(1)}, f32[128,128]{1,0:T(8,128)S(1)}, /*index=5*/f32[96,256]{1,0:T(8,128)S(1)}) custom-call(bf16[16,72,128]{2,1,0:T(8,128)(2,1)S(1)} %all_to_all.11.own_ref, bf16[2,256,512]{2,1,0:T(8,128)(2,1)S(1)} %get-tuple-element.20.step_ref, ...), custom_call_target="tpu_custom_call" | custom-call | flops 500000000 | bytes 1048576 | tf_op jit(solution)/shard_map/pallas_call | solution.py:459
  41.1 0.0 collective-permute-done.other_ref
  41.1 0.1 copy-done
  41.2 4.2 %shard_map.103 = f32[2,32,256]{2,1,0:T(8,128)} custom-call(bf16[16,72,128]{2,1,0:T(8,128)(2,1)S(1)} %all_to_all.11.own_ref, bf16[16,72,128]{2,1,0:T(8,128)(2,1)S(1)} %collective-permute-done.other_ref, bf16[512,512]{1,0:T(8,128)(2,1)S(1)} %get-tuple-element.21.z_ref, f32[8,128]{1,0:T(8,128)S(1)} %get-tuple-element.22.total_ref, ...), custom_call_target="tpu_custom_call" | custom-call | flops 2500000000 | bytes 1048576 | tf_op jit(solution)/shard_map/pallas_call | solution.py:459
Async XLA Ops:
  13.9 25.8 %copy-start.3 = (f32[128,512]{1,0:T(8,128)S(1)}, f32[128,512]{1,0:T(8,128)}, u32[]{:S(2)}) copy-start(f32[128,512]{1,0:T(8,128)} %constant.14.clone.base_ref) | copy-start | bytes 786436
  13.9 25.8 %copy-start.5 = (f32[128,128]{1,0:T(8,128)S(1)}, f32[128,128]{1,0:T(8,128)}, u32[]{:S(2)}) copy-start(f32[128,128]{1,0:T(8,128)} %constant.15.clone.turn_ref) | copy-start | bytes 196612
  14.0 25.7 %copy-start.1 = (bf16[512,256]{1,0:T(8,128)(2,1)S(1)}, bf16[512,256]{1,0:T(8,128)(2,1)}, u32[]{:S(2)}) copy-start(bf16[512,256]{1,0:T(8,128)(2,1)} %constant.22.back_ref) | copy-start | bytes 786436
  14.0 25.7 %copy-start.2 = (bf16[256,512]{1,0:T(8,128)(2,1)S(1)}, bf16[256,512]{1,0:T(8,128)(2,1)}, u32[]{:S(2)}) copy-start(bf16[256,512]{1,0:T(8,128)(2,1)} %constant.21.fold2_ref) | copy-start | bytes 786436
  14.0 25.7 %copy-start.4 = (f32[32,512]{1,0:T(8,128)S(1)}, f32[32,512]{1,0:T(8,128)}, u32[]{:S(2)}) copy-start(f32[32,512]{1,0:T(8,128)} %constant.20.clone.start_ref) | copy-start | bytes 196612
  35.8 4.4 %copy-start.6 = (f32[16,512]{1,0:T(8,128)S(1)}, f32[16,512]{1,0:T(8,128)}, u32[]{:S(2)}) copy-start(f32[16,512]{1,0:T(8,128)} %constant.19.clone.phase_ref) | copy-start | bytes 98308
  35.8 5.3 %collective-permute-start = (bf16[16,72,128]{2,1,0:T(8,128)(2,1)S(1)}, bf16[16,72,128]{2,1,0:T(8,128)(2,1)S(1)}, u32[]{:S(2)}, u32[]{:S(2)}) collective-permute-start(bf16[16,72,128]{2,1,0:T(8,128)(2,1)S(1)} %all_to_all.11.own_ref), channel_id=1, source_target_pairs={{0,8},{8,0},{1,9},{9,1},{2,10},{10,2},{3,11},{11,3},{4,12},{12,4},... | collective-permute-start | bytes 884744 | tf_op jit(solution)/shard_map/ppermute | solution.py:562
  40.2 1.0 %copy-start = (bf16[256,512]{1,0:T(8,128)(2,1)S(1)}, bf16[256,512]{1,0:T(8,128)(2,1)}, u32[]{:S(2)}) copy-start(bf16[256,512]{1,0:T(8,128)(2,1)} %constant.23.step2_ref) | copy-start | bytes 786436

commit v11 on v10

--- a/solution.py
+++ b/solution.py
@@ -199,8 +199,13 @@
 
 
 def table_kernel(
-    ids, base_ref, turn_ref, fold2_ref, start_ref, back_ref, fold_ref, step_ref, short_ref, phases_ref, side_ref, last_s
+    ids,
+    base_ref, turn_ref, fold2_ref, start_ref, back_ref, step2_in, phase_in,
+    fold_ref, step_ref, short_ref, phases_ref, side_ref, step2_ref, phase_ref,
+    last_s,
 ):
+    step2_ref[...] = step2_in[...]
+    phase_ref[...] = phase_in[...]
     _, dish, _ = ids()
     lane = lax.broadcasted_iota(jnp.int32, (GRAIN, 128), 1)
     turn = turn_ref[...]
@@ -480,17 +485,18 @@
             pltpu.VMEM((2 * FREQS, 2 * FREQS), BF16),
             pltpu.VMEM((128, 2 * FREQS), BF16),
             pltpu.VMEM((GRAIN, 2 * FREQS), BF16),
+            pltpu.VMEM((2 * GRAIN, 2 * FREQS), BF16),
+            pltpu.VMEM((SPAN, 2 * FREQS), F32),
         ),
-        [given[k] for k in ("base", "turn", "fold2", "start", "back")],
+        [given[k] for k in ("base", "turn", "fold2", "start", "back", "step2", "phase")],
         [pltpu.VMEM((2 * GRAIN, 2 * FREQS), BF16)],
         us=3.0,
     )
-    return given, made
-
-
-def spectrum(own, other, ids, given, made):
-    fold, step, short, phases, side = made
-    phase = given["phase"]
+    return made
+
+
+def spectrum(own, other, ids, made):
+    fold, step, short, phases, side, step2, phase = made
     half = call(
         functools.partial(half_kernel, ids),
         (
@@ -516,7 +522,7 @@
     return call(
         functools.partial(spectrum_kernel, ids),
         jax.ShapeDtypeStruct((2, BINS, FREQS), F32),
-        (own, other, *half, fold, step, short, phases, side, given["step2"], phase),
+        (own, other, *half, fold, step, short, phases, side, step2, phase),
         scratch,
         mib=16,
         us=5.0,
@@ -554,13 +560,13 @@
         owner = (lax.axis_index("z") * 2 + lax.axis_index("xh")) * 2 + core
         return owner, lax.axis_index("dish"), core
 
-    given, made = make_tables(ids)
+    made = make_tables(ids)
     partial_beam, visits = front(voltages, beam_weights, phase_bins.reshape(PER_BLOCK, GRAIN))
     parts = lax.all_to_all(partial_beam, "dish", 0, 0, tiled=True)
     packed = call(pack_kernel, pltpu.VMEM((CHIPS, ROWS, GRAIN), BF16), (parts, visits), us=0.3)
     own = lax.all_to_all(packed, ("z", "xh"), 0, 0, tiled=True)
     other = lax.ppermute(own, "core", [(0, 1), (1, 0)])
-    return jnp.transpose(spectrum(own, other, ids, given, made), (2, 0, 1))
+    return jnp.transpose(spectrum(own, other, ids, made), (2, 0, 1))
 
 
 def solution(mesh):

time: 45.7 us -> 45.6 us (level)
  no operation moved by 1% of the time
where the time goes in v11:
time: 45.6 us; the launch traced here: 45.3 us
  blocking collectives  33.7 us (74%)
  Pallas kernels  7.61 us (17%)
  starting transfers between devices  3.88 us (9%)
    all_to_all x1, blocking collectives, steps(): own = lax.all_to_all(packed, ('z', 'xh'), 0, 0, tiled=True)  21.8 us
    all_to_all x1, blocking collectives, steps(): parts = lax.all_to_all(partial_beam, 'dish', 0, 0, tiled=True)  11.9 us
    pallas_call x4, Pallas kernels, call(): pl.pallas_call(kernel, out_shape=outs if one else tuple(outs), in_specs=[...  5.65 us
    ppermute x1, starting transfers between devices, steps(): other = lax.ppermute(own, 'core', [(0, 1), (1, 0)])  3.88 us
    pallas_call x1, Pallas kernels, front(): pl.pallas_call(front_kernel, out_shape=(pltpu.VMEM((DISH_WAYS, 2 * PER_BL...  1.96 us
  transfers between devices with their start and end apart: 1, of which 0 were waited for; matrix products, arithmetic and copies ran while one was open for 0% of the time, Pallas kernels for 3%

profile of v11, /device:TPU:1, one launch (start us, length us, event | category | flops | bytes accessed | tf_op | source)
XLA Modules:
  0.0 45.3 jit_solution(9782599271559418835)
XLA Ops:
  0.0 2.0 %front.1 = (f32[8,64,128]{2,1,0:T(8,128)S(1)}, bf16[16,8,128]{2,1,0:T(8,128)(2,1)S(1)}) custom-call(bf16[2,8,4096]{2,1,0:T(8,128)(2,1)} %volts_hbm.1, bf16[2,8]{1,0:T(2,128)(2,1)} %weights_hbm.1, s32[32,128]{1,0:T(8,128)} %bitcast.2), custom_call_target="tpu_custom_call" | custom-call | flops 1048576 | bytes 1048576 | tf_op jit(solution)/shard_map/front/pallas_call | solution.py:535
  2.0 0.0 copy-start.6
  2.0 11.9 %all_to_all.10.parts_ref = f32[8,64,128]{2,1,0:T(8,128)S(1)} all-to-all(f32[8,64,128]{2,1,0:T(8,128)S(1)} %get-tuple-element.20), channel_id=1, replica_groups=mesh['z'=8,'xh'=2,'core'=2,'dish'=8] {'dish'}, dimensions={0} | all-to-all | bytes 524288 | tf_op jit(solution)/shard_map/all_to_all | solution.py:565
  13.9 0.0 copy-start.2
  13.9 0.0 copy-start.3
  13.9 0.0 copy-start.5
  13.9 0.1 shard_map.100
  14.0 0.0 copy-start
  14.0 0.0 copy-start.1
  14.0 0.0 copy-start.4
  14.0 21.8 %all_to_all.11.own_ref = bf16[16,72,128]{2,1,0:T(8,128)(2,1)S(1)} all-to-all(bf16[16,72,128]{2,1,0:T(8,128)(2,1)S(1)} %shard_map.100), channel_id=1, replica_groups=mesh['z'=8,'xh'=2,'core'=2,'dish'=8] {'z','xh'}, dimensions={0} | all-to-all | bytes 589824 | tf_op jit(solution)/shard_map/all_to_all | solution.py:567
  35.8 3.9 %collective-permute-start = (bf16[16,72,128]{2,1,0:T(8,128)(2,1)S(1)}, bf16[16,72,128]{2,1,0:T(8,128)(2,1)S(1)}, u32[]{:S(2)}, u32[]{:S(2)}) collective-permute-start(bf16[16,72,128]{2,1,0:T(8,128)(2,1)S(1)} %all_to_all.11.own_ref), channel_id=1, source_target_pairs={{0,8},{8,0},{1,9},{9,1},{2,10},{10,2},{3,11},{11,3},{4,12},{12,4},... | collective-permute-start | bytes 884744 | tf_op jit(solution)/shard_map/ppermute | solution.py:568
  39.7 0.0 copy-done.6
  39.7 0.0 copy-done.2
  39.7 0.0 copy-done.3
  39.7 0.0 copy-done.5
  39.7 0.0 copy-done
  39.7 0.0 copy-done.1
  39.7 0.0 copy-done.4
  39.8 0.5 %shard_map.101 = (bf16[256,1024]{1,0:T(8,128)(2,1)S(1)}, bf16[2,256,512]{2,1,0:T(8,128)(2,1)S(1)}, bf16[512,512]{1,0:T(8,128)(2,1)S(1)}, bf16[128,512]{1,0:T(8,1...) custom-call(f32[128,512]{1,0:T(8,128)S(1)} %copy-done.3, ...), custom_call_target="tpu_custom_call" | custom-call | flops 1500000000 | bytes 1048576 | tf_op jit(solution)/shard_map/pallas_call | solution.py:464
  40.2 0.8 %shard_map.102 = (bf16[512,512]{1,0:T(8,128)(2,1)S(1)}, f32[8,128]{1,0:T(8,128)S(1)}, f32[96,128]{1,0:T(8,128)S(1)}, f32[96,128]{1,0:T(8,128)S(1)}, f32[128,128]{1,0:T(8,128)S(1)}, /*index=5*/f32[96,256]{1,0:T(8,128)S(1)}) custom-call(bf16[16,72,128]{2,1,0:T(8,128)(2,1)S(1)} %all_to_all.11.own_ref, bf16[2,256,512]{2,1,0:T(8,128)(2,1)S(1)} %get-tuple-element.22.step_ref, ...), custom_call_target="tpu_custom_call" | custom-call | flops 500000000 | bytes 1048576 | tf_op jit(solution)/shard_map/pallas_call | solution.py:464
  41.1 0.0 collective-permute-done.other_ref
  41.1 4.2 %shard_map.103 = f32[2,32,256]{2,1,0:T(8,128)} custom-call(bf16[16,72,128]{2,1,0:T(8,128)(2,1)S(1)} %all_to_all.11.own_ref, bf16[16,72,128]{2,1,0:T(8,128)(2,1)S(1)} %collective-permute-done.other_ref, bf16[512,512]{1,0:T(8,128)(2,1)S(1)} %get-tuple-element.24.z_ref, f32[8,128]{1,0:T(8,128)S(1)} %get-tuple-element.25.total_ref, ...), custom_call_target="tpu_custom_call" | custom-call | flops 2500000000 | bytes 1048576 | tf_op jit(solution)/shard_map/pallas_call | solution.py:464
Async XLA Ops:
  2.0 37.8 %copy-start.6 = (f32[16,512]{1,0:T(8,128)S(1)}, f32[16,512]{1,0:T(8,128)}, u32[]{:S(2)}) copy-start(f32[16,512]{1,0:T(8,128)} %constant.19.clone.phase_in) | copy-start | bytes 98308
  13.9 25.8 %copy-start.2 = (bf16[256,512]{1,0:T(8,128)(2,1)S(1)}, bf16[256,512]{1,0:T(8,128)(2,1)}, u32[]{:S(2)}) copy-start(bf16[256,512]{1,0:T(8,128)(2,1)} %constant.21.fold2_ref) | copy-start | bytes 786436
  13.9 25.8 %copy-start.3 = (f32[128,512]{1,0:T(8,128)S(1)}, f32[128,512]{1,0:T(8,128)}, u32[]{:S(2)}) copy-start(f32[128,512]{1,0:T(8,128)} %constant.14.clone.base_ref) | copy-start | bytes 786436
  13.9 25.8 %copy-start.5 = (f32[128,128]{1,0:T(8,128)S(1)}, f32[128,128]{1,0:T(8,128)}, u32[]{:S(2)}) copy-start(f32[128,128]{1,0:T(8,128)} %constant.15.clone.turn_ref) | copy-start | bytes 196612
  14.0 25.7 %copy-start = (bf16[256,512]{1,0:T(8,128)(2,1)S(1)}, bf16[256,512]{1,0:T(8,128)(2,1)}, u32[]{:S(2)}) copy-start(bf16[256,512]{1,0:T(8,128)(2,1)} %constant.23.step2_in) | copy-start | bytes 786436
  14.0 25.7 %copy-start.1 = (bf16[512,256]{1,0:T(8,128)(2,1)S(1)}, bf16[512,256]{1,0:T(8,128)(2,1)}, u32[]{:S(2)}) copy-start(bf16[512,256]{1,0:T(8,128)(2,1)} %constant.22.back_ref) | copy-start | bytes 786436
  14.0 25.7 %copy-start.4 = (f32[32,512]{1,0:T(8,128)S(1)}, f32[32,512]{1,0:T(8,128)}, u32[]{:S(2)}) copy-start(f32[32,512]{1,0:T(8,128)} %constant.20.clone.start_ref) | copy-start | bytes 196612
  35.8 5.3 %collective-permute-start = (bf16[16,72,128]{2,1,0:T(8,128)(2,1)S(1)}, bf16[16,72,128]{2,1,0:T(8,128)(2,1)S(1)}, u32[]{:S(2)}, u32[]{:S(2)}) collective-permute-start(bf16[16,72,128]{2,1,0:T(8,128)(2,1)S(1)} %all_to_all.11.own_ref), channel_id=1, source_target_pairs={{0,8},{8,0},{1,9},{9,1},{2,10},{10,2},{3,11},{11,3},{4,12},{12,4},... | collective-permute-start | bytes 884744 | tf_op jit(solution)/shard_map/ppermute | solution.py:568

commit v12 on v10

--- a/solution.py
+++ b/solution.py
@@ -105,6 +105,10 @@
         beam_ref[way] = rows
 
 
+def pair_at(place):
+    return 2 * (place & 7) + (place >> 3)
+
+
 def pack_kernel(parts_ref, visit_ref, out_ref):
     total = parts_ref[0]
     for way in range(1, DISH_WAYS):
@@ -116,7 +120,7 @@
     rows = jnp.concatenate([early_side, late_side], 0).astype(BF16)
     for chip in range(CHIPS):
         out_ref[chip, : 2 * PER_BLOCK, :] = rows
-        out_ref[chip, 2 * PER_BLOCK :, :] = visit_ref[chip]
+        out_ref[chip, 2 * PER_BLOCK :, :] = visit_ref[pair_at(chip)]
 
 
 def coded_times(shape):
@@ -319,7 +323,7 @@
 
 def grain_row(which):
     place = lax.broadcasted_iota(jnp.int32, (8, HALF), 1)
-    grain = (2 * (place >> 5) + which) * PER_BLOCK + (place & (PER_BLOCK - 1))
+    grain = (2 * pair_at(place >> 5) + which) * PER_BLOCK + (place & (PER_BLOCK - 1))
     return grain.astype(F32)[0:1, :]
 
 
@@ -348,7 +352,7 @@
         which = jnp.where(is_mine, core, 1 - core)
         side = place & (2 * PER_BLOCK - 1)
         in_block, odd = side >> 1, (side & 1).astype(F32)
-        grain = ((2 * (place >> 6) + which) * PER_BLOCK + in_block).astype(F32)
+        grain = ((2 * pair_at(place >> 6) + which) * PER_BLOCK + in_block).astype(F32)
         here = mine[3] + more[3]
         ends = mine[1] + more[1]
         for k in range(2):
@@ -558,7 +562,7 @@
     partial_beam, visits = front(voltages, beam_weights, phase_bins.reshape(PER_BLOCK, GRAIN))
     parts = lax.all_to_all(partial_beam, "dish", 0, 0, tiled=True)
     packed = call(pack_kernel, pltpu.VMEM((CHIPS, ROWS, GRAIN), BF16), (parts, visits), us=0.3)
-    own = lax.all_to_all(packed, ("z", "xh"), 0, 0, tiled=True)
+    own = lax.all_to_all(packed, ("xh", "z"), 0, 0, tiled=True)
     other = lax.ppermute(own, "core", [(0, 1), (1, 0)])
     return jnp.transpose(spectrum(own, other, ids, given, made), (2, 0, 1))
 

time: 45.7 us -> 43.6 us (0.954)
  blocking collectives: 33.7 us -> 31.7 us
    all_to_all x1, blocking collectives: 21.8 us -> 19.8 us  [steps(): own = lax.all_to_all(packed, ('xh', 'z'), 0, 0, tiled=True)]
where the time goes in v12:
time: 43.6 us; the launch traced here: 43.3 us
  blocking collectives  31.7 us (73%)
  Pallas kernels  7.61 us (17%)
  starting transfers between devices  3.75 us (9%)
    all_to_all x1, blocking collectives, steps(): own = lax.all_to_all(packed, ('xh', 'z'), 0, 0, tiled=True)  19.8 us
    all_to_all x1, blocking collectives, steps(): parts = lax.all_to_all(partial_beam, 'dish', 0, 0, tiled=True)  11.9 us
    pallas_call x4, Pallas kernels, call(): pl.pallas_call(kernel, out_shape=outs if one else tuple(outs), in_specs=[...  5.66 us
    ppermute x1, starting transfers between devices, steps(): other = lax.ppermute(own, 'core', [(0, 1), (1, 0)])  3.75 us
    pallas_call x1, Pallas kernels, front(): pl.pallas_call(front_kernel, out_shape=(pltpu.VMEM((DISH_WAYS, 2 * PER_BL...  1.96 us
  transfers between devices with their start and end apart: 1, of which 0 were waited for; matrix products, arithmetic and copies ran while one was open for 0% of the time, Pallas kernels for 3%

profile of v12, /device:TPU:1, one launch (start us, length us, event | category | flops | bytes accessed | tf_op | source)
XLA Modules:
  0.0 43.3 jit_solution(10174165444931094942)
XLA Ops:
  0.0 2.0 %front.1 = (f32[8,64,128]{2,1,0:T(8,128)S(1)}, bf16[16,8,128]{2,1,0:T(8,128)(2,1)S(1)}) custom-call(bf16[2,8,4096]{2,1,0:T(8,128)(2,1)} %volts_hbm.1, bf16[2,8]{1,0:T(2,128)(2,1)} %weights_hbm.1, s32[32,128]{1,0:T(8,128)} %bitcast.2), custom_call_target="tpu_custom_call" | custom-call | flops 1048576 | bytes 1048576 | tf_op jit(solution)/shard_map/front/pallas_call | solution.py:533
  2.0 11.9 %all_to_all.10.parts_ref = f32[8,64,128]{2,1,0:T(8,128)S(1)} all-to-all(f32[8,64,128]{2,1,0:T(8,128)S(1)} %get-tuple-element.18), channel_id=1, replica_groups=mesh['z'=8,'xh'=2,'core'=2,'dish'=8] {'dish'}, dimensions={0} | all-to-all | bytes 524288 | tf_op jit(solution)/shard_map/all_to_all | solution.py:563
  13.9 0.0 copy-start.3
  13.9 0.0 copy-start.5
  13.9 0.1 shard_map.100
  14.0 0.0 copy-start.1
  14.0 0.0 copy-start.2
  14.0 0.0 copy-start.4
  14.0 19.8 %all_to_all.11.own_ref = bf16[16,72,128]{2,1,0:T(8,128)(2,1)S(1)} all-to-all(bf16[16,72,128]{2,1,0:T(8,128)(2,1)S(1)} %shard_map.100), channel_id=1, replica_groups=mesh['z'=8,'xh'=2,'core'=2,'dish'=8] {'xh','z'}, dimensions={0} | all-to-all | bytes 589824 | tf_op jit(solution)/shard_map/all_to_all | solution.py:565
  33.8 0.0 copy-start.6
  33.8 3.7 %collective-permute-start = (bf16[16,72,128]{2,1,0:T(8,128)(2,1)S(1)}, bf16[16,72,128]{2,1,0:T(8,128)(2,1)S(1)}, u32[]{:S(2)}, u32[]{:S(2)}) collective-permute-start(bf16[16,72,128]{2,1,0:T(8,128)(2,1)S(1)} %all_to_all.11.own_ref), channel_id=1, source_target_pairs={{0,8},{8,0},{1,9},{9,1},{2,10},{10,2},{3,11},{11,3},{4,12},{12,4},... | collective-permute-start | bytes 884744 | tf_op jit(solution)/shard_map/ppermute | solution.py:566
  37.6 0.0 copy-done.3
  37.6 0.0 copy-done.5
  37.6 0.0 copy-done.1
  37.6 0.0 copy-done.2
  37.6 0.0 copy-done.4
  37.6 0.5 %shard_map.101 = (bf16[256,1024]{1,0:T(8,128)(2,1)S(1)}, bf16[2,256,512]{2,1,0:T(8,128)(2,1)S(1)}, bf16[512,512]{1,0:T(8,128)(2,1)S(1)}, bf16[128,512]{1,0:T(8,128)(2,1)S(1)}, bf16[128,512]{1,0:T(8,128)(2,1)S(1)}) custom-call(f32[128,512]{1,0:T(8,128)S(1)} %copy-done.3, f32[128,128]{1,0:T(8,128)S(1)} %copy-done.5, bf16[256,512]{1,0:T(8,128)(2,1)S(1)} %copy-done.2, ...), custom_call_target="tpu_custom_call" | custom-call | flops 1500000000 | bytes 1048576 | tf_op jit(solution)/shard_map/pallas_call | solution.py:463
  38.1 0.0 copy-done.6
  38.1 0.0 copy-start
  38.1 0.8 %shard_map.102 = (bf16[512,512]{1,0:T(8,128)(2,1)S(1)}, f32[8,128]{1,0:T(8,128)S(1)}, f32[96,128]{1,0:T(8,128)S(1)}, f32[96,128]{1,0:T(8,128)S(1)}, f32[128,128]{1,0:T(8,128)S(1)}, /*index=5*/f32[96,256]{1,0:T(8,128)S(1)}) custom-call(bf16[16,72,128]{2,1,0:T(8,128)(2,1)S(1)} %all_to_all.11.own_ref, bf16[2,256,512]{2,1,0:T(8,128)(2,1)S(1)} %get-tuple-element.20.step_ref, ...), custom_call_target="tpu_custom_call" | custom-call | flops 500000000 | bytes 1048576 | tf_op jit(solution)/shard_map/pallas_call | solution.py:463
  38.9 0.0 collective-permute-done.other_ref
  39.0 0.1 copy-done
  39.0 4.3 %shard_map.103 = f32[2,32,256]{2,1,0:T(8,128)} custom-call(bf16[16,72,128]{2,1,0:T(8,128)(2,1)S(1)} %all_to_all.11.own_ref, bf16[16,72,128]{2,1,0:T(8,128)(2,1)S(1)} %collective-permute-done.other_ref, bf16[512,512]{1,0:T(8,128)(2,1)S(1)} %get-tuple-element.21.z_ref, f32[8,128]{1,0:T(8,128)S(1)} %get-tuple-element.22.total_ref, ...), custom_call_target="tpu_custom_call" | custom-call | flops 2500000000 | bytes 1048576 | tf_op jit(solution)/shard_map/pallas_call | solution.py:463
Async XLA Ops:
  13.9 23.7 %copy-start.3 = (f32[128,512]{1,0:T(8,128)S(1)}, f32[128,512]{1,0:T(8,128)}, u32[]{:S(2)}) copy-start(f32[128,512]{1,0:T(8,128)} %constant.14.clone.base_ref) | copy-start | bytes 786436
  13.9 23.7 %copy-start.5 = (f32[128,128]{1,0:T(8,128)S(1)}, f32[128,128]{1,0:T(8,128)}, u32[]{:S(2)}) copy-start(f32[128,128]{1,0:T(8,128)} %constant.15.clone.turn_ref) | copy-start | bytes 196612
  14.0 23.6 %copy-start.1 = (bf16[512,256]{1,0:T(8,128)(2,1)S(1)}, bf16[512,256]{1,0:T(8,128)(2,1)}, u32[]{:S(2)}) copy-start(bf16[512,256]{1,0:T(8,128)(2,1)} %constant.22.back_ref) | copy-start | bytes 786436
  14.0 23.6 %copy-start.2 = (bf16[256,512]{1,0:T(8,128)(2,1)S(1)}, bf16[256,512]{1,0:T(8,128)(2,1)}, u32[]{:S(2)}) copy-start(bf16[256,512]{1,0:T(8,128)(2,1)} %constant.21.fold2_ref) | copy-start | bytes 786436
  14.0 23.6 %copy-start.4 = (f32[32,512]{1,0:T(8,128)S(1)}, f32[32,512]{1,0:T(8,128)}, u32[]{:S(2)}) copy-start(f32[32,512]{1,0:T(8,128)} %constant.20.clone.start_ref) | copy-start | bytes 196612
  33.8 4.2 %copy-start.6 = (f32[16,512]{1,0:T(8,128)S(1)}, f32[16,512]{1,0:T(8,128)}, u32[]{:S(2)}) copy-start(f32[16,512]{1,0:T(8,128)} %constant.19.clone.phase_ref) | copy-start | bytes 98308
  33.8 5.1 %collective-permute-start = (bf16[16,72,128]{2,1,0:T(8,128)(2,1)S(1)}, bf16[16,72,128]{2,1,0:T(8,128)(2,1)S(1)}, u32[]{:S(2)}, u32[]{:S(2)}) collective-permute-start(bf16[16,72,128]{2,1,0:T(8,128)(2,1)S(1)} %all_to_all.11.own_ref), channel_id=1, source_target_pairs={{0,8},{8,0},{1,9},{9,1},{2,10},{10,2},{3,11},{11,3},{4,12},{12,4},... | collective-permute-start | bytes 884744 | tf_op jit(solution)/shard_map/ppermute | solution.py:566
  38.1 1.0 %copy-start = (bf16[256,512]{1,0:T(8,128)(2,1)S(1)}, bf16[256,512]{1,0:T(8,128)(2,1)}, u32[]{:S(2)}) copy-start(bf16[256,512]{1,0:T(8,128)(2,1)} %constant.23.step2_ref) | copy-start | bytes 786436

commit v13 on v12

--- a/solution.py
+++ b/solution.py
@@ -556,11 +556,11 @@
     def ids():
         core = lax.axis_index("core")
         owner = (lax.axis_index("z") * 2 + lax.axis_index("xh")) * 2 + core
-        return owner, lax.axis_index("dish"), core
+        return owner, lax.axis_index("y") * 2 + lax.axis_index("xl"), core
 
     given, made = make_tables(ids)
     partial_beam, visits = front(voltages, beam_weights, phase_bins.reshape(PER_BLOCK, GRAIN))
-    parts = lax.all_to_all(partial_beam, "dish", 0, 0, tiled=True)
+    parts = lax.all_to_all(partial_beam, ("xl", "y"), 0, 0, tiled=True)
     packed = call(pack_kernel, pltpu.VMEM((CHIPS, ROWS, GRAIN), BF16), (parts, visits), us=0.3)
     own = lax.all_to_all(packed, ("xh", "z"), 0, 0, tiled=True)
     other = lax.ppermute(own, "core", [(0, 1), (1, 0)])
@@ -568,12 +568,12 @@
 
 
 def solution(mesh):
-    split = jax.sharding.Mesh(mesh.devices.reshape(8, 2, 2, 8), ("z", "xh", "core", "dish"))
-    time = ("z", "xh", "core")
+    split = jax.sharding.Mesh(mesh.devices.reshape(8, 2, 2, 4, 2), ("z", "xh", "core", "y", "xl"))
+    time, dish = ("z", "xh", "core"), ("y", "xl")
     return jax.shard_map(
         steps,
         mesh=split,
-        in_specs=(P(None, "dish", time), P(None, "dish"), P(time)),
-        out_specs=P("dish", None, time),
+        in_specs=(P(None, dish, time), P(None, dish), P(time)),
+        out_specs=P(dish, None, time),
         check_vma=False,
     )

time: 43.6 us -> 43.5 us (level)
  no operation moved by 1% of the time
where the time goes in v13:
time: 43.5 us; the launch traced here: 43.2 us
  blocking collectives  31.6 us (73%)
  Pallas kernels  7.61 us (17%)
  starting transfers between devices  3.75 us (9%)
    all_to_all x1, blocking collectives, steps(): own = lax.all_to_all(packed, ('xh', 'z'), 0, 0, tiled=True)  19.8 us
    all_to_all x1, blocking collectives, steps(): parts = lax.all_to_all(partial_beam, ('xl', 'y'), 0, 0, tiled=True)  11.8 us
    pallas_call x4, Pallas kernels, call(): pl.pallas_call(kernel, out_shape=outs if one else tuple(outs), in_specs=[...  5.65 us
    ppermute x1, starting transfers between devices, steps(): other = lax.ppermute(own, 'core', [(0, 1), (1, 0)])  3.75 us
    pallas_call x1, Pallas kernels, front(): pl.pallas_call(front_kernel, out_shape=(pltpu.VMEM((DISH_WAYS, 2 * PER_BL...  1.96 us
  transfers between devices with their start and end apart: 1, of which 0 were waited for; matrix products, arithmetic and copies ran while one was open for 0% of the time, Pallas kernels for 3%

profile of v13, /device:TPU:1, one launch (start us, length us, event | category | flops | bytes accessed | tf_op | source)
XLA Modules:
  0.0 43.2 jit_solution(9750754115282629093)
XLA Ops:
  0.0 2.0 %front.1 = (f32[8,64,128]{2,1,0:T(8,128)S(1)}, bf16[16,8,128]{2,1,0:T(8,128)(2,1)S(1)}) custom-call(bf16[2,8,4096]{2,1,0:T(8,128)(2,1)} %volts_hbm.1, bf16[2,8]{1,0:T(2,128)(2,1)} %weights_hbm.1, s32[32,128]{1,0:T(8,128)} %bitcast.2), custom_call_target="tpu_custom_call" | custom-call | flops 1048576 | bytes 1048576 | tf_op jit(solution)/shard_map/front/pallas_call | solution.py:533
  2.0 11.8 %all_to_all.10.parts_ref = f32[8,64,128]{2,1,0:T(8,128)S(1)} all-to-all(f32[8,64,128]{2,1,0:T(8,128)S(1)} %get-tuple-element.18), channel_id=1, replica_groups=mesh['z'=8,'xh'=2,'core'=2,'y'=4,'xl'=2] {'xl','y'}, dimensions={0} | all-to-all | bytes 524288 | tf_op jit(solution)/shard_map/all_to_all | solution.py:563
  13.8 0.0 copy-start.3
  13.8 0.0 copy-start.5
  13.8 0.1 shard_map.100
  13.9 0.0 copy-start.1
  13.9 0.0 copy-start.2
  13.9 0.0 copy-start.4
  13.9 19.8 %all_to_all.11.own_ref = bf16[16,72,128]{2,1,0:T(8,128)(2,1)S(1)} all-to-all(bf16[16,72,128]{2,1,0:T(8,128)(2,1)S(1)} %shard_map.100), channel_id=1, replica_groups=mesh['z'=8,'xh'=2,'core'=2,'y'=4,'xl'=2] {'xh','z'}, dimensions={0} | all-to-all | bytes 589824 | tf_op jit(solution)/shard_map/all_to_all | solution.py:565
  33.8 0.0 copy-start.6
  33.8 3.8 %collective-permute-start = (bf16[16,72,128]{2,1,0:T(8,128)(2,1)S(1)}, bf16[16,72,128]{2,1,0:T(8,128)(2,1)S(1)}, u32[]{:S(2)}, u32[]{:S(2)}) collective-permute-start(bf16[16,72,128]{2,1,0:T(8,128)(2,1)S(1)} %all_to_all.11.own_ref), channel_id=1, source_target_pairs={{0,8},{8,0},{1,9},{9,1},{2,10},{10,2},{3,11},{11,3},{4,12},{12,4},... | collective-permute-start | bytes 884744 | tf_op jit(solution)/shard_map/ppermute | solution.py:566
  37.5 0.0 copy-done.3
  37.5 0.0 copy-done.5
  37.5 0.0 copy-done.1
  37.5 0.0 copy-done.2
  37.5 0.0 copy-done.4
  37.5 0.5 %shard_map.101 = (bf16[256,1024]{1,0:T(8,128)(2,1)S(1)}, bf16[2,256,512]{2,1,0:T(8,128)(2,1)S(1)}, bf16[512,512]{1,0:T(8,128)(2,1)S(1)}, bf16[128,512]{1,0:T(8,128)(2,1)S(1)}, bf16[128,512]{1,0:T(8,128)(2,1)S(1)}) custom-call(f32[128,512]{1,0:T(8,128)S(1)} %copy-done.3, f32[128,128]{1,0:T(8,128)S(1)} %copy-done.5, bf16[256,512]{1,0:T(8,128)(2,1)S(1)} %copy-done.2, ...), custom_call_target="tpu_custom_call" | custom-call | flops 1500000000 | bytes 1048576 | tf_op jit(solution)/shard_map/pallas_call | solution.py:463
  38.0 0.0 copy-done.6
  38.0 0.0 copy-start
  38.0 0.8 %shard_map.102 = (bf16[512,512]{1,0:T(8,128)(2,1)S(1)}, f32[8,128]{1,0:T(8,128)S(1)}, f32[96,128]{1,0:T(8,128)S(1)}, f32[96,128]{1,0:T(8,128)S(1)}, f32[128,128]{1,0:T(8,128)S(1)}, /*index=5*/f32[96,256]{1,0:T(8,128)S(1)}) custom-call(bf16[16,72,128]{2,1,0:T(8,128)(2,1)S(1)} %all_to_all.11.own_ref, bf16[2,256,512]{2,1,0:T(8,128)(2,1)S(1)} %get-tuple-element.20.step_ref, ...), custom_call_target="tpu_custom_call" | custom-call | flops 500000000 | bytes 1048576 | tf_op jit(solution)/shard_map/pallas_call | solution.py:463
  38.9 0.0 collective-permute-done.other_ref
  38.9 0.1 copy-done
  39.0 4.2 %shard_map.103 = f32[2,32,256]{2,1,0:T(8,128)} custom-call(bf16[16,72,128]{2,1,0:T(8,128)(2,1)S(1)} %all_to_all.11.own_ref, bf16[16,72,128]{2,1,0:T(8,128)(2,1)S(1)} %collective-permute-done.other_ref, bf16[512,512]{1,0:T(8,128)(2,1)S(1)} %get-tuple-element.21.z_ref, f32[8,128]{1,0:T(8,128)S(1)} %get-tuple-element.22.total_ref, ...), custom_call_target="tpu_custom_call" | custom-call | flops 2500000000 | bytes 1048576 | tf_op jit(solution)/shard_map/pallas_call | solution.py:463
Async XLA Ops:
  13.8 23.7 %copy-start.3 = (f32[128,512]{1,0:T(8,128)S(1)}, f32[128,512]{1,0:T(8,128)}, u32[]{:S(2)}) copy-start(f32[128,512]{1,0:T(8,128)} %constant.14.clone.base_ref) | copy-start | bytes 786436
  13.8 23.7 %copy-start.5 = (f32[128,128]{1,0:T(8,128)S(1)}, f32[128,128]{1,0:T(8,128)}, u32[]{:S(2)}) copy-start(f32[128,128]{1,0:T(8,128)} %constant.15.clone.turn_ref) | copy-start | bytes 196612
  13.9 23.6 %copy-start.1 = (bf16[512,256]{1,0:T(8,128)(2,1)S(1)}, bf16[512,256]{1,0:T(8,128)(2,1)}, u32[]{:S(2)}) copy-start(bf16[512,256]{1,0:T(8,128)(2,1)} %constant.22.back_ref) | copy-start | bytes 786436
  13.9 23.6 %copy-start.2 = (bf16[256,512]{1,0:T(8,128)(2,1)S(1)}, bf16[256,512]{1,0:T(8,128)(2,1)}, u32[]{:S(2)}) copy-start(bf16[256,512]{1,0:T(8,128)(2,1)} %constant.21.fold2_ref) | copy-start | bytes 786436
  13.9 23.6 %copy-start.4 = (f32[32,512]{1,0:T(8,128)S(1)}, f32[32,512]{1,0:T(8,128)}, u32[]{:S(2)}) copy-start(f32[32,512]{1,0:T(8,128)} %constant.20.clone.start_ref) | copy-start | bytes 196612
  33.8 4.3 %copy-start.6 = (f32[16,512]{1,0:T(8,128)S(1)}, f32[16,512]{1,0:T(8,128)}, u32[]{:S(2)}) copy-start(f32[16,512]{1,0:T(8,128)} %constant.19.clone.phase_ref) | copy-start | bytes 98308
  33.8 5.1 %collective-permute-start = (bf16[16,72,128]{2,1,0:T(8,128)(2,1)S(1)}, bf16[16,72,128]{2,1,0:T(8,128)(2,1)S(1)}, u32[]{:S(2)}, u32[]{:S(2)}) collective-permute-start(bf16[16,72,128]{2,1,0:T(8,128)(2,1)S(1)} %all_to_all.11.own_ref), channel_id=1, source_target_pairs={{0,8},{8,0},{1,9},{9,1},{2,10},{10,2},{3,11},{11,3},{4,12},{12,4},... | collective-permute-start | bytes 884744 | tf_op jit(solution)/shard_map/ppermute | solution.py:566
  38.0 1.0 %copy-start = (bf16[256,512]{1,0:T(8,128)(2,1)S(1)}, bf16[256,512]{1,0:T(8,128)(2,1)}, u32[]{:S(2)}) copy-start(bf16[256,512]{1,0:T(8,128)(2,1)} %constant.23.step2_ref) | copy-start | bytes 786436

commit v14 on v13

--- a/solution.py
+++ b/solution.py
@@ -106,7 +106,7 @@
 
 
 def pair_at(place):
-    return 2 * (place & 7) + (place >> 3)
+    return 8 * (place & 1) + 2 * ((place >> 1) & 3) + (place >> 3)
 
 
 def pack_kernel(parts_ref, visit_ref, out_ref):
@@ -555,21 +555,22 @@
 def steps(voltages, beam_weights, phase_bins):
     def ids():
         core = lax.axis_index("core")
-        owner = (lax.axis_index("z") * 2 + lax.axis_index("xh")) * 2 + core
+        z = lax.axis_index("zh") * 4 + lax.axis_index("zl")
+        owner = (z * 2 + lax.axis_index("xh")) * 2 + core
         return owner, lax.axis_index("y") * 2 + lax.axis_index("xl"), core
 
     given, made = make_tables(ids)
     partial_beam, visits = front(voltages, beam_weights, phase_bins.reshape(PER_BLOCK, GRAIN))
     parts = lax.all_to_all(partial_beam, ("xl", "y"), 0, 0, tiled=True)
     packed = call(pack_kernel, pltpu.VMEM((CHIPS, ROWS, GRAIN), BF16), (parts, visits), us=0.3)
-    own = lax.all_to_all(packed, ("xh", "z"), 0, 0, tiled=True)
+    own = lax.all_to_all(packed, ("xh", "zl", "zh"), 0, 0, tiled=True)
     other = lax.ppermute(own, "core", [(0, 1), (1, 0)])
     return jnp.transpose(spectrum(own, other, ids, given, made), (2, 0, 1))
 
 
 def solution(mesh):
-    split = jax.sharding.Mesh(mesh.devices.reshape(8, 2, 2, 4, 2), ("z", "xh", "core", "y", "xl"))
-    time, dish = ("z", "xh", "core"), ("y", "xl")
+    split = jax.sharding.Mesh(mesh.devices.reshape(2, 4, 2, 2, 4, 2), ("zh", "zl", "xh", "core", "y", "xl"))
+    time, dish = ("zh", "zl", "xh", "core"), ("y", "xl")
     return jax.shard_map(
         steps,
         mesh=split,

time: 43.5 us -> 45.3 us (1.041)
  blocking collectives: 31.6 us -> 33 us
    all_to_all x1, blocking collectives: 19.8 us -> 21.2 us  [steps(): own = lax.all_to_all(packed, ('xh', 'zl', 'zh'), 0, 0, tiled=True)]
where the time goes in v14:
time: 45.3 us; the launch traced here: 45 us
  blocking collectives  33 us (73%)
  Pallas kernels  7.62 us (17%)
  starting transfers between devices  4.1 us (9%)
    all_to_all x1, blocking collectives, steps(): own = lax.all_to_all(packed, ('xh', 'zl', 'zh'), 0, 0, tiled=True)  21.2 us
    all_to_all x1, blocking collectives, steps(): parts = lax.all_to_all(partial_beam, ('xl', 'y'), 0, 0, tiled=True)  11.8 us
    pallas_call x4, Pallas kernels, call(): pl.pallas_call(kernel, out_shape=outs if one else tuple(outs), in_specs=[...  5.67 us
    ppermute x1, starting transfers between devices, steps(): other = lax.ppermute(own, 'core', [(0, 1), (1, 0)])  4.1 us
    pallas_call x1, Pallas kernels, front(): pl.pallas_call(front_kernel, out_shape=(pltpu.VMEM((DISH_WAYS, 2 * PER_BL...  1.96 us
  transfers between devices with their start and end apart: 1, of which 0 were waited for; matrix products, arithmetic and copies ran while one was open for 0% of the time, Pallas kernels for 3%

profile of v14, /device:TPU:1, one launch (start us, length us, event | category | flops | bytes accessed | tf_op | source)
XLA Modules:
  0.0 45.0 jit_solution(10014567893665635045)
XLA Ops:
  0.0 2.0 %front.1 = (f32[8,64,128]{2,1,0:T(8,128)S(1)}, bf16[16,8,128]{2,1,0:T(8,128)(2,1)S(1)}) custom-call(bf16[2,8,4096]{2,1,0:T(8,128)(2,1)} %volts_hbm.1, bf16[2,8]{1,0:T(2,128)(2,1)} %weights_hbm.1, s32[32,128]{1,0:T(8,128)} %bitcast.2), custom_call_target="tpu_custom_call" | custom-call | flops 1048576 | bytes 1048576 | tf_op jit(solution)/shard_map/front/pallas_call | solution.py:533
  2.0 11.8 %all_to_all.10.parts_ref = f32[8,64,128]{2,1,0:T(8,128)S(1)} all-to-all(f32[8,64,128]{2,1,0:T(8,128)S(1)} %get-tuple-element.18), channel_id=1, replica_groups=mesh['zh'=2,'zl'=4,'xh'=2,'core'=2,'y'=4,'xl'=2] {'xl','y'}, dimensions={0} | all-to-all | bytes 524288 | tf_op jit(solution)/shard_map/all_to_all | solution.py:564
  13.8 0.0 copy-start.3
  13.8 0.0 copy-start.5
  13.8 0.1 shard_map.100
  13.9 0.0 copy-start.1
  13.9 0.0 copy-start.2
  13.9 0.0 copy-start.4
  13.9 21.2 %all_to_all.11.own_ref = bf16[16,72,128]{2,1,0:T(8,128)(2,1)S(1)} all-to-all(bf16[16,72,128]{2,1,0:T(8,128)(2,1)S(1)} %shard_map.100), channel_id=1, replica_groups=mesh['zh'=2,'zl'=4,'xh'=2,'core'=2,'y'=4,'xl'=2] {'xh','zl','zh'}, dimensions={0} | all-to-all | bytes 589824 | tf_op jit(solution)/shard_map/all_to_all | solution.py:566
  35.1 0.0 copy-start.6
  35.1 4.1 %collective-permute-start = (bf16[16,72,128]{2,1,0:T(8,128)(2,1)S(1)}, bf16[16,72,128]{2,1,0:T(8,128)(2,1)S(1)}, u32[]{:S(2)}, u32[]{:S(2)}) collective-permute-start(bf16[16,72,128]{2,1,0:T(8,128)(2,1)S(1)} %all_to_all.11.own_ref), channel_id=1, source_target_pairs={{0,8},{8,0},{1,9},{9,1},{2,10},{10,2},{3,11},{11,3},{4,12},{12,4},... | collective-permute-start | bytes 884744 | tf_op jit(solution)/shard_map/ppermute | solution.py:567
  39.3 0.0 copy-done.3
  39.3 0.0 copy-done.5
  39.3 0.0 copy-done.1
  39.3 0.0 copy-done.2
  39.3 0.0 copy-done.4
  39.3 0.5 %shard_map.101 = (bf16[256,1024]{1,0:T(8,128)(2,1)S(1)}, bf16[2,256,512]{2,1,0:T(8,128)(2,1)S(1)}, bf16[512,512]{1,0:T(8,128)(2,1)S(1)}, bf16[128,512]{1,0:T(8,128)(2,1)S(1)}, bf16[128,512]{1,0:T(8,128)(2,1)S(1)}) custom-call(f32[128,512]{1,0:T(8,128)S(1)} %copy-done.3, f32[128,128]{1,0:T(8,128)S(1)} %copy-done.5, bf16[256,512]{1,0:T(8,128)(2,1)S(1)} %copy-done.2, ...), custom_call_target="tpu_custom_call" | custom-call | flops 1500000000 | bytes 1048576 | tf_op jit(solution)/shard_map/pallas_call | solution.py:463
  39.8 0.0 copy-done.6
  39.8 0.0 copy-start
  39.8 0.8 %shard_map.102 = (bf16[512,512]{1,0:T(8,128)(2,1)S(1)}, f32[8,128]{1,0:T(8,128)S(1)}, f32[96,128]{1,0:T(8,128)S(1)}, f32[96,128]{1,0:T(8,128)S(1)}, f32[128,128]{1,0:T(8,128)S(1)}, /*index=5*/f32[96,256]{1,0:T(8,128)S(1)}) custom-call(bf16[16,72,128]{2,1,0:T(8,128)(2,1)S(1)} %all_to_all.11.own_ref, bf16[2,256,512]{2,1,0:T(8,128)(2,1)S(1)} %get-tuple-element.20.step_ref, ...), custom_call_target="tpu_custom_call" | custom-call | flops 500000000 | bytes 1048576 | tf_op jit(solution)/shard_map/pallas_call | solution.py:463
  40.6 0.0 collective-permute-done.other_ref
  40.6 0.1 copy-done
  40.7 4.3 %shard_map.103 = f32[2,32,256]{2,1,0:T(8,128)} custom-call(bf16[16,72,128]{2,1,0:T(8,128)(2,1)S(1)} %all_to_all.11.own_ref, bf16[16,72,128]{2,1,0:T(8,128)(2,1)S(1)} %collective-permute-done.other_ref, bf16[512,512]{1,0:T(8,128)(2,1)S(1)} %get-tuple-element.21.z_ref, f32[8,128]{1,0:T(8,128)S(1)} %get-tuple-element.22.total_ref, ...), custom_call_target="tpu_custom_call" | custom-call | flops 2500000000 | bytes 1048576 | tf_op jit(solution)/shard_map/pallas_call | solution.py:463
Async XLA Ops:
  13.8 25.5 %copy-start.3 = (f32[128,512]{1,0:T(8,128)S(1)}, f32[128,512]{1,0:T(8,128)}, u32[]{:S(2)}) copy-start(f32[128,512]{1,0:T(8,128)} %constant.14.clone.base_ref) | copy-start | bytes 786436
  13.8 25.5 %copy-start.5 = (f32[128,128]{1,0:T(8,128)S(1)}, f32[128,128]{1,0:T(8,128)}, u32[]{:S(2)}) copy-start(f32[128,128]{1,0:T(8,128)} %constant.15.clone.turn_ref) | copy-start | bytes 196612
  13.9 25.4 %copy-start.1 = (bf16[512,256]{1,0:T(8,128)(2,1)S(1)}, bf16[512,256]{1,0:T(8,128)(2,1)}, u32[]{:S(2)}) copy-start(bf16[512,256]{1,0:T(8,128)(2,1)} %constant.22.back_ref) | copy-start | bytes 786436
  13.9 25.3 %copy-start.2 = (bf16[256,512]{1,0:T(8,128)(2,1)S(1)}, bf16[256,512]{1,0:T(8,128)(2,1)}, u32[]{:S(2)}) copy-start(bf16[256,512]{1,0:T(8,128)(2,1)} %constant.21.fold2_ref) | copy-start | bytes 786436
  13.9 25.3 %copy-start.4 = (f32[32,512]{1,0:T(8,128)S(1)}, f32[32,512]{1,0:T(8,128)}, u32[]{:S(2)}) copy-start(f32[32,512]{1,0:T(8,128)} %constant.20.clone.start_ref) | copy-start | bytes 196612
  35.1 4.6 %copy-start.6 = (f32[16,512]{1,0:T(8,128)S(1)}, f32[16,512]{1,0:T(8,128)}, u32[]{:S(2)}) copy-start(f32[16,512]{1,0:T(8,128)} %constant.19.clone.phase_ref) | copy-start | bytes 98308
  35.1 5.5 %collective-permute-start = (bf16[16,72,128]{2,1,0:T(8,128)(2,1)S(1)}, bf16[16,72,128]{2,1,0:T(8,128)(2,1)S(1)}, u32[]{:S(2)}, u32[]{:S(2)}) collective-permute-start(bf16[16,72,128]{2,1,0:T(8,128)(2,1)S(1)} %all_to_all.11.own_ref), channel_id=1, source_target_pairs={{0,8},{8,0},{1,9},{9,1},{2,10},{10,2},{3,11},{11,3},{4,12},{12,4},... | collective-permute-start | bytes 884744 | tf_op jit(solution)/shard_map/ppermute | solution.py:567
  39.8 1.0 %copy-start = (bf16[256,512]{1,0:T(8,128)(2,1)S(1)}, bf16[256,512]{1,0:T(8,128)(2,1)}, u32[]{:S(2)}) copy-start(bf16[256,512]{1,0:T(8,128)(2,1)} %constant.23.step2_ref) | copy-start | bytes 786436

commit v15 on v11

--- a/solution.py
+++ b/solution.py
@@ -105,6 +105,10 @@
         beam_ref[way] = rows
 
 
+def pair_at(place):
+    return 2 * (place & 7) + (place >> 3)
+
+
 def pack_kernel(parts_ref, visit_ref, out_ref):
     total = parts_ref[0]
     for way in range(1, DISH_WAYS):
@@ -116,7 +120,7 @@
     rows = jnp.concatenate([early_side, late_side], 0).astype(BF16)
     for chip in range(CHIPS):
         out_ref[chip, : 2 * PER_BLOCK, :] = rows
-        out_ref[chip, 2 * PER_BLOCK :, :] = visit_ref[chip]
+        out_ref[chip, 2 * PER_BLOCK :, :] = visit_ref[pair_at(chip)]
 
 
 def coded_times(shape):
@@ -324,7 +328,7 @@
 
 def grain_row(which):
     place = lax.broadcasted_iota(jnp.int32, (8, HALF), 1)
-    grain = (2 * (place >> 5) + which) * PER_BLOCK + (place & (PER_BLOCK - 1))
+    grain = (2 * pair_at(place >> 5) + which) * PER_BLOCK + (place & (PER_BLOCK - 1))
     return grain.astype(F32)[0:1, :]
 
 
@@ -353,7 +357,7 @@
         which = jnp.where(is_mine, core, 1 - core)
         side = place & (2 * PER_BLOCK - 1)
         in_block, odd = side >> 1, (side & 1).astype(F32)
-        grain = ((2 * (place >> 6) + which) * PER_BLOCK + in_block).astype(F32)
+        grain = ((2 * pair_at(place >> 6) + which) * PER_BLOCK + in_block).astype(F32)
         here = mine[3] + more[3]
         ends = mine[1] + more[1]
         for k in range(2):
@@ -558,24 +562,24 @@
     def ids():
         core = lax.axis_index("core")
         owner = (lax.axis_index("z") * 2 + lax.axis_index("xh")) * 2 + core
-        return owner, lax.axis_index("dish"), core
+        return owner, lax.axis_index("y") * 2 + lax.axis_index("xl"), core
 
     made = make_tables(ids)
     partial_beam, visits = front(voltages, beam_weights, phase_bins.reshape(PER_BLOCK, GRAIN))
-    parts = lax.all_to_all(partial_beam, "dish", 0, 0, tiled=True)
+    parts = lax.all_to_all(partial_beam, ("xl", "y"), 0, 0, tiled=True)
     packed = call(pack_kernel, pltpu.VMEM((CHIPS, ROWS, GRAIN), BF16), (parts, visits), us=0.3)
-    own = lax.all_to_all(packed, ("z", "xh"), 0, 0, tiled=True)
+    own = lax.all_to_all(packed, ("xh", "z"), 0, 0, tiled=True)
     other = lax.ppermute(own, "core", [(0, 1), (1, 0)])
     return jnp.transpose(spectrum(own, other, ids, made), (2, 0, 1))
 
 
 def solution(mesh):
-    split = jax.sharding.Mesh(mesh.devices.reshape(8, 2, 2, 8), ("z", "xh", "core", "dish"))
-    time = ("z", "xh", "core")
+    split = jax.sharding.Mesh(mesh.devices.reshape(8, 2, 2, 4, 2), ("z", "xh", "core", "y", "xl"))
+    time, dish = ("z", "xh", "core"), ("y", "xl")
     return jax.shard_map(
         steps,
         mesh=split,
-        in_specs=(P(None, "dish", time), P(None, "dish"), P(time)),
-        out_specs=P("dish", None, time),
+        in_specs=(P(None, dish, time), P(None, dish), P(time)),
+        out_specs=P(dish, None, time),
         check_vma=False,
     )

time: 45.6 us -> 43.4 us (0.952)
  blocking collectives: 33.7 us -> 31.6 us
    all_to_all x2, blocking collectives: 33.7 us -> 31.6 us  [the longest x1 19.8 us: steps(): own = lax.all_to_all(packed, ('xh', 'z'), 0, 0, tiled=True)]
where the time goes in v15:
time: 43.4 us; the launch traced here: 43.1 us
  blocking collectives  31.6 us (73%)
  Pallas kernels  7.62 us (18%)
  starting transfers between devices  3.75 us (9%)
    all_to_all x1, blocking collectives, steps(): own = lax.all_to_all(packed, ('xh', 'z'), 0, 0, tiled=True)  19.8 us
    all_to_all x1, blocking collectives, steps(): parts = lax.all_to_all(partial_beam, ('xl', 'y'), 0, 0, tiled=True)  11.8 us
    pallas_call x4, Pallas kernels, call(): pl.pallas_call(kernel, out_shape=outs if one else tuple(outs), in_specs=[...  5.66 us
    ppermute x1, starting transfers between devices, steps(): other = lax.ppermute(own, 'core', [(0, 1), (1, 0)])  3.75 us
    pallas_call x1, Pallas kernels, front(): pl.pallas_call(front_kernel, out_shape=(pltpu.VMEM((DISH_WAYS, 2 * PER_BL...  1.96 us
  transfers between devices with their start and end apart: 1, of which 0 were waited for; matrix products, arithmetic and copies ran while one was open for 0% of the time, Pallas kernels for 3%

profile of v15, /device:TPU:1, one launch (start us, length us, event | category | flops | bytes accessed | tf_op | source)
XLA Modules:
  0.0 43.1 jit_solution(18149846579018898832)
XLA Ops:
  0.0 2.0 %front.1 = (f32[8,64,128]{2,1,0:T(8,128)S(1)}, bf16[16,8,128]{2,1,0:T(8,128)(2,1)S(1)}) custom-call(bf16[2,8,4096]{2,1,0:T(8,128)(2,1)} %volts_hbm.1, bf16[2,8]{1,0:T(2,128)(2,1)} %weights_hbm.1, s32[32,128]{1,0:T(8,128)} %bitcast.2), custom_call_target="tpu_custom_call" | custom-call | flops 1048576 | bytes 1048576 | tf_op jit(solution)/shard_map/front/pallas_call | solution.py:539
  2.0 0.0 copy-start.6
  2.0 11.8 %all_to_all.10.parts_ref = f32[8,64,128]{2,1,0:T(8,128)S(1)} all-to-all(f32[8,64,128]{2,1,0:T(8,128)S(1)} %get-tuple-element.20), channel_id=1, replica_groups=mesh['z'=8,'xh'=2,'core'=2,'y'=4,'xl'=2] {'xl','y'}, dimensions={0} | all-to-all | bytes 524288 | tf_op jit(solution)/shard_map/all_to_all | solution.py:569
  13.8 0.0 copy-start.2
  13.8 0.0 copy-start.3
  13.8 0.0 copy-start.5
  13.8 0.1 shard_map.100
  13.9 0.0 copy-start
  13.9 0.0 copy-start.1
  13.9 0.0 copy-start.4
  14.0 19.8 %all_to_all.11.own_ref = bf16[16,72,128]{2,1,0:T(8,128)(2,1)S(1)} all-to-all(bf16[16,72,128]{2,1,0:T(8,128)(2,1)S(1)} %shard_map.100), channel_id=1, replica_groups=mesh['z'=8,'xh'=2,'core'=2,'y'=4,'xl'=2] {'xh','z'}, dimensions={0} | all-to-all | bytes 589824 | tf_op jit(solution)/shard_map/all_to_all | solution.py:571
  33.8 3.8 %collective-permute-start = (bf16[16,72,128]{2,1,0:T(8,128)(2,1)S(1)}, bf16[16,72,128]{2,1,0:T(8,128)(2,1)S(1)}, u32[]{:S(2)}, u32[]{:S(2)}) collective-permute-start(bf16[16,72,128]{2,1,0:T(8,128)(2,1)S(1)} %all_to_all.11.own_ref), channel_id=1, source_target_pairs={{0,8},{8,0},{1,9},{9,1},{2,10},{10,2},{3,11},{11,3},{4,12},{12,4},... | collective-permute-start | bytes 884744 | tf_op jit(solution)/shard_map/ppermute | solution.py:572
  37.5 0.0 copy-done.6
  37.5 0.0 copy-done.2
  37.5 0.0 copy-done.3
  37.5 0.0 copy-done.5
  37.5 0.0 copy-done
  37.5 0.0 copy-done.1
  37.5 0.0 copy-done.4
  37.6 0.5 %shard_map.101 = (bf16[256,1024]{1,0:T(8,128)(2,1)S(1)}, bf16[2,256,512]{2,1,0:T(8,128)(2,1)S(1)}, bf16[512,512]{1,0:T(8,128)(2,1)S(1)}, bf16[128,512]{1,0:T(8,1...) custom-call(f32[128,512]{1,0:T(8,128)S(1)} %copy-done.3, ...), custom_call_target="tpu_custom_call" | custom-call | flops 1500000000 | bytes 1048576 | tf_op jit(solution)/shard_map/pallas_call | solution.py:468
  38.0 0.8 %shard_map.102 = (bf16[512,512]{1,0:T(8,128)(2,1)S(1)}, f32[8,128]{1,0:T(8,128)S(1)}, f32[96,128]{1,0:T(8,128)S(1)}, f32[96,128]{1,0:T(8,128)S(1)}, f32[128,128]{1,0:T(8,128)S(1)}, /*index=5*/f32[96,256]{1,0:T(8,128)S(1)}) custom-call(bf16[16,72,128]{2,1,0:T(8,128)(2,1)S(1)} %all_to_all.11.own_ref, bf16[2,256,512]{2,1,0:T(8,128)(2,1)S(1)} %get-tuple-element.22.step_ref, ...), custom_call_target="tpu_custom_call" | custom-call | flops 500000000 | bytes 1048576 | tf_op jit(solution)/shard_map/pallas_call | solution.py:468
  38.9 0.0 collective-permute-done.other_ref
  38.9 4.2 %shard_map.103 = f32[2,32,256]{2,1,0:T(8,128)} custom-call(bf16[16,72,128]{2,1,0:T(8,128)(2,1)S(1)} %all_to_all.11.own_ref, bf16[16,72,128]{2,1,0:T(8,128)(2,1)S(1)} %collective-permute-done.other_ref, bf16[512,512]{1,0:T(8,128)(2,1)S(1)} %get-tuple-element.24.z_ref, f32[8,128]{1,0:T(8,128)S(1)} %get-tuple-element.25.total_ref, ...), custom_call_target="tpu_custom_call" | custom-call | flops 2500000000 | bytes 1048576 | tf_op jit(solution)/shard_map/pallas_call | solution.py:468
Async XLA Ops:
  2.0 35.6 %copy-start.6 = (f32[16,512]{1,0:T(8,128)S(1)}, f32[16,512]{1,0:T(8,128)}, u32[]{:S(2)}) copy-start(f32[16,512]{1,0:T(8,128)} %constant.19.clone.phase_in) | copy-start | bytes 98308
  13.8 23.7 %copy-start.2 = (bf16[256,512]{1,0:T(8,128)(2,1)S(1)}, bf16[256,512]{1,0:T(8,128)(2,1)}, u32[]{:S(2)}) copy-start(bf16[256,512]{1,0:T(8,128)(2,1)} %constant.21.fold2_ref) | copy-start | bytes 786436
  13.8 23.7 %copy-start.3 = (f32[128,512]{1,0:T(8,128)S(1)}, f32[128,512]{1,0:T(8,128)}, u32[]{:S(2)}) copy-start(f32[128,512]{1,0:T(8,128)} %constant.14.clone.base_ref) | copy-start | bytes 786436
  13.8 23.7 %copy-start.5 = (f32[128,128]{1,0:T(8,128)S(1)}, f32[128,128]{1,0:T(8,128)}, u32[]{:S(2)}) copy-start(f32[128,128]{1,0:T(8,128)} %constant.15.clone.turn_ref) | copy-start | bytes 196612
  13.9 23.6 %copy-start = (bf16[256,512]{1,0:T(8,128)(2,1)S(1)}, bf16[256,512]{1,0:T(8,128)(2,1)}, u32[]{:S(2)}) copy-start(bf16[256,512]{1,0:T(8,128)(2,1)} %constant.23.step2_in) | copy-start | bytes 786436
  13.9 23.6 %copy-start.1 = (bf16[512,256]{1,0:T(8,128)(2,1)S(1)}, bf16[512,256]{1,0:T(8,128)(2,1)}, u32[]{:S(2)}) copy-start(bf16[512,256]{1,0:T(8,128)(2,1)} %constant.22.back_ref) | copy-start | bytes 786436
  13.9 23.6 %copy-start.4 = (f32[32,512]{1,0:T(8,128)S(1)}, f32[32,512]{1,0:T(8,128)}, u32[]{:S(2)}) copy-start(f32[32,512]{1,0:T(8,128)} %constant.20.clone.start_ref) | copy-start | bytes 196612
  33.8 5.1 %collective-permute-start = (bf16[16,72,128]{2,1,0:T(8,128)(2,1)S(1)}, bf16[16,72,128]{2,1,0:T(8,128)(2,1)S(1)}, u32[]{:S(2)}, u32[]{:S(2)}) collective-permute-start(bf16[16,72,128]{2,1,0:T(8,128)(2,1)S(1)} %all_to_all.11.own_ref), channel_id=1, source_target_pairs={{0,8},{8,0},{1,9},{9,1},{2,10},{10,2},{3,11},{11,3},{4,12},{12,4},... | collective-permute-start | bytes 884744 | tf_op jit(solution)/shard_map/ppermute | solution.py:572
